TPU v7x, 32 devices: a whole 2x2x4 slice. The times are simulated.
32 devices in a mesh: section: 2 (over x), dp: 8 (over z, core), tensor: 2 (over y).
Axes of the slice: x: 2, y: 2, z: 4, core: 2. Of those that a mesh axis runs over, the one named last changes fastest.
Arguments:
- x_in: bfloat16 [4, 2048, 768], P(None, ('dp', 'tensor')), may hold values from -6 to 6
- d_out: bfloat16 [4, 2048, 768], P(None, ('dp', 'tensor')), may hold values from -6 to 6
- lengths: int32 [4, 8, 4], P(None, 'dp'), may hold values from 1 to 192, 256 in all within a row
- routes: int32 [2, 4, 2048, 1], P('section', None, 'dp'), may hold values from 0 to 7; in each aligned block of 256 rows (0 to 255, 256 to 511, ..., all dimensions but the last counted through in order) at most 64 rows name the same one
- gain_attn: bfloat16 [2, 768], P('section'), may hold values from 0.5 to 1.5
- w_qkv: bfloat16 [2, 3, 768, 768], P('section', None, 'dp', 'tensor'), may hold values from -0.21875 to 0.21875
- w_attn_out: bfloat16 [2, 768, 768], P('section', 'tensor', 'dp'), may hold values from -0.875 to 0.875
- gain_ffn: bfloat16 [2, 768], P('section'), may hold values from 0.5 to 1.5
- w_router: bfloat16 [2, 768, 8], P('section'), may hold values from -0.15625 to 0.15625
- w_in: bfloat16 [2, 8, 768, 3072], P('section', 'dp', None, 'tensor'), may hold values from -0.21875 to 0.21875
- w_exp_out: bfloat16 [2, 8, 3072, 768], P('section', 'dp', 'tensor'), may hold values from -0.875 to 0.875
Outputs:
- section_out: bfloat16 [2, 4, 2048, 768], P('section', None, ('dp', 'tensor'))
- section_in_grad: bfloat16 [2, 4, 2048, 768], P('section', None, ('dp', 'tensor'))
- g_gain_attn: float32 [2, 768], P('section')
- g_w_qkv: float32 [2, 3, 768, 768], P('section', None, 'dp', 'tensor')
- g_w_attn_out: float32 [2, 768, 768], P('section', 'tensor', 'dp')
- g_gain_ffn: float32 [2, 768], P('section')
- g_w_router: float32 [2, 768, 8], P('section')
- g_w_in: float32 [2, 8, 768, 3072], P('section', 'dp', None, 'tensor')
- g_w_exp_out: float32 [2, 8, 3072, 768], P('section', 'dp', 'tensor')
Inputs may be any that keep to these rules, and one draw needn't show every extreme that they name: The 4 lengths of each group sum to 256, and the longest of each group is exactly 192. `routes`: within the 256 tokens of one group, one micro-batch and one layer, no expert is named by more than 64 tokens; in some of these blocks one expert is named by exactly 64.
All inputs are finite; a program needn't handle non-finite values.
Results may differ from a plain program's by a relative error of at most 0.025.
Values may be sent and summed in bfloat16 or wider, within the bound.
No kernel may reach another device: no remote copies, remote signals or barrier semaphores. Data moves between devices by JAX's collectives and lax.ppermute only.
A program may use at most 256 MiB of HBM per device.

v0:
```python
import functools
import math

import jax
import jax.numpy as jnp
from jax import lax
from jax.experimental import pallas as pl
from jax.experimental.pallas import tpu as pltpu
from jax.sharding import PartitionSpec as P

HD = 64
LANES = 128
EPSILON = 1e-06
NEGATIVE = -1e30
F32 = jnp.float32
BF16 = jnp.bfloat16
CUBIC = 0.044715
VMEM_LIMIT = 56 * 1024 * 1024
SLOPE = math.sqrt(2.0 / math.pi)


def swap(values, axis):
    return lax.ppermute(values, axis, [(0, 1), (1, 0)])


def one_way(values, axis, source, target):
    return lax.ppermute(values, axis, [(source, target)])


def all_to_all(values):
    return lax.all_to_all(values, "dp", split_axis=0, concat_axis=0, tiled=True)


def after(value, *anchors):
    return lax.optimization_barrier((value, anchors))[0]


def dot(left, right, left_dim, right_dim):
    return lax.dot_general(
        left, right, (((left_dim,), (right_dim,)), ((), ())), preferred_element_type=F32
    )


def ordered(index, own, other):
    return jnp.where(
        index == 0, jnp.concatenate([own, other], axis=0), jnp.concatenate([other, own], axis=0)
    )


def entry(array, index):
    return lax.dynamic_index_in_dim(array, index, 0, keepdims=False)


def norm_forward(inputs, gain):
    scaling = lax.rsqrt(jnp.mean(inputs * inputs, axis=-1, keepdims=True) + EPSILON)
    return inputs * scaling * gain


def norm_back(upstream, inputs, gain):
    scaling = lax.rsqrt(jnp.mean(inputs * inputs, axis=-1, keepdims=True) + EPSILON)
    weighted = upstream * gain
    scaled = inputs * scaling
    inner = jnp.mean(weighted * inputs, axis=-1, keepdims=True)
    return (
        scaling * weighted - scaled * (scaling * scaling * inner),
        jnp.sum(upstream * scaled, axis=0, keepdims=True),
    )


def smooth_gate(values):
    return jax.nn.gelu(values, approximate=True)


def routing(route_row, experts):
    count = route_row.shape[0]
    capacity = 2 * count // experts
    hot = route_row[:, None] == jnp.arange(experts, dtype=jnp.int32)[None, :]
    places = jnp.arange(count, dtype=jnp.int32)
    earlier = (places[:, None] > places[None, :]).astype(BF16)
    ranks = dot(earlier, hot.astype(BF16), 1, 0)
    ranking = jnp.sum(ranks * hot.astype(F32), axis=1).astype(jnp.int32)
    slots = route_row * capacity + ranking
    places = jnp.arange(experts * capacity, dtype=jnp.int32)
    return (
        (slots[None, :] == places[:, None]).astype(BF16),
        (slots[:, None] == places[None, :]).astype(BF16),
    )


def head_lanes(count):
    return lax.broadcasted_iota(jnp.int32, (count, LANES), 1) // HD


def attention_bias(seg_col, seg_row, count):
    rows = lax.broadcasted_iota(jnp.int32, (count, count), 0)
    cols = lax.broadcasted_iota(jnp.int32, (count, count), 1)
    return jnp.where((seg_col == seg_row) & (rows >= cols), 0.0, NEGATIVE)


def expert_chances(rows, router, experts):
    logits = dot(rows, router, 1, 1)
    lane = lax.broadcasted_iota(jnp.int32, logits.shape, 1)
    logits = jnp.where(lane < experts, logits, NEGATIVE)
    raised = jnp.exp(logits - jnp.max(logits, axis=-1, keepdims=True))
    return raised * (1.0 / jnp.sum(raised, axis=-1, keepdims=True))


def forward_kernel(get, outs, send, *, experts, joined):
    (xn_ref, qkv_ref, lse_ref, *o_refs) = outs[:5]
    (h_ref, gate_ref, out_ref) = outs[5:8]
    if joined:
        mixed_in = dot(get("taking")[...], get("back")[...], 1, 0)
        result = (get("h_before")[...] + get("gate_before")[...] * mixed_in).astype(BF16)
        outs[8][...] = result
        send(8)
        a = result.astype(F32)
    else:
        a = get("a")[...].astype(F32)
    count, width = a.shape
    part = width // 2
    pairs = part // LANES
    gains = get("gains")
    xn = norm_forward(a, gains[0:1, :]).astype(BF16)
    xn_ref[...] = xn
    send(0)
    bias = attention_bias(get("seg_col")[...], get("seg_row")[...], count)
    lanes = head_lanes(count)
    scale = 1.0 / math.sqrt(HD)
    w_ref = get("weights")
    for half in range(2):
        base = half * 3 * part
        qkv_ref[:, base:base + 3 * part] = dot(
            xn, w_ref[:, half * 4 * part:half * 4 * part + 3 * part], 1, 0
        ).astype(BF16)
    send(1)
    attended = a
    lse = jnp.zeros((count, LANES), F32)
    for half in range(2):
        base = half * 3 * part
        for pair in range(pairs):
            at = base + pair * LANES
            query = qkv_ref[:, at:at + LANES]
            key = qkv_ref[:, at + part:at + part + LANES]
            value = qkv_ref[:, at + 2 * part:at + 2 * part + LANES]
            mixed = None
            for head in range(2):
                own = jnp.where(lanes == head, query, jnp.zeros_like(query))
                scores = dot(own, key, 1, 1) * scale + bias
                top = jnp.max(scores, axis=-1, keepdims=True)
                weight = jnp.exp(scores - top)
                total = jnp.sum(weight, axis=-1, keepdims=True)
                probs = (weight * (1.0 / total)).astype(BF16)
                number = (half * pairs + pair) * 2 + head
                lse = jnp.where(
                    lax.broadcasted_iota(jnp.int32, lse.shape, 1) == number,
                    top + jnp.log(total), lse,
                )
                part_out = dot(probs, value, 1, 0)
                mixed = part_out if head == 0 else jnp.where(lanes == 0, mixed, part_out)
            o_refs[half][:, pair * LANES:(pair + 1) * LANES] = mixed.astype(BF16)
        send(3 + half)
        attended = attended + dot(
            o_refs[half][...],
            w_ref[:, half * 4 * part + 3 * part:(half + 1) * 4 * part], 1, 1,
        )
    lse_ref[...] = lse
    send(2)
    h_ref[...] = attended
    send(5)
    hn = norm_forward(attended, gains[1:2, :]).astype(BF16)
    out_ref[...] = dot(get("placing")[...], hn, 1, 0).astype(BF16)
    send(7)
    chances = expert_chances(hn, get("router")[...], experts)
    lane = lax.broadcasted_iota(jnp.int32, chances.shape, 1)
    gate_ref[...] = jnp.sum(
        jnp.where(lane == get("route")[...], chances, 0.0), axis=-1, keepdims=True
    )
    send(6)


def hidden_kernel(get, outs, send):
    (dattn_ref, dh_ref, small_ref) = outs
    hn_grad = dot(get("taking")[...], get("back")[...], 1, 0)
    gains = get("gains")
    dz = get("dz")[...].astype(F32)
    hidden_part, small_ref[...] = norm_back(hn_grad, get("h")[...], gains[1:2, :])
    hidden_grad = dz + hidden_part
    dattn_ref[...] = hidden_grad.astype(BF16)
    send(0)
    dh_ref[...] = hidden_grad
    send(1)
    send(2)


def backward_kernel(get, outs, send, *, spread):
    (da_ref, *dqkv_refs, small_ref) = outs[:4]
    gains = get("gains")
    attended_grad = get("dattn")[...]
    count, width = attended_grad.shape
    part = width // 2
    pairs = part // LANES
    bias = attention_bias(get("seg_col")[...], get("seg_row")[...], count)
    lanes = head_lanes(count)
    scale = 1.0 / math.sqrt(HD)
    w_ref, qkv_ref, lse_ref = (get("weights"), get("qkv"), get("lse"))
    normed_grad = jnp.zeros((count, width), F32)
    for half in range(2):
        base = half * 3 * part
        mixed_grad = dot(
            attended_grad, w_ref[:, half * 4 * part + 3 * part:(half + 1) * 4 * part], 1, 0
        ).astype(BF16)
        for pair in range(pairs):
            at = base + pair * LANES
            query = qkv_ref[:, at:at + LANES]
            key = qkv_ref[:, at + part:at + part + LANES]
            value = qkv_ref[:, at + 2 * part:at + 2 * part + LANES]
            grad = mixed_grad[:, pair * LANES:(pair + 1) * LANES]
            dq = dk = dv = None
            for head in range(2):
                number = (half * pairs + pair) * 2 + head
                zero = jnp.zeros_like(query)
                own_q = jnp.where(lanes == head, query, zero)
                own_g = jnp.where(lanes == head, grad, zero)
                scores = dot(own_q, key, 1, 1) * scale + bias
                probs = jnp.exp(scores - lse_ref[:, number:number + 1])
                prob_grad = dot(own_g, value, 1, 1)
                inner = jnp.sum(probs * prob_grad, axis=-1, keepdims=True)
                score_grad = (probs * (prob_grad - inner)).astype(BF16)
                head_dv = dot(probs.astype(BF16), own_g, 0, 0)
                head_dk = dot(score_grad, own_q, 0, 0)
                head_dq = dot(score_grad, key, 1, 0)
                if head == 0:
                    dq, dk, dv = (head_dq, head_dk, head_dv)
                else:
                    dq = jnp.where(lanes == 0, dq, head_dq)
                    dk = dk + head_dk
                    dv = dv + head_dv
            at = pair * LANES
            dqkv_refs[half][:, at:at + LANES] = (dq * scale).astype(BF16)
            dqkv_refs[half][:, at + part:at + part + LANES] = (dk * scale).astype(BF16)
            dqkv_refs[half][:, at + 2 * part:at + 2 * part + LANES] = dv.astype(BF16)
        send(1 + half)
        normed_grad = normed_grad + dot(
            dqkv_refs[half][...],
            w_ref[:, half * 4 * part:half * 4 * part + 3 * part], 1, 1,
        )
    input_part, small_ref[...] = norm_back(
        normed_grad, get("a")[...].astype(F32), gains[0:1, :]
    )
    input_grad = (get("dh")[...] + input_part).astype(BF16)
    if spread:
        outs[4][...] = dot(get("placing")[...], input_grad, 1, 0).astype(BF16)
        send(4)
    da_ref[...] = input_grad
    send(0)
    send(3)


def staged_call(kernel, inputs, outs, flops):
    names = list(inputs)
    args = [inputs[name] for name in names]
    count = len(args)
    total = count + len(outs)

    def body(*refs):
        held, marks = (refs[total:-1], refs[-1])
        copies = [
            pltpu.make_async_copy(*pair, marks.at[number])
            for number, pair in enumerate(
                [(refs[i], held[i]) for i in range(count)]
                + [(held[i], refs[i]) for i in range(count, total)]
            )
        ]
        for copy in copies[:count]:
            copy.start()
        ready = set()

        def get(name):
            number = names.index(name)
            if number not in ready:
                ready.add(number)
                copies[number].wait()
            return held[number]

        kernel(get, held[count:], lambda number: copies[count + number].start())
        for copy in copies[count:]:
            copy.wait()

    moved = sum(math.prod(v.shape) * v.dtype.itemsize for v in (*args, *outs))
    return pl.pallas_call(
        body,
        out_shape=outs,
        in_specs=[pl.BlockSpec(memory_space=pltpu.HBM)] * count,
        out_specs=[pl.BlockSpec(memory_space=pltpu.HBM)] * len(outs),
        scratch_shapes=[pltpu.VMEM(v.shape, v.dtype) for v in (*args, *outs)]
        + [pltpu.SemaphoreType.DMA((total,))],
        compiler_params=pltpu.CompilerParams(vmem_limit_bytes=VMEM_LIMIT),
        cost_estimate=pl.CostEstimate(flops=flops, bytes_accessed=moved, transcendentals=0),
    )(*args)


def layer_start(source, params, segments, route_col, placing):
    gains, weights, router_w, experts = params
    joined = "back" in source
    struct = jax.ShapeDtypeStruct
    count = route_col.shape[0]
    width = weights.shape[0]
    outs = [
        struct((count, width), BF16),
        struct((count, 3 * width), BF16),
        struct((count, LANES), F32),
        struct((count, width // 2), BF16),
        struct((count, width // 2), BF16),
        struct((count, width), F32),
        struct((count, 1), F32),
        struct((placing.shape[0], width), BF16),
    ]
    if joined:
        outs.append(struct((count, width), BF16))
    inputs = dict(
        source, gains=gains, seg_col=segments[0], seg_row=segments[1], weights=weights,
        placing=placing, router=router_w, route=route_col,
    )
    return staged_call(
        functools.partial(forward_kernel, experts=experts, joined=joined), inputs, outs, 3 * 10**9
    )


def hidden_end(back, taking, upstream, state, params):
    count, width = upstream.shape
    struct = jax.ShapeDtypeStruct
    outs = [struct((count, width), BF16), struct((count, width), F32), struct((1, width), F32)]
    given = dict(taking=taking, back=back, gains=params[0], dz=upstream, h=state["h"])
    return staged_call(hidden_kernel, given, outs, 3 * 10**8)


def layer_end(dattn, hidden_grad, inputs, state, params, segments, placing):
    gains, weights = params[:2]
    count, width = inputs.shape
    struct = jax.ShapeDtypeStruct
    outs = [
        struct((count, width), BF16),
        struct((count, 3 * width // 2), BF16),
        struct((count, 3 * width // 2), BF16),
        struct((1, width), F32),
    ]
    given = dict(
        gains=gains, dattn=dattn, seg_col=segments[0], seg_row=segments[1], weights=weights,
        qkv=state["qkv"], lse=state["lse"], a=inputs, dh=hidden_grad,
    )
    if placing is not None:
        given["placing"] = placing
        outs.append(struct((placing.shape[0], width), BF16))
    return staged_call(
        functools.partial(backward_kernel, spread=placing is not None), given, outs, 5 * 10**9
    )


def split_dot(left, right, left_dim, right_dim):
    high = left.astype(BF16)
    low = (left - high.astype(F32)).astype(BF16)
    return dot(high, right, left_dim, right_dim) + dot(low, right, left_dim, right_dim)


def expert_kernel(
    rows_ref, dz_ref, in_ref, out_ref, router_ref, hot_ref,
    dx_ref, act_ref, dpre_ref, dy_ref, g_router_ref, chance_ref, gate_ref, total_ref, *, experts,
):
    step = pl.program_id(0)
    rows = rows_ref[...]

    @pl.when(step == 0)
    def _():
        chances = expert_chances(rows, router_ref[...], experts)
        chance_ref[...] = chances
        gate = jnp.sum(chances * hot_ref[...], axis=-1, keepdims=True)
        dy_ref[...] = (gate * dz_ref[...].astype(F32)).astype(BF16)
        gate_ref[...] = jnp.zeros_like(gate_ref)
        total_ref[...] = jnp.zeros_like(total_ref)

    before = dot(rows, in_ref[...], 1, 0)
    square = before * before
    bent = jnp.tanh(SLOPE * before * (1.0 + CUBIC * square))
    lifted = 0.5 * (1.0 + bent)
    act = (before * lifted).astype(BF16)
    slope = lifted + 0.5 * before * (1.0 - bent * bent) * (
        SLOPE * (1.0 + 3.0 * CUBIC * square)
    )
    act_grad = dot(dy_ref[...], out_ref[...], 1, 1)
    dpre = (act_grad * slope).astype(BF16)
    act_ref[...] = act
    dpre_ref[...] = dpre
    gate_ref[...] += jnp.sum(act_grad * act.astype(F32), axis=-1, keepdims=True)
    total_ref[...] += dot(dpre, in_ref[...], 1, 1)

    @pl.when(step == pl.num_programs(0) - 1)
    def _():
        logit_grad = (hot_ref[...] - chance_ref[...]) * gate_ref[...]
        g_router_ref[...] = split_dot(logit_grad, rows, 0, 0)
        dx_ref[...] = (total_ref[...] + split_dot(logit_grad, router_ref[...], 1, 0)).astype(
            dx_ref.dtype
        )


def expert_back(rows, dz, in_w, expert_w, layer, router_w, hot_row, experts, kind):
    count, width = rows.shape
    hidden = in_w.shape[1]
    block = 512
    struct = jax.ShapeDtypeStruct
    whole = pl.BlockSpec((count, width), lambda j: (0, 0))
    wide = pl.BlockSpec((count, block), lambda j: (0, j))
    router_spec = pl.BlockSpec((LANES, width), lambda j: (0, 0))
    return pl.pallas_call(
        functools.partial(expert_kernel, experts=experts),
        grid=(hidden // block,),
        out_shape=[
            struct((count, width), kind),
            struct((count, hidden), BF16),
            struct((count, hidden), BF16),
            struct((count, width), BF16),
            struct((LANES, width), F32),
        ],
        in_specs=[
            whole,
            whole,
            pl.BlockSpec((width, block), lambda j: (0, j)),
            pl.BlockSpec((None, block, width), lambda j: (layer, j, 0)),
            router_spec,
            pl.BlockSpec((1, LANES), lambda j: (0, 0)),
        ],
        out_specs=[whole, wide, wide, whole, router_spec],
        scratch_shapes=[
            pltpu.VMEM((count, LANES), F32),
            pltpu.VMEM((count, 1), F32),
            pltpu.VMEM((count, width), F32),
        ],
        compiler_params=pltpu.CompilerParams(
            dimension_semantics=("arbitrary",), vmem_limit_bytes=VMEM_LIMIT
        ),
        cost_estimate=pl.CostEstimate(
            flops=6 * count * width * hidden, bytes_accessed=12 * 10**6, transcendentals=0
        ),
    )(rows, dz, in_w, expert_w, router_w, hot_row)


def across_parts(grad, section):
    width = grad.shape[0]
    count = lax.axis_size("dp")
    halves = grad.reshape(count, 2, width // count // 2, -1)
    keep = lax.dynamic_index_in_dim(halves, section, 1, keepdims=False)
    send = lax.dynamic_index_in_dim(halves, 1 - section, 1, keepdims=False)
    return (keep, send.astype(BF16))


def across_sum(keep, send):
    return (keep + swap(send, "section").astype(F32)).astype(BF16)


def exchange_across(grad, section):
    return across_sum(*across_parts(grad, section))


def pair_up(values, tensor):
    half = values.shape[0] // 2
    halves = values.reshape(2, half, -1)
    own = entry(halves, tensor)
    other = swap(entry(halves, 1 - tensor), "tensor")
    return ordered(tensor, own[None], other[None])


def by_section(pairs, fars, section):
    own = jnp.where(section == 0, pairs[0], pairs[1])
    return ordered(section, own, jnp.where(section == 0, fars[0], fars[1]))


def gelu_pair(before, active_grad):
    activated, back = jax.vjp(smooth_gate, before)
    return (activated.astype(BF16), back(active_grad)[0].astype(BF16))


def shards(
    x_in, d_out, lengths, routes, gain_attn, w_qkv, w_attn_out, gain_ffn, w_router, w_in, w_exp_out
):
    section = lax.axis_index("section")
    tensor = lax.axis_index("tensor")
    count = lax.axis_size("dp")
    width = x_in.shape[2]
    part = width // 2
    rows = 2 * x_in.shape[1]
    experts = w_router.shape[2]
    own_batch = 2 * section + tensor
    peer_batch = 2 * section + 1 - tensor

    def of_layer(layer, own, other):
        return jnp.where(section == layer, own, other)

    def by_layer(own):
        other = swap(own, "section")
        return [of_layer(layer, own, other) for layer in range(2)]

    def whole_group(array):
        return ordered(
            tensor, entry(array, own_batch), swap(entry(array, peer_batch), "tensor")
        )

    packed = jnp.concatenate([w_qkv[0], w_attn_out[0].T[None]], axis=0)
    packed = jnp.moveaxis(packed, 0, 1).reshape(width // count, -1)
    small = by_layer(jnp.concatenate([gain_attn, gain_ffn, w_router[0].T], axis=0))
    own_route = entry(routes[0, :, :, 0], own_batch)
    other_route = swap(entry(routes[0, :, :, 0], 2 * (1 - section) + tensor), "section")
    route = [of_layer(layer, own_route, other_route) for layer in range(2)]
    first_pack = of_layer(0, packed, one_way(packed, "section", 0, 1))
    first_beside = swap(first_pack, "tensor")
    first_packs = jnp.concatenate([first_pack, first_beside], axis=1)
    first_w = lax.all_gather(first_packs, "dp", axis=0, tiled=True)
    x_own = whole_group(x_in)
    later_pack, d_last = after((packed, d_out), first_beside)
    second_pack = of_layer(1, packed, one_way(later_pack, "section", 1, 0))
    second_pack = jnp.concatenate([second_pack, swap(second_pack, "tensor")], axis=1)
    dz_last = whole_group(d_last)
    far_in = swap(w_in[0, 0], "section")
    in_w = [of_layer(layer, w_in[0, 0], far_in) for layer in range(2)]
    both_out = lax.all_gather(after(w_exp_out[0, 0], first_packs), "section", axis=0)
    expert_w = [both_out[0], both_out[1]]

    tables = [routing(row, experts) for row in route]
    placing = [table[0] for table in tables]
    taking = [table[1] for table in tables]
    route_col = [row[:, None] for row in route]
    gains = [small[layer][:2].astype(F32) for layer in range(2)]
    router_w = [jnp.pad(small[layer][2:], ((0, LANES - experts), (0, 0))) for layer in range(2)]
    bounds = jnp.cumsum(entry(lengths[:, 0], own_batch))
    places = jnp.arange(rows, dtype=jnp.int32)
    segment = jnp.sum((places[:, None] >= bounds[None, :]).astype(jnp.int32), axis=1)
    segments = (segment[:, None], segment[None, :])
    hot_row = (
        jnp.arange(LANES, dtype=jnp.int32)[None, :] == lax.axis_index("dp")
    ).astype(F32)
    keys = ("xn", "qkv", "lse", "o", "o_far", "h", "gate")

    def expert_forward(values, layer):
        active = smooth_gate(dot(values, in_w[layer], 1, 0)).astype(BF16)
        return dot(active, expert_w[layer], 1, 0)

    def fold(own, peer):
        own = lax.optimization_barrier(own)
        return (own + swap(peer.astype(BF16), "tensor").astype(F32)).astype(BF16)

    params0 = (gains[0], first_w, router_w[0], experts)
    *state0, outgoing0 = layer_start(
        {"a": after(x_own, far_in)}, params0, segments, route_col[0], placing[0]
    )
    state0 = dict(zip(keys, state0))
    mine0 = all_to_all(outgoing0)
    side_xn0 = swap(state0["xn"], "tensor")
    side_o0 = swap(state0["o_far"], "tensor")
    peer0 = swap(
        after(mine0, side_xn0, side_o0, in_w), "tensor"
    )
    second_w = lax.all_gather(after(second_pack, mine0), "dp", axis=0, tiled=True)
    back0 = all_to_all(fold(expert_forward(mine0, 0), expert_forward(peer0, 0)))

    far_mine0 = one_way(after(mine0, peer0), "section", 1, 0)
    far_peer0 = one_way(after(peer0, back0), "section", 1, 0)
    dz_out1 = dot(placing[1], dz_last, 1, 0).astype(BF16)
    mine_dz1 = all_to_all(after(dz_out1, back0))
    params1 = (gains[1], second_w, router_w[1], experts)
    *state1, outgoing1, out0 = layer_start(
        {"taking": taking[0], "back": after(back0, far_mine0), "h_before": state0["h"],
         "gate_before": state0["gate"]},
        params1, segments, route_col[1], placing[1],
    )
    state1 = dict(zip(keys, state1))
    peer_dz1 = swap(mine_dz1, "tensor")
    pair_out0 = pair_up(out0, tensor)
    mine1 = all_to_all(after(outgoing1, mine_dz1, pair_out0, far_peer0))
    peer1 = swap(after(mine1, peer_dz1), "tensor")

    def both_back(layer, mine, peer, mine_dz, peer_dz):
        args = (in_w[layer], both_out, layer, router_w[layer], hot_row, experts)
        own = expert_back(mine, mine_dz, *args, F32)
        peer, peer_dz = after((peer, peer_dz), own[0])
        return (own, expert_back(peer, peer_dz, *args, BF16))

    own_b1, peer_b1 = both_back(1, mine1, peer1, mine_dz1, peer_dz1)
    peer_dx1 = swap(peer_b1[0], "tensor")
    far_mine1 = one_way(mine1, "section", 0, 1)
    far_peer1 = one_way(after(peer1, own_b1[0]), "section", 0, 1)
    far_out0 = one_way(pair_out0, "section", 1, 0)
    far_peer0 = one_way(after(peer0, own_b1[0]), "section", 1, 0)
    dback1 = all_to_all(
        after((own_b1[0] + peer_dx1.astype(F32)).astype(BF16), far_mine1)
    )
    late_mine1, late_peer1 = after((mine1, peer1), peer_b1[0])
    peer_y1 = expert_forward(late_peer1, 1).astype(BF16)
    own_y1 = expert_forward(late_mine1, 1)
    side_y1 = swap(after(peer_y1, peer_dx1), "tensor")
    total_y1 = (own_y1 + side_y1.astype(F32)).astype(BF16)
    side_xn1, side_o1 = [
        swap(half, "tensor")
        for half in after((state1["xn"], state1["o_far"]), peer_dx1)
    ]
    dattn1, dh1, gain_f1 = hidden_end(
        after(dback1, own_y1, peer_y1, side_xn1, side_o1, far_out0, far_peer1), taking[1], dz_last, state1, params1
    )
    side_dattn1 = swap(dattn1, "tensor")
    grad1, dqkv1, dqkv_far1, gain_a1, outgoing_dz0 = layer_end(
        dattn1, dh1, out0, state1, params1, segments, placing[0]
    )

    mine_dz0 = all_to_all(outgoing_dz0)
    side_dqkv1 = swap(dqkv_far1, "tensor")
    def stack(first, second):
        return jnp.concatenate([first, second], axis=0)

    def attention_grad(xn, side_xn, dqkv, side_dqkv):
        return dot(stack(xn, side_xn), stack(dqkv, side_dqkv), 0, 0)

    def output_grad(dattn, side_dattn, mixed, side_mixed):
        return dot(stack(dattn, side_dattn), stack(mixed, side_mixed), 0, 0)

    full1 = jnp.concatenate(
        [
            attention_grad(state1["xn"], side_xn1, dqkv1, side_dqkv1),
            output_grad(dattn1, side_dattn1, state1["o"], side_o1),
        ],
        axis=1,
    )
    keep1, send1 = across_parts(full1, section)
    peer_dz0 = swap(after(mine_dz0, send1, side_y1), "tensor")
    across1 = swap(send1, "section")
    back1 = all_to_all(after(total_y1, mine_dz0))
    peer_dz0 = after(peer_dz0, across1, back1)
    own_b0, peer_b0 = both_back(0, mine0, peer0, mine_dz0, peer_dz0)
    keep1, across1 = after((keep1, across1), own_b0[0])
    reduced1 = all_to_all((keep1 + across1.astype(F32)).astype(BF16))
    peer_dx0 = swap(peer_b0[0], "tensor")
    pair_grad1 = pair_up(after(grad1, peer_dx0), tensor)
    far_grad1 = one_way(pair_grad1, "section", 0, 1)

    def pick(first, second, index=section):
        return jnp.where(index == 0, first, second)

    def gather_rows(number, index):
        return stack((own_b0, own_b1)[number][index], (peer_b0, peer_b1)[number][index])

    late_mine0, late_mine1, own_b1, peer_b1 = after((mine0, mine1, own_b1, peer_b1), peer_b0[0])
    near_rows = pick(stack(late_mine0, peer0), stack(late_mine1, peer1))
    near_dpre = pick(gather_rows(0, 2), gather_rows(1, 2))
    near_in = dot(near_rows, near_dpre, 0, 0)
    far_dys1 = [
        one_way(after(part_b1[3], peer_b0[0]), "section", 0, 1) for part_b1 in (own_b1, peer_b1)
    ]
    far_dys0 = [
        one_way(after(part_b0[3], peer_b0[0]), "section", 1, 0) for part_b0 in (own_b0, peer_b0)
    ]
    total_dx0 = after(
        (own_b0[0] + peer_dx0.astype(F32)).astype(BF16), near_in, reduced1
    )
    dback0 = all_to_all(total_dx0)
    dy0, dy1 = (gather_rows(0, 3), gather_rows(1, 3))
    late = after(section, total_dx0)
    near_dy = pick(dy0, dy1)
    late_back1 = after(back1, total_dx0)
    out1 = (state1["h"] + state1["gate"] * dot(taking[1], late_back1, 1, 0)).astype(BF16)
    pair_out1 = pair_up(out1, tensor)
    far_out1 = one_way(pair_out1, "section", 0, 1)
    near_act = pick(gather_rows(0, 1), gather_rows(1, 1), late)
    near_out = dot(near_act, near_dy, 0, 0)
    dattn0, dh0, gain_f0 = hidden_end(
        after(dback0, near_out, pair_out1), taking[0], grad1, state0, params0
    )
    side_dattn0 = swap(dattn0, "tensor")
    grad0, dqkv0, dqkv_far0, gain_a0 = layer_end(
        dattn0, dh0, x_own, state0, params0, segments, None
    )

    side_dqkv0 = swap(dqkv_far0, "tensor")
    late_dattn0, late_side = after((dattn0, side_dattn0), dqkv0)
    out_keep, out_send = across_parts(
        output_grad(late_dattn0, late_side, state0["o"], side_o0), section
    )
    smalls = jnp.stack(
        [
            jnp.concatenate([*gain, (own[4] + peer[4])[:experts]], axis=0)
            for gain, own, peer in (
                ((gain_a0, gain_f0), own_b0, peer_b0), ((gain_a1, gain_f1), own_b1, peer_b1)
            )
        ]
    )
    smalls = after(smalls, out_send)
    smalls = all_to_all(jnp.broadcast_to(smalls[None], (count,) + smalls.shape))
    smalls = smalls.sum(axis=0)
    ready_xn0 = after(state0["xn"], out_send)
    qkv_keep, qkv_send = across_parts(
        attention_grad(ready_xn0, side_xn0, dqkv0, side_dqkv0), section
    )
    late = after(section, qkv_send)
    far_rows = stack(pick(far_mine0, far_mine1, late), pick(far_peer0, far_peer1, late))
    far_dy = stack(pick(far_dys0[0], far_dys1[0], late), pick(far_dys0[1], far_dys1[1], late))
    far_before = dot(far_rows, w_in[0, 0], 1, 0)
    half0 = jnp.concatenate(
        [
            across_sum(after(qkv_keep, far_before, far_dy), qkv_send),
            across_sum(out_keep, out_send),
        ],
        axis=2,
    )
    reduced0 = all_to_all(half0)
    pair_grad0 = pair_up(after(grad0, qkv_send), tensor)
    far_grad0 = one_way(after(pair_grad0, half0), "section", 1, 0)
    far_dy, reduced1 = after((far_dy, reduced1), half0)
    far_act, far_dpre = gelu_pair(far_before, dot(far_dy, w_exp_out[0, 0], 1, 1))
    in_w_grad = near_in + dot(far_rows, far_dpre, 0, 0)
    expert_w_grad = near_out + dot(far_act, far_dy, 0, 0)

    smalls = after(smalls, qkv_send)
    smalls = smalls + swap(smalls, "tensor")
    own_small = pick(smalls[0], smalls[1]) + swap(pick(smalls[1], smalls[0]), "section")

    reduced1 = reduced1.astype(F32).sum(axis=0)
    reduced0 = after(reduced0, in_w_grad, expert_w_grad, far_grad0, far_out1, own_small)
    reduced0 = reduced0.astype(F32).sum(axis=0)
    own_half = pick(reduced0, reduced1)
    other_half = swap(pick(reduced1, reduced0).astype(BF16), "section").astype(F32)
    joined = ordered(section, own_half, other_half)
    qkv_grad = jnp.stack([joined[:, part * kind:part * (kind + 1)] for kind in range(3)])
    out_grad = joined[:, 3 * part:].T
    section_out = by_section([pair_out0, pair_out1], [far_out0, far_out1], section)
    section_in_grad = by_section([pair_grad0, pair_grad1], [far_grad0, far_grad1], section)
    return (
        section_out[None],
        section_in_grad[None],
        own_small[0][None],
        qkv_grad[None],
        out_grad[None],
        own_small[1][None],
        own_small[2:].T[None],
        in_w_grad[None, None],
        expert_w_grad[None, None],
    )


def solution(mesh):
    in_specs = (
        P(None, ("dp", "tensor"), None),
        P(None, ("dp", "tensor"), None),
        P(None, "dp", None),
        P("section", None, "dp", None),
        P("section", None),
        P("section", None, "dp", "tensor"),
        P("section", "tensor", "dp"),
        P("section", None),
        P("section", None, None),
        P("section", "dp", None, "tensor"),
        P("section", "dp", "tensor", None),
    )
    out_specs = (
        P("section", None, ("dp", "tensor"), None),
        P("section", None, ("dp", "tensor"), None),
        P("section", None),
        P("section", None, "dp", "tensor"),
        P("section", "tensor", "dp"),
        P("section", None),
        P("section", None, None),
        P("section", "dp", None, "tensor"),
        P("section", "dp", "tensor", None),
    )
    return jax.shard_map(shards, mesh=mesh, in_specs=in_specs, out_specs=out_specs, check_vma=False)
```

profile of v0, /device:TPU:0, one launch (start us, length us, event | category | flops | bytes accessed | tf_op | source)
XLA Modules:
  0.0 622.9 jit_solution(15583706398089032341)
XLA Ops:
  8.3 4.9 collective-permute-start.4
  13.2 6.2 collective-permute-done.4
  21.0 6.4 %collective-permute-done.5 = bf16[96,1536]{1,0:T(8,128)(2,1)S(1)} collective-permute-done((bf16[96,1536]{1,0:T(8,128)(2,1)S(1)}, bf16[96,1536]{1,0:T(8,128)(2,1)S(1)}, u32[]{:S(2)}, u32[]{:S(2)}) %collective-permute-start.5) | collective-permute-done | bytes 294944 | tf_op jit(solution)/shard_map/ppermute | solution.py:23
  29.0 2.5 collective-permute-start.2
  37.4 44.0 %collective-permute-done = s32[256]{0:T(256)S(1)} collective-permute-done((s32[256]{0:T(256)S(1)}, s32[256]{0:T(256)S(1)}, u32[]{:S(2)}, u32[]{:S(2)}) %collective-permute-start) | collective-permute-done | bytes 1056 | tf_op jit(solution)/shard_map/ppermute | solution.py:23
  86.7 8.9 %shard_map.178 = (bf16[256,768]{1,0:T(8,128)(2,1)}, bf16[256,2304]{1,0:T(8,128)(2,1)}, f32[256,128]{1,0:T(8,128)}, bf16[256,384]{1,0:T(8,128)(2,1)}, bf16[256,38...) custom-call(bf16[256,768]{1,0:T(8,128)(2,1)} %maximum_select_fusion.11.refs_0_.refs_7_, ...), custom_call_target="tpu_custom_call" | custom-call | flops 3000000000 | bytes 9250816 | tf_op jit(solution)/shard_map/pallas_call | solution.py:290
  95.6 4.8 all-to-all-start
  103.1 7.8 %collective-permute-done.12 = bf16[96,1536]{1,0:T(8,128)(2,1)S(1)} collective-permute-done((bf16[96,1536]{1,0:T(8,128)(2,1)S(1)}, bf16[96,1536]{1,0:T(8,128)(2,1)S(1)}, u32[]{:S(2)}, u32[]{:S(2)}) %collective-permute-start.12) | collective-permute-done | bytes 294944 | tf_op jit(solution)/shard_map/ppermute | solution.py:23
  111.9 9.5 %all-to-all-done = bf16[8,64,768]{2,1,0:T(8,128)(2,1)S(1)} async-done(((bf16[8,64,768]{2,1,0:T(8,128)(2,1)}), bf16[8,64,768]{2,1,0:T(8,128)(2,1)S(1)}, u32[]{:S(2)}, u32[]{:S(2)}) %all-to-all-start) | async-done | bytes 786464 | tf_op jit(solution)/shard_map/all_to_all | solution.py:31
  123.5 4.2 broadcast_select_fusion
  129.6 7.1 %collective-permute-done.6 = bf16[256,768]{1,0:T(8,128)(2,1)S(1)} collective-permute-done((bf16[256,768]{1,0:T(8,128)(2,1)}, bf16[256,768]{1,0:T(8,128)(2,1)S(1)}, u32[]{:S(2)}, u32[]{:S(2)}) %collective-permute-start.6) | collective-permute-done | bytes 393248 | tf_op jit(solution)/shard_map/ppermute | solution.py:23
  138.9 6.5 %all-gather.9.cloned.1.call-done = bf16[3072,768]{1,0:T(8,128)(2,1)} async-done(((bf16[1536,768]{1,0:T(8,128)(2,1)}), bf16[3072,768]{1,0:T(8,128)(2,1)}) %all-gather.9.cloned.1.call-update) | async-done | bytes 4718608 | tf_op jit(solution)/shard_map/all_gather | solution.py:523
  145.4 10.3 %collective-permute-done.8.rows_ref = bf16[512,768]{1,0:T(8,128)(2,1)} collective-permute-done((bf16[512,768]{1,0:T(8,128)(2,1)S(1)}, bf16[512,768]{1,0:T(8,128)(2,1)}, u32[]{:S(2)}, u32[]{:S(2)}) %collective-permute-start.8) | collective-permute-done | bytes 786464 | tf_op jit(solution)/shard_map/ppermute | solution.py:23
  155.7 6.3 %fusion.93 = bf16[512,768]{1,0:T(8,128)(2,1)} fusion(bf16[3072,768]{1,0:T(8,128)(2,1)} %all-gather.9.cloned.1.call-done, bf16[512,768]{1,0:T(8,128)(2,1)} %collective-permute-done.8.rows_ref, bf16[768,1536]{1,0:T(8,128)(2,1)} %get-tuple-element.239.in_ref), kind=kOutput, calls=%fused_computation.118 | convolution fusion | flops 2423390208 | bytes 6291456 | tf_op jit(solution)/shard_map/dot_general | solution.py:39
  163.6 5.7 fusion.61
  169.3 10.9 %collective-permute-done.9 = bf16[512,768]{1,0:T(8,128)(2,1)} collective-permute-done((bf16[512,768]{1,0:T(8,128)(2,1)}, bf16[512,768]{1,0:T(8,128)(2,1)}, u32[]{:S(2)}, u32[]{:S(2)}) %collective-permute-start.9) | collective-permute-done | bytes 786464 | tf_op jit(solution)/shard_map/ppermute | solution.py:23
  180.2 2.6 add_convert_fusion.5
  182.9 4.4 all-to-all-start.1
  189.9 5.3 collective-permute-done.14
  197.9 16.2 %all-to-all-done.1 = bf16[8,64,768]{2,1,0:T(8,128)(2,1)S(1)} async-done(((bf16[8,64,768]{2,1,0:T(8,128)(2,1)}), bf16[8,64,768]{2,1,0:T(8,128)(2,1)S(1)}, u32[]{:S(2)}, u32[]{:S(2)}) %all-to-all-start.1) | async-done | bytes 786464 | tf_op jit(solution)/shard_map/all_to_all | solution.py:31
  214.9 3.5 all-to-all-start.2
  221.4 9.4 %shard_map.179 = (bf16[256,768]{1,0:T(8,128)(2,1)}, bf16[256,2304]{1,0:T(8,128)(2,1)}, f32[256,128]{1,0:T(8,128)}, bf16[256,384]{1,0:T(8,128)(2,1)}, bf16[256,38...) custom-call(bf16[256,512]{1,0:T(8,128)(2,1)} %fusion.135.refs_0_, ...), custom_call_target="tpu_custom_call" | custom-call | flops 3000000000 | bytes 11086848 | tf_op jit(solution)/shard_map/pallas_call | solution.py:290
  233.4 5.8 collective-permute-done.13
  240.6 4.7 all-to-all-start.3
  246.9 18.6 %collective-permute-done.15.dz_ref = bf16[512,768]{1,0:T(8,128)(2,1)} collective-permute-done((bf16[512,768]{1,0:T(8,128)(2,1)S(1)}, bf16[512,768]{1,0:T(8,128)(2,1)}, u32[]{:S(2)}, u32[]{:S(2)}) %collective-permute-start.15) | collective-permute-done | bytes 786464 | tf_op jit(solution)/shard_map/ppermute | solution.py:23
  268.5 10.9 %shard_map.180 = (f32[512,768]{1,0:T(8,128)}, bf16[512,1536]{1,0:T(8,128)(2,1)}, bf16[512,1536]{1,0:T(8,128)(2,1)}, bf16[512,768]{1,0:T(8,128)(2,1)}, f32[128,768]{1,0:T(8,128)}) custom-call(bf16[512,768]{1,0:T(8,128)(2,1)} %bitcast.31.rows_ref, bf16[512,768]{1,0:T(8,128)(2,1)} %bitcast.164, bf16[768,1536]{1,0:T(8,128)(2,1)} %get-tuple-element.238.in_ref, ...), custom_call_target="tpu_custom_call" | custom-call | flops 3623878656 | bytes 12000000 | tf_op jit(solution)/shard_map/pallas_call | solution.py:413
  279.4 6.4 %collective-permute-done.16.rows_ref = bf16[512,768]{1,0:T(8,128)(2,1)S(1)} collective-permute-done((bf16[512,768]{1,0:T(8,128)(2,1)}, bf16[512,768]{1,0:T(8,128)(2,1)S(1)}, u32[]{:S(2)}, u32[]{:S(2)}) %collective-permute-start.16) | collective-permute-done | bytes 786464 | tf_op jit(solution)/shard_map/ppermute | solution.py:23
  286.6 10.9 %shard_map.181 = (bf16[512,768]{1,0:T(8,128)(2,1)}, bf16[512,1536]{1,0:T(8,128)(2,1)}, bf16[512,1536]{1,0:T(8,128)(2,1)}, bf16[512,768]{1,0:T(8,128)(2,1)}, f32[128,768]{1,0:T(8,128)}) custom-call(bf16[512,768]{1,0:T(8,128)(2,1)} %copy-done.43, bf16[512,768]{1,0:T(8,128)(2,1)} %collective-permute-done.15.dz_ref, ...), custom_call_target="tpu_custom_call" | custom-call | flops 3623878656 | bytes 12000000 | tf_op jit(solution)/shard_map/pallas_call | solution.py:413
  299.1 3.4 collective-permute-start.19
  302.5 5.6 fusion.98
  308.1 8.0 %collective-permute-done.17 = bf16[512,768]{1,0:T(8,128)(2,1)} collective-permute-done((bf16[512,768]{1,0:T(8,128)(2,1)}, bf16[512,768]{1,0:T(8,128)(2,1)}, u32[]{:S(2)}, u32[]{:S(2)}) %collective-permute-start.17) | collective-permute-done | bytes 786464 | tf_op jit(solution)/shard_map/ppermute | solution.py:23
  317.6 2.7 add_convert_fusion.3
  321.2 3.5 all-to-all-start.4
  324.7 4.3 collective-permute-start.23
  333.7 5.7 add_convert_fusion.4
  339.4 3.6 collective-permute-done.22
  343.0 2.7 collective-permute-done.23
  347.9 3.1 shard_map.182
  351.0 11.8 %shard_map.183 = (bf16[256,768]{1,0:T(8,128)(2,1)}, bf16[256,1152]{1,0:T(8,128)(2,1)}, bf16[256,1152]{1,0:T(8,128)(2,1)}, f32[1,768]{1,0:T(1,128)}, bf16[512,768]{1,0:T(8,128)(2,1)}) custom-call(f32[2,768]{1,0:T(2,128)} %slice_convert_fusion.refs_4_.refs_2_.refs_0_, bf16[256,768]{1,0:T(8,128)(2,1)} %get-tuple-element.155.refs_1_, ...), custom_call_target="tpu_custom_call" | custom-call | flops 5000000000 | bytes 10234880 | tf_op jit(solution)/shard_map/pallas_call | solution.py:290
  365.0 5.0 all-to-all-start.5
  370.1 16.0 %collective-permute-done.25 = bf16[256,768]{1,0:T(8,128)(2,1)S(1)} collective-permute-done((bf16[256,768]{1,0:T(8,128)(2,1)S(1)}, bf16[256,768]{1,0:T(8,128)(2,1)S(1)}, u32[]{:S(2)}, u32[]{:S(2)}) %collective-permute-start.25) | collective-permute-done | bytes 393248 | tf_op jit(solution)/shard_map/ppermute | solution.py:23
  395.0 4.5 all-to-all-start.6
  402.0 10.9 %shard_map.184 = (f32[512,768]{1,0:T(8,128)}, bf16[512,1536]{1,0:T(8,128)(2,1)}, bf16[512,1536]{1,0:T(8,128)(2,1)}, bf16[512,768]{1,0:T(8,128)(2,1)}, f32[128,768]{1,0:T(8,128)}) custom-call(bf16[512,768]{1,0:T(8,128)(2,1)} %bitcast.160, bf16[512,768]{1,0:T(8,128)(2,1)} %bitcast.36.dz_ref, bf16[768,1536]{1,0:T(8,128)(2,1)} %get-tuple-element.239.in_ref, ...), custom_call_target="tpu_custom_call" | custom-call | flops 3623878656 | bytes 12000000 | tf_op jit(solution)/shard_map/pallas_call | solution.py:413
  412.8 6.4 %collective-permute-done.27 = bf16[8,48,1536]{2,1,0:T(8,128)(2,1)S(1)} collective-permute-done((bf16[8,48,1536]{2,1,0:T(8,128)(2,1)S(1)}, bf16[8,48,1536]{2,1,0:T(8,128)(2,1)S(1)}, u32[]{:S(2)}, u32[]{:S(2)}) %collective-permute-start.27) | collective-permute-done | bytes 1179680 | tf_op jit(solution)/shard_map/ppermute | solution.py:23
  420.6 4.3 all-to-all-start.7
  426.4 10.9 %shard_map.185 = (bf16[512,768]{1,0:T(8,128)(2,1)}, bf16[512,1536]{1,0:T(8,128)(2,1)}, bf16[512,1536]{1,0:T(8,128)(2,1)}, bf16[512,768]{1,0:T(8,128)(2,1)}, f32[128,768]{1,0:T(8,128)}) custom-call(bf16[512,768]{1,0:T(8,128)(2,1)} %collective-permute-done.8.rows_ref, bf16[512,768]{1,0:T(8,128)(2,1)} %collective-permute-done.26.dz_ref, ...), custom_call_target="tpu_custom_call" | custom-call | flops 3623878656 | bytes 12000000 | tf_op jit(solution)/shard_map/pallas_call | solution.py:413
  438.0 6.3 %collective-permute-start.39 = (bf16[512,768]{1,0:T(8,128)(2,1)}, bf16[512,768]{1,0:T(8,128)(2,1)}, u32[]{:S(2)}, u32[]{:S(2)}) collective-permute-start(bf16[512,768]{1,0:T(8,128)(2,1)} %get-tuple-element.217), channel_id=1, source_target_pairs={{0,16},{1,17},{2,18},{3,19},{4,20},{5,21},{6,22},{7,23},{8,24},{9,... | collective-permute-start | bytes 2359304 | tf_op jit(solution)/shard_map/ppermute | solution.py:27
  449.3 7.5 %fusion.39 = f32[768,1536]{1,0:T(8,128)} fusion(bf16[512,1536]{1,0:T(8,128)(2,1)} %get-tuple-element.181, bf16[512,1536]{1,0:T(8,128)(2,1)} %get-tuple-element.180, bf16[512,1536]{1,0:T(8,128)(2,1)S(1)} %copy-done.57, bf16[512,1536]{1,0:T(8,128)(2,1)S(1)} %copy-done.56, pred[]{:T(512)S(6)} %eq.58, bf16[512,768]{1,0:T(8,128)(2,1)} %collective-permute-done.8.rows_ref, ...), kind=kOutput, calls=%fused_computation.50 | convolution fusion | flops 2437152768 | bytes 14155777 | tf_op jit(solution)/shard_map/dot_general | solution.py:39
  458.6 4.9 all-to-all-start.8
  465.9 5.4 collective-permute-done.29
  472.7 5.6 collective-permute-start.30
  478.3 8.7 %fusion.45 = f32[1536,768]{1,0:T(8,128)} fusion(bf16[512,1536]{1,0:T(8,128)(2,1)} %get-tuple-element.190, bf16[512,1536]{1,0:T(8,128)(2,1)} %get-tuple-element.189, bf16[512,1536]{1,0:T(8,128)(2,1)} %get-tuple-element.192, bf16[512,1536]{1,0:T(8,128)(2,1)} %get-tuple-element.191, pred[]{:T(512)S(6)} %eq.158, bf16[512,768]{1,0:T(8,128)(2,1)} %get-tuple-element.216, ...), kind=kOutput, calls=%fused_computation.57 | convolution fusion | flops 2437152768 | bytes 14155778 | tf_op jit(solution)/shard_map/dot_general | solution.py:39
  488.0 3.1 shard_map.186
  491.8 11.2 %shard_map.187 = (bf16[256,768]{1,0:T(8,128)(2,1)}, bf16[256,1152]{1,0:T(8,128)(2,1)}, bf16[256,1152]{1,0:T(8,128)(2,1)}, f32[1,768]{1,0:T(1,128)}) custom-call(f32[2,768]{1,0:T(2,128)} %slice_convert_fusion.1.refs_1_.refs_2_.refs_0_, bf16[256,768]{1,0:T(8,128)(2,1)} %get-tuple-element.205.refs_1_, s32[256,1]{1,0:T(8,128)} %copy.53.refs_2_.refs_5_, ...), custom_call_target="tpu_custom_call" | custom-call | flops 5000000000 | bytes 9186304 | tf_op jit(solution)/shard_map/pallas_call | solution.py:290
  510.9 4.7 all-to-all-start.9
  528.9 3.6 collective-permute-start.41
  534.5 11.2 %collective-permute-done.38 = bf16[512,768]{1,0:T(8,128)(2,1)} collective-permute-done((bf16[512,768]{1,0:T(8,128)(2,1)}, bf16[512,768]{1,0:T(8,128)(2,1)}, u32[]{:S(2)}, u32[]{:S(2)}) %collective-permute-start.38) | collective-permute-done | bytes 786464 | tf_op jit(solution)/shard_map/ppermute | solution.py:27
  548.2 5.2 fusion.116
  560.7 4.7 collective-permute-start.43
  565.4 4.5 collective-permute-done.45
  573.6 4.4 all-to-all-start.10
  578.0 15.1 %convolution_add_fusion.1 = f32[768,1536]{1,0:T(8,128)} fusion(f32[768,1536]{1,0:T(8,128)} %fusion.39, f32[1024,1536]{1,0:T(8,128)} %fusion.116, bf16[512,768]{1,0:T(8,128)(2,1)} %copy-done.21, bf16[512,768]{1,0:T(8,128)(2,1)} %copy-done.20, bf16[1024,768]{1,0:T(8,128)(2,1)} %pad_maximum_fusion.2, bf16[1,1,1536,768]{3,2,1,0:T(8,128)(2,1)} %param.21), kind=kOutput, calls=%fused_computation.16 | convolution fusion | flops 4867620864 | bytes 21233664 | tf_op jit(solution)/shard_map/dot_general | solution.py:39
  594.6 10.5 %convolution_add_fusion = f32[1536,768]{1,0:T(8,128)} fusion(f32[1536,768]{1,0:T(8,128)} %fusion.45, bf16[1024,768]{1,0:T(8,128)(2,1)} %pad_maximum_fusion.2, f32[1024,1536]{1,0:T(8,128)} %fusion.116), kind=kOutput, calls=%fused_computation.15 | convolution fusion | flops 2431254528 | bytes 17301504 | tf_op jit(solution)/shard_map/dot_general | solution.py:39
  610.4 4.2 collective-permute-done.46
  (289 shorter events, 129.9 us)
Async XLA Ops:
  7.2 79.5 %all-gather.5.cloned.1.call-start = ((), (), s32[]{:S(2)}) async-start(), calls=%async_computation.11 | async-start | bytes 5308416 | tf_op jit(solution)/shard_map/all_gather | solution.py:515
  8.3 11.1 %collective-permute-start.4 = (bf16[96,1536]{1,0:T(8,128)(2,1)S(1)}, bf16[96,1536]{1,0:T(8,128)(2,1)S(1)}, u32[]{:S(2)}, u32[]{:S(2)}) collective-permute-start(bf16[96,1536]{1,0:T(8,128)(2,1)S(1)} %bitcast.147), channel_id=1, source_target_pairs={{0,16},{1,17},{2,18},{3,19},{4,20},{5,21},{6,22},{7,23},{8,24},{9,... | collective-permute-start | bytes 884744 | tf_op jit(solution)/shard_map/ppermute | solution.py:27
  19.4 7.9 %collective-permute-start.5 = (bf16[96,1536]{1,0:T(8,128)(2,1)S(1)}, bf16[96,1536]{1,0:T(8,128)(2,1)S(1)}, u32[]{:S(2)}, u32[]{:S(2)}) collective-permute-start(bf16[96,1536]{1,0:T(8,128)(2,1)S(1)} %broadcast_select_fusion.7), channel_id=1, source_target_pairs={{0,1},{1,0},{2,3},{3,2},{4,5},{5,4},{6,7},{7,6},{8,9},{9,8},{10,11... | collective-permute-start | bytes 884744 | tf_op jit(solution)/shard_map/ppermute | solution.py:23
  28.3 117.1 %all-gather.9.cloned.1.call-start = ((), (), s32[]{:S(2)}) async-start(), calls=%async_computation.13 | async-start | bytes 7077888 | tf_op jit(solution)/shard_map/all_gather | solution.py:523
  29.0 57.6 %collective-permute-start.2 = (bf16[768,1536]{1,0:T(8,128)(2,1)S(1)}, bf16[768,1536]{1,0:T(8,128)(2,1)}, u32[]{:S(2)}, u32[]{:S(2)}) collective-permute-start(bf16[768,1536]{1,0:T(8,128)(2,1)S(1)} %bitcast.151), channel_id=1, source_target_pairs={{0,16},{16,0},{1,17},{17,1},{2,18},{18,2},{3,19},{19,3},{4,20},{20... | collective-permute-start | bytes 7077896 | tf_op jit(solution)/shard_map/ppermute | solution.py:23
  31.6 49.8 %collective-permute-start = (s32[256]{0:T(256)S(1)}, s32[256]{0:T(256)S(1)}, u32[]{:S(2)}, u32[]{:S(2)}) collective-permute-start(s32[256]{0:T(256)S(1)} %bitcast.189), channel_id=1, source_target_pairs={{0,16},{16,0},{1,17},{17,1},{2,18},{18,2},{3,19},{19,3},{4,20},{20... | collective-permute-start | bytes 3080 | tf_op jit(solution)/shard_map/ppermute | solution.py:23
  31.7 51.5 %collective-permute-start.3 = (bf16[10,768]{1,0:T(8,128)(2,1)S(1)}, bf16[10,768]{1,0:T(8,128)(2,1)S(1)}, u32[]{:S(2)}, u32[]{:S(2)}) collective-permute-start(bf16[10,768]{1,0:T(8,128)(2,1)S(1)} %pad_maximum_fusion.9), channel_id=1, source_target_pairs={{0,16},{16,0},{1,17},{17,1},{2,18},{18,2},{3,19},{19,3},{4,20},{20... | collective-permute-start | bytes 46088 | tf_op jit(solution)/shard_map/ppermute | solution.py:23
  34.7 49.8 %collective-permute-start.1 = (bf16[128,768]{1,0:T(8,128)(2,1)S(1)}, bf16[128,768]{1,0:T(8,128)(2,1)S(1)}, u32[]{:S(2)}, u32[]{:S(2)}) collective-permute-start(bf16[128,768]{1,0:T(8,128)(2,1)S(1)} %get-tuple-element.243), channel_id=1, source_target_pairs={{0,1},{1,0},{2,3},{3,2},{4,5},{5,4},{6,7},{7,6},{8,9},{9,8},{10,11... | collective-permute-start | bytes 589832 | tf_op jit(solution)/shard_map/ppermute | solution.py:23
  36.6 50.1 %copy-start.41 = (s32[256]{0:T(256)}, s32[256]{0:T(256)S(1)}, u32[]{:S(2)}) copy-start(s32[256]{0:T(256)S(1)} %convert_reduce_fusion.2) | copy-start | bytes 3076
  85.4 15.1 %collective-permute-start.11 = (bf16[96,1536]{1,0:T(8,128)(2,1)S(1)}, bf16[96,1536]{1,0:T(8,128)(2,1)}, u32[]{:S(2)}, u32[]{:S(2)}) collective-permute-start(bf16[96,1536]{1,0:T(8,128)(2,1)S(1)} %bitcast.149), channel_id=1, source_target_pairs={{16,0},{17,1},{18,2},{19,3},{20,4},{21,5},{22,6},{23,7},{24,8},{25... | collective-permute-start | bytes 884744 | tf_op jit(solution)/shard_map/ppermute | solution.py:27
  95.6 25.8 %all-to-all-start = ((bf16[8,64,768]{2,1,0:T(8,128)(2,1)}), bf16[8,64,768]{2,1,0:T(8,128)(2,1)S(1)}, u32[]{:S(2)}, u32[]{:S(2)}) async-start(bf16[8,64,768]{2,1,0:T(8,128)(2,1)} %bitcast.168), calls=%async_computation | async-start | bytes 1572864 | tf_op jit(solution)/shard_map/all_to_all | solution.py:31
  100.5 120.9 %all-gather.7.cloned.1.call-start = ((), (), s32[]{:S(2)}) async-start(), calls=%async_computation.12 | async-start | bytes 5308416 | tf_op jit(solution)/shard_map/all_gather | solution.py:560
  101.5 9.4 %collective-permute-start.12 = (bf16[96,1536]{1,0:T(8,128)(2,1)S(1)}, bf16[96,1536]{1,0:T(8,128)(2,1)S(1)}, u32[]{:S(2)}, u32[]{:S(2)}) collective-permute-start(bf16[96,1536]{1,0:T(8,128)(2,1)S(1)} %broadcast_select_fusion.6), channel_id=1, source_target_pairs={{0,1},{1,0},{2,3},{3,2},{4,5},{5,4},{6,7},{7,6},{8,9},{9,8},{10,11... | collective-permute-start | bytes 884744 | tf_op jit(solution)/shard_map/ppermute | solution.py:23
  121.4 73.8 %copy-start.22 = (bf16[8,64,768]{2,1,0:T(8,128)(2,1)}, bf16[8,64,768]{2,1,0:T(8,128)(2,1)S(1)}, u32[]{:S(2)}) copy-start(bf16[8,64,768]{2,1,0:T(8,128)(2,1)S(1)} %all-to-all-done) | copy-start | bytes 2359300
  121.5 8.1 %collective-permute-start.7 = (bf16[256,384]{1,0:T(8,128)(2,1)}, bf16[256,384]{1,0:T(8,128)(2,1)S(1)}, u32[]{:S(2)}, u32[]{:S(2)}) collective-permute-start(bf16[256,384]{1,0:T(8,128)(2,1)} %get-tuple-element.125), channel_id=1, source_target_pairs={{0,1},{1,0},{2,3},{3,2},{4,5},{5,4},{6,7},{7,6},{8,9},{9,8},{10,11... | collective-permute-start | bytes 589832 | tf_op jit(solution)/shard_map/ppermute | solution.py:23
  123.1 13.5 %collective-permute-start.6 = (bf16[256,768]{1,0:T(8,128)(2,1)}, bf16[256,768]{1,0:T(8,128)(2,1)S(1)}, u32[]{:S(2)}, u32[]{:S(2)}) collective-permute-start(bf16[256,768]{1,0:T(8,128)(2,1)} %get-tuple-element.208), channel_id=1, source_target_pairs={{0,1},{1,0},{2,3},{3,2},{4,5},{5,4},{6,7},{7,6},{8,9},{9,8},{10,11... | collective-permute-start | bytes 1179656 | tf_op jit(solution)/shard_map/ppermute | solution.py:23
  137.3 18.4 %collective-permute-start.8 = (bf16[512,768]{1,0:T(8,128)(2,1)S(1)}, bf16[512,768]{1,0:T(8,128)(2,1)}, u32[]{:S(2)}, u32[]{:S(2)}) collective-permute-start(bf16[512,768]{1,0:T(8,128)(2,1)S(1)} %bitcast.157), channel_id=1, source_target_pairs={{0,1},{1,0},{2,3},{3,2},{4,5},{5,4},{6,7},{7,6},{8,9},{9,8},{10,11... | collective-permute-start | bytes 2359304 | tf_op jit(solution)/shard_map/ppermute | solution.py:23
  162.0 18.2 %collective-permute-start.9 = (bf16[512,768]{1,0:T(8,128)(2,1)}, bf16[512,768]{1,0:T(8,128)(2,1)}, u32[]{:S(2)}, u32[]{:S(2)}) collective-permute-start(bf16[512,768]{1,0:T(8,128)(2,1)} %fusion.93), channel_id=1, source_target_pairs={{0,1},{1,0},{2,3},{3,2},{4,5},{5,4},{6,7},{7,6},{8,9},{9,8},{10,11... | collective-permute-start | bytes 2359304 | tf_op jit(solution)/shard_map/ppermute | solution.py:23
  182.9 31.2 %all-to-all-start.1 = ((bf16[8,64,768]{2,1,0:T(8,128)(2,1)}), bf16[8,64,768]{2,1,0:T(8,128)(2,1)S(1)}, u32[]{:S(2)}, u32[]{:S(2)}) async-start(bf16[8,64,768]{2,1,0:T(8,128)(2,1)} %bitcast.20), calls=%async_computation.1 | async-start | bytes 1572864 | tf_op jit(solution)/shard_map/all_to_all | solution.py:31
  188.3 6.9 %collective-permute-start.14 = (bf16[128,768]{1,0:T(8,128)(2,1)S(1)}, bf16[128,768]{1,0:T(8,128)(2,1)S(1)}, u32[]{:S(2)}, u32[]{:S(2)}) collective-permute-start(bf16[128,768]{1,0:T(8,128)(2,1)S(1)} %get-tuple-element.241), channel_id=1, source_target_pairs={{0,1},{1,0},{2,3},{3,2},{4,5},{5,4},{6,7},{7,6},{8,9},{9,8},{10,11... | collective-permute-start | bytes 589832 | tf_op jit(solution)/shard_map/ppermute | solution.py:23
  195.3 35.5 %copy-start.3 = (bf16[256,768]{1,0:T(8,128)(2,1)}, bf16[256,768]{1,0:T(8,128)(2,1)S(1)}, u32[]{:S(2)}) copy-start(bf16[256,768]{1,0:T(8,128)(2,1)S(1)} %maximum_select_fusion.13.refs_3_) | copy-start | bytes 1179652
  195.3 26.1 %collective-permute-start.10 = (bf16[512,768]{1,0:T(8,128)(2,1)S(1)}, bf16[512,768]{1,0:T(8,128)(2,1)S(1)}, u32[]{:S(2)}, u32[]{:S(2)}) collective-permute-start(bf16[512,768]{1,0:T(8,128)(2,1)S(1)} %bitcast.159), channel_id=1, source_target_pairs={{16,0},{17,1},{18,2},{19,3},{20,4},{21,5},{22,6},{23,7},{24,8},{25... | collective-permute-start | bytes 2359304 | tf_op jit(solution)/shard_map/ppermute | solution.py:27
  214.9 25.7 %all-to-all-start.2 = ((bf16[8,64,768]{2,1,0:T(8,128)(2,1)}), bf16[8,64,768]{2,1,0:T(8,128)(2,1)S(1)}, u32[]{:S(2)}, u32[]{:S(2)}) async-start(bf16[8,64,768]{2,1,0:T(8,128)(2,1)} %bitcast.28), calls=%async_computation.2 | async-start | bytes 1572864 | tf_op jit(solution)/shard_map/all_to_all | solution.py:31
  231.9 7.3 %collective-permute-start.13 = (bf16[128,768]{1,0:T(8,128)(2,1)S(1)}, bf16[128,768]{1,0:T(8,128)(2,1)S(1)}, u32[]{:S(2)}, u32[]{:S(2)}) collective-permute-start(bf16[128,768]{1,0:T(8,128)(2,1)S(1)} %get-tuple-element.255), channel_id=1, source_target_pairs={{0,1},{1,0},{2,3},{3,2},{4,5},{5,4},{6,7},{7,6},{8,9},{9,8},{10,11... | collective-permute-start | bytes 589832 | tf_op jit(solution)/shard_map/ppermute | solution.py:23
  240.6 25.8 %all-to-all-start.3 = ((bf16[8,64,768]{2,1,0:T(8,128)(2,1)}), bf16[8,64,768]{2,1,0:T(8,128)(2,1)}, u32[]{:S(2)}, u32[]{:S(2)}) async-start(bf16[8,64,768]{2,1,0:T(8,128)(2,1)} %bitcast.167), calls=%async_computation.3 | async-start | bytes 1572864 | tf_op jit(solution)/shard_map/all_to_all | solution.py:31
  245.4 20.1 %collective-permute-start.15 = (bf16[512,768]{1,0:T(8,128)(2,1)S(1)}, bf16[512,768]{1,0:T(8,128)(2,1)}, u32[]{:S(2)}, u32[]{:S(2)}) collective-permute-start(bf16[512,768]{1,0:T(8,128)(2,1)S(1)} %bitcast.163), channel_id=1, source_target_pairs={{0,1},{1,0},{2,3},{3,2},{4,5},{5,4},{6,7},{7,6},{8,9},{9,8},{10,11... | collective-permute-start | bytes 2359304 | tf_op jit(solution)/shard_map/ppermute | solution.py:23
  266.5 19.3 %collective-permute-start.16 = (bf16[512,768]{1,0:T(8,128)(2,1)}, bf16[512,768]{1,0:T(8,128)(2,1)S(1)}, u32[]{:S(2)}, u32[]{:S(2)}) collective-permute-start(bf16[512,768]{1,0:T(8,128)(2,1)} %bitcast.31.rows_ref), channel_id=1, source_target_pairs={{0,1},{1,0},{2,3},{3,2},{4,5},{5,4},{6,7},{7,6},{8,9},{9,8},{10,11... | collective-permute-start | bytes 2359304 | tf_op jit(solution)/shard_map/ppermute | solution.py:23
  297.6 18.6 %collective-permute-start.17 = (bf16[512,768]{1,0:T(8,128)(2,1)}, bf16[512,768]{1,0:T(8,128)(2,1)}, u32[]{:S(2)}, u32[]{:S(2)}) collective-permute-start(bf16[512,768]{1,0:T(8,128)(2,1)} %get-tuple-element.144), channel_id=1, source_target_pairs={{0,1},{1,0},{2,3},{3,2},{4,5},{5,4},{6,7},{7,6},{8,9},{9,8},{10,11... | collective-permute-start | bytes 2359304 | tf_op jit(solution)/shard_map/ppermute | solution.py:23
  299.1 21.2 %collective-permute-start.19 = (bf16[512,768]{1,0:T(8,128)(2,1)}, bf16[512,768]{1,0:T(8,128)(2,1)S(1)}, u32[]{:S(2)}, u32[]{:S(2)}) collective-permute-start(bf16[512,768]{1,0:T(8,128)(2,1)} %bitcast.31.rows_ref), channel_id=1, source_target_pairs={{0,16},{1,17},{2,18},{3,19},{4,20},{5,21},{6,22},{7,23},{8,24},{9,... | collective-permute-start | bytes 2359304 | tf_op jit(solution)/shard_map/ppermute | solution.py:27
  316.1 17.6 %collective-permute-start.18 = (bf16[512,768]{1,0:T(8,128)(2,1)}, bf16[512,768]{1,0:T(8,128)(2,1)}, u32[]{:S(2)}, u32[]{:S(2)}) collective-permute-start(bf16[512,768]{1,0:T(8,128)(2,1)} %fusion.98), channel_id=1, source_target_pairs={{0,1},{1,0},{2,3},{3,2},{4,5},{5,4},{6,7},{7,6},{8,9},{9,8},{10,11... | collective-permute-start | bytes 2359304 | tf_op jit(solution)/shard_map/ppermute | solution.py:23
  321.2 25.8 %all-to-all-start.4 = ((bf16[8,64,768]{2,1,0:T(8,128)(2,1)}), bf16[8,64,768]{2,1,0:T(8,128)(2,1)S(1)}, u32[]{:S(2)}, u32[]{:S(2)}) async-start(bf16[8,64,768]{2,1,0:T(8,128)(2,1)} %bitcast.33), calls=%async_computation.4 | async-start | bytes 1572864 | tf_op jit(solution)/shard_map/all_to_all | solution.py:31
  324.7 21.0 %collective-permute-start.23 = (bf16[512,768]{1,0:T(8,128)(2,1)}, bf16[512,768]{1,0:T(8,128)(2,1)}, u32[]{:S(2)}, u32[]{:S(2)}) collective-permute-start(bf16[512,768]{1,0:T(8,128)(2,1)} %copy-done.43), channel_id=1, source_target_pairs={{0,16},{1,17},{2,18},{3,19},{4,20},{5,21},{6,22},{7,23},{8,24},{9,... | collective-permute-start | bytes 2359304 | tf_op jit(solution)/shard_map/ppermute | solution.py:27
  329.8 13.2 %collective-permute-start.22 = (bf16[2,128,768]{2,1,0:T(8,128)(2,1)}, bf16[2,128,768]{2,1,0:T(8,128)(2,1)S(1)}, u32[]{:S(2)}, u32[]{:S(2)}) collective-permute-start(bf16[2,128,768]{2,1,0:T(8,128)(2,1)} %maximum_select_fusion.12), channel_id=1, source_target_pairs={{16,0},{17,1},{18,2},{19,3},{20,4},{21,5},{22,6},{23,7},{24,8},{25... | collective-permute-start | bytes 1179656 | tf_op jit(solution)/shard_map/ppermute | solution.py:27
  331.3 14.4 %collective-permute-start.21 = (bf16[256,384]{1,0:T(8,128)(2,1)}, bf16[256,384]{1,0:T(8,128)(2,1)}, u32[]{:S(2)}, u32[]{:S(2)}) collective-permute-start(bf16[256,384]{1,0:T(8,128)(2,1)} %get-tuple-element.152), channel_id=1, source_target_pairs={{0,1},{1,0},{2,3},{3,2},{4,5},{5,4},{6,7},{7,6},{8,9},{9,8},{10,11... | collective-permute-start | bytes 589832 | tf_op jit(solution)/shard_map/ppermute | solution.py:23
  331.9 15.1 %collective-permute-start.20 = (bf16[256,768]{1,0:T(8,128)(2,1)}, bf16[256,768]{1,0:T(8,128)(2,1)}, u32[]{:S(2)}, u32[]{:S(2)}) collective-permute-start(bf16[256,768]{1,0:T(8,128)(2,1)} %get-tuple-element.151), channel_id=1, source_target_pairs={{0,1},{1,0},{2,3},{3,2},{4,5},{5,4},{6,7},{7,6},{8,9},{9,8},{10,11... | collective-permute-start | bytes 1179656 | tf_op jit(solution)/shard_map/ppermute | solution.py:23
  362.9 24.7 %collective-permute-start.24 = (bf16[256,1152]{1,0:T(8,128)(2,1)}, bf16[256,1152]{1,0:T(8,128)(2,1)S(1)}, u32[]{:S(2)}, u32[]{:S(2)}) collective-permute-start(bf16[256,1152]{1,0:T(8,128)(2,1)} %get-tuple-element.163), channel_id=1, source_target_pairs={{0,1},{1,0},{2,3},{3,2},{4,5},{5,4},{6,7},{7,6},{8,9},{9,8},{10,11... | collective-permute-start | bytes 1769480 | tf_op jit(solution)/shard_map/ppermute | solution.py:23
  363.8 22.3 %collective-permute-start.25 = (bf16[256,768]{1,0:T(8,128)(2,1)S(1)}, bf16[256,768]{1,0:T(8,128)(2,1)S(1)}, u32[]{:S(2)}, u32[]{:S(2)}) collective-permute-start(bf16[256,768]{1,0:T(8,128)(2,1)S(1)} %copy-done.50), channel_id=1, source_target_pairs={{0,1},{1,0},{2,3},{3,2},{4,5},{5,4},{6,7},{7,6},{8,9},{9,8},{10,11... | collective-permute-start | bytes 1179656 | tf_op jit(solution)/shard_map/ppermute | solution.py:23
  365.0 30.0 %all-to-all-start.5 = ((bf16[8,64,768]{2,1,0:T(8,128)(2,1)}), bf16[8,64,768]{2,1,0:T(8,128)(2,1)}, u32[]{:S(2)}, u32[]{:S(2)}) async-start(bf16[8,64,768]{2,1,0:T(8,128)(2,1)} %bitcast.166), calls=%async_computation.5 | async-start | bytes 1572864 | tf_op jit(solution)/shard_map/all_to_all | solution.py:31
  392.8 26.4 %collective-permute-start.27 = (bf16[8,48,1536]{2,1,0:T(8,128)(2,1)S(1)}, bf16[8,48,1536]{2,1,0:T(8,128)(2,1)S(1)}, u32[]{:S(2)}, u32[]{:S(2)}) collective-permute-start(bf16[8,48,1536]{2,1,0:T(8,128)(2,1)S(1)} %fusion.105), channel_id=1, source_target_pairs={{0,16},{16,0},{1,17},{17,1},{2,18},{18,2},{3,19},{19,3},{4,20},{20... | collective-permute-start | bytes 3538952 | tf_op jit(solution)/shard_map/ppermute | solution.py:23
  395.0 25.6 %all-to-all-start.6 = ((bf16[8,64,768]{2,1,0:T(8,128)(2,1)}), bf16[8,64,768]{2,1,0:T(8,128)(2,1)S(1)}, u32[]{:S(2)}, u32[]{:S(2)}) async-start(bf16[8,64,768]{2,1,0:T(8,128)(2,1)} %bitcast.162), calls=%async_computation.6 | async-start | bytes 1572864 | tf_op jit(solution)/shard_map/all_to_all | solution.py:31
  401.3 25.0 %collective-permute-start.26 = (bf16[512,768]{1,0:T(8,128)(2,1)}, bf16[512,768]{1,0:T(8,128)(2,1)}, u32[]{:S(2)}, u32[]{:S(2)}) collective-permute-start(bf16[512,768]{1,0:T(8,128)(2,1)} %bitcast.36.dz_ref), channel_id=1, source_target_pairs={{0,1},{1,0},{2,3},{3,2},{4,5},{5,4},{6,7},{7,6},{8,9},{9,8},{10,11... | collective-permute-start | bytes 2359304 | tf_op jit(solution)/shard_map/ppermute | solution.py:23
  420.6 38.0 %all-to-all-start.7 = ((bf16[8,48,1536]{2,1,0:T(8,128)(2,1)}), bf16[8,48,1536]{2,1,0:T(8,128)(2,1)S(1)}, u32[]{:S(2)}, u32[]{:S(2)}) async-start(bf16[8,48,1536]{2,1,0:T(8,128)(2,1)} %add_convert_fusion), calls=%async_computation.7 | async-start | bytes 2359296 | tf_op jit(solution)/shard_map/all_to_all | solution.py:31
  425.0 101.2 %collective-permute-start.35 = (bf16[512,768]{1,0:T(8,128)(2,1)}, bf16[512,768]{1,0:T(8,128)(2,1)}, u32[]{:S(2)}, u32[]{:S(2)}) collective-permute-start(bf16[512,768]{1,0:T(8,128)(2,1)} %collective-permute-done.8.rows_ref), channel_id=1, source_target_pairs={{16,0},{17,1},{18,2},{19,3},{20,4},{21,5},{22,6},{23,7},{24,8},{25... | collective-permute-start | bytes 2359304 | tf_op jit(solution)/shard_map/ppermute | solution.py:27
  437.2 20.2 %collective-permute-start.28 = (bf16[512,768]{1,0:T(8,128)(2,1)}, bf16[512,768]{1,0:T(8,128)(2,1)S(1)}, u32[]{:S(2)}, u32[]{:S(2)}) collective-permute-start(bf16[512,768]{1,0:T(8,128)(2,1)} %get-tuple-element.169), channel_id=1, source_target_pairs={{0,1},{1,0},{2,3},{3,2},{4,5},{5,4},{6,7},{7,6},{8,9},{9,8},{10,11... | collective-permute-start | bytes 2359304 | tf_op jit(solution)/shard_map/ppermute | solution.py:23
  438.0 95.8 %collective-permute-start.39 = (bf16[512,768]{1,0:T(8,128)(2,1)}, bf16[512,768]{1,0:T(8,128)(2,1)}, u32[]{:S(2)}, u32[]{:S(2)}) collective-permute-start(bf16[512,768]{1,0:T(8,128)(2,1)} %get-tuple-element.217), channel_id=1, source_target_pairs={{0,16},{1,17},{2,18},{3,19},{4,20},{5,21},{6,22},{7,23},{8,24},{9,... | collective-permute-start | bytes 2359304 | tf_op jit(solution)/shard_map/ppermute | solution.py:27
  444.3 84.6 %collective-permute-start.37 = (bf16[512,768]{1,0:T(8,128)(2,1)}, bf16[512,768]{1,0:T(8,128)(2,1)}, u32[]{:S(2)}, u32[]{:S(2)}) collective-permute-start(bf16[512,768]{1,0:T(8,128)(2,1)} %get-tuple-element.215), channel_id=1, source_target_pairs={{0,16},{1,17},{2,18},{3,19},{4,20},{5,21},{6,22},{7,23},{8,24},{9,... | collective-permute-start | bytes 2359304 | tf_op jit(solution)/shard_map/ppermute | solution.py:27
  458.6 28.5 %all-to-all-start.8 = ((bf16[8,64,768]{2,1,0:T(8,128)(2,1)}), bf16[8,64,768]{2,1,0:T(8,128)(2,1)S(1)}, u32[]{:S(2)}, u32[]{:S(2)}) async-start(bf16[8,64,768]{2,1,0:T(8,128)(2,1)} %bitcast.146), calls=%async_computation.8 | async-start | bytes 1572864 | tf_op jit(solution)/shard_map/all_to_all | solution.py:31
  463.9 7.4 %collective-permute-start.29 = (bf16[128,768]{1,0:T(8,128)(2,1)S(1)}, bf16[128,768]{1,0:T(8,128)(2,1)S(1)}, u32[]{:S(2)}, u32[]{:S(2)}) collective-permute-start(bf16[128,768]{1,0:T(8,128)(2,1)S(1)} %get-tuple-element.252), channel_id=1, source_target_pairs={{0,1},{1,0},{2,3},{3,2},{4,5},{5,4},{6,7},{7,6},{8,9},{9,8},{10,11... | collective-permute-start | bytes 589832 | tf_op jit(solution)/shard_map/ppermute | solution.py:23
  472.7 14.3 %collective-permute-start.30 = (bf16[2,128,768]{2,1,0:T(8,128)(2,1)S(1)}, bf16[2,128,768]{2,1,0:T(8,128)(2,1)S(1)}, u32[]{:S(2)}, u32[]{:S(2)}) collective-permute-start(bf16[2,128,768]{2,1,0:T(8,128)(2,1)S(1)} %get-tuple-element.237), channel_id=1, source_target_pairs={{0,16},{1,17},{2,18},{3,19},{4,20},{5,21},{6,22},{7,23},{8,24},{9,... | collective-permute-start | bytes 1179656 | tf_op jit(solution)/shard_map/ppermute | solution.py:27
  491.1 15.1 %collective-permute-start.31 = (bf16[256,768]{1,0:T(8,128)(2,1)}, bf16[256,768]{1,0:T(8,128)(2,1)S(1)}, u32[]{:S(2)}, u32[]{:S(2)}) collective-permute-start(bf16[256,768]{1,0:T(8,128)(2,1)} %get-tuple-element.205.refs_1_), channel_id=1, source_target_pairs={{0,1},{1,0},{2,3},{3,2},{4,5},{5,4},{6,7},{7,6},{8,9},{9,8},{10,11... | collective-permute-start | bytes 1179656 | tf_op jit(solution)/shard_map/ppermute | solution.py:23
  503.0 14.8 %collective-permute-start.32 = (bf16[256,1152]{1,0:T(8,128)(2,1)}, bf16[256,1152]{1,0:T(8,128)(2,1)S(1)}, u32[]{:S(2)}, u32[]{:S(2)}) collective-permute-start(bf16[256,1152]{1,0:T(8,128)(2,1)} %get-tuple-element.209), channel_id=1, source_target_pairs={{0,1},{1,0},{2,3},{3,2},{4,5},{5,4},{6,7},{7,6},{8,9},{9,8},{10,11... | collective-permute-start | bytes 1769480 | tf_op jit(solution)/shard_map/ppermute | solution.py:23
  506.2 26.4 %collective-permute-start.36 = (bf16[512,768]{1,0:T(8,128)(2,1)}, bf16[512,768]{1,0:T(8,128)(2,1)}, u32[]{:S(2)}, u32[]{:S(2)}) collective-permute-start(bf16[512,768]{1,0:T(8,128)(2,1)} %get-tuple-element.214), channel_id=1, source_target_pairs={{16,0},{17,1},{18,2},{19,3},{20,4},{21,5},{22,6},{23,7},{24,8},{25... | collective-permute-start | bytes 2359304 | tf_op jit(solution)/shard_map/ppermute | solution.py:27
  510.9 42.7 %all-to-all-start.9 = ((f32[8,2,10,768]{3,1,2,0:T(2,128)}), f32[8,2,10,768]{3,1,2,0:T(2,128)S(1)}, u32[]{:S(2)}, u32[]{:S(2)}) async-start(f32[8,2,10,768]{3,1,2,0:T(2,128)} %broadcast_in_dim.27), calls=%async_computation.9 | async-start | bytes 983040 | tf_op jit(solution)/shard_map/all_to_all | solution.py:31
  517.7 28.0 %collective-permute-start.38 = (bf16[512,768]{1,0:T(8,128)(2,1)}, bf16[512,768]{1,0:T(8,128)(2,1)}, u32[]{:S(2)}, u32[]{:S(2)}) collective-permute-start(bf16[512,768]{1,0:T(8,128)(2,1)} %get-tuple-element.216), channel_id=1, source_target_pairs={{16,0},{17,1},{18,2},{19,3},{20,4},{21,5},{22,6},{23,7},{24,8},{25... | collective-permute-start | bytes 2359304 | tf_op jit(solution)/shard_map/ppermute | solution.py:27
  526.2 32.0 %collective-permute-start.34 = (bf16[128,768]{1,0:T(8,128)(2,1)}, bf16[128,768]{1,0:T(8,128)(2,1)}, u32[]{:S(2)}, u32[]{:S(2)}) collective-permute-start(bf16[128,768]{1,0:T(8,128)(2,1)} %get-tuple-element.250), channel_id=1, source_target_pairs={{0,1},{1,0},{2,3},{3,2},{4,5},{5,4},{6,7},{7,6},{8,9},{9,8},{10,11... | collective-permute-start | bytes 589832 | tf_op jit(solution)/shard_map/ppermute | solution.py:23
  528.9 25.5 %collective-permute-start.41 = (bf16[8,48,384]{2,1,0:T(8,128)(2,1)}, bf16[8,48,384]{2,1,0:T(8,128)(2,1)}, u32[]{:S(2)}, u32[]{:S(2)}) collective-permute-start(bf16[8,48,384]{2,1,0:T(8,128)(2,1)} %fusion.143), channel_id=1, source_target_pairs={{0,16},{16,0},{1,17},{17,1},{2,18},{18,2},{3,19},{19,3},{4,20},{20... | collective-permute-start | bytes 884744 | tf_op jit(solution)/shard_map/ppermute | solution.py:23
  532.5 38.6 %collective-permute-start.40 = (bf16[8,48,1152]{2,1,0:T(8,128)(2,1)}, bf16[8,48,1152]{2,1,0:T(8,128)(2,1)}, u32[]{:S(2)}, u32[]{:S(2)}) collective-permute-start(bf16[8,48,1152]{2,1,0:T(8,128)(2,1)} %fusion.117), channel_id=1, source_target_pairs={{0,16},{16,0},{1,17},{17,1},{2,18},{18,2},{3,19},{19,3},{4,20},{20... | collective-permute-start | bytes 2654216 | tf_op jit(solution)/shard_map/ppermute | solution.py:23
  533.8 24.4 %collective-permute-start.33 = (bf16[128,768]{1,0:T(8,128)(2,1)}, bf16[128,768]{1,0:T(8,128)(2,1)}, u32[]{:S(2)}, u32[]{:S(2)}) collective-permute-start(bf16[128,768]{1,0:T(8,128)(2,1)} %get-tuple-element.248), channel_id=1, source_target_pairs={{0,1},{1,0},{2,3},{3,2},{4,5},{5,4},{6,7},{7,6},{8,9},{9,8},{10,11... | collective-permute-start | bytes 589832 | tf_op jit(solution)/shard_map/ppermute | solution.py:23
  553.7 4.3 collective-permute-start.44
  558.1 11.7 %collective-permute-start.45 = (f32[10,768]{1,0:T(8,128)S(1)}, f32[10,768]{1,0:T(8,128)S(1)}, u32[]{:S(2)}, u32[]{:S(2)}) collective-permute-start(f32[10,768]{1,0:T(8,128)S(1)} %bitcast.178), channel_id=1, source_target_pairs={{0,16},{16,0},{1,17},{17,1},{2,18},{18,2},{3,19},{19,3},{4,20},{20... | collective-permute-start | bytes 92168 | tf_op jit(solution)/shard_map/ppermute | solution.py:23
  560.7 44.5 %collective-permute-start.43 = (bf16[2,128,768]{2,1,0:T(8,128)(2,1)}, bf16[2,128,768]{2,1,0:T(8,128)(2,1)}, u32[]{:S(2)}, u32[]{:S(2)}) collective-permute-start(bf16[2,128,768]{2,1,0:T(8,128)(2,1)} %get-tuple-element.234), channel_id=1, source_target_pairs={{0,16},{1,17},{2,18},{3,19},{4,20},{5,21},{6,22},{7,23},{8,24},{9,... | collective-permute-start | bytes 1179656 | tf_op jit(solution)/shard_map/ppermute | solution.py:27
  573.6 34.0 %all-to-all-start.10 = ((bf16[8,48,1536]{2,1,0:T(8,128)(2,1)}), bf16[8,48,1536]{2,1,0:T(8,128)(2,1)S(1)}, u32[]{:S(2)}, u32[]{:S(2)}) async-start(bf16[8,48,1536]{2,1,0:T(8,128)(2,1)} %pad_maximum_fusion.3), calls=%async_computation.10 | async-start | bytes 2359296 | tf_op jit(solution)/shard_map/all_to_all | solution.py:31
  593.1 13.4 %collective-permute-start.42 = (bf16[2,128,768]{2,1,0:T(8,128)(2,1)S(1)}, bf16[2,128,768]{2,1,0:T(8,128)(2,1)S(1)}, u32[]{:S(2)}, u32[]{:S(2)}) collective-permute-start(bf16[2,128,768]{2,1,0:T(8,128)(2,1)S(1)} %copy-done.28), channel_id=1, source_target_pairs={{16,0},{17,1},{18,2},{19,3},{20,4},{21,5},{22,6},{23,7},{24,8},{25... | collective-permute-start | bytes 1179656 | tf_op jit(solution)/shard_map/ppermute | solution.py:27
  608.0 6.6 %collective-permute-start.46 = (bf16[48,1536]{1,0:T(8,128)(2,1)S(1)}, bf16[48,1536]{1,0:T(8,128)(2,1)S(1)}, u32[]{:S(2)}, u32[]{:S(2)}) collective-permute-start(bf16[48,1536]{1,0:T(8,128)(2,1)S(1)} %select_convert_fusion), channel_id=1, source_target_pairs={{0,16},{16,0},{1,17},{17,1},{2,18},{18,2},{3,19},{19,3},{4,20},{20... | collective-permute-start | bytes 442376 | tf_op jit(solution)/shard_map/ppermute | solution.py:23
  (55 other events, 712.0 us)
Sparse Core Ops, SparseCore 0:
  28.4 53.9 all-gather.4
  83.9 61.4 all-gather.8
  147.0 57.9 all-gather.6
where the time goes:
time: 634 us; the launch traced here: 623 us
  waiting for transfers between devices  235 us (37%)
  starting transfers between devices  134 us (21%)
  Pallas kernels  91 us (14%)
  matrix products  79.1 us (12%)
  other arithmetic  43.2 us (7%)
  local copies, waits for them, and re-layouts  26.3 us (4%)
  between operations  15 us (2%)
    ppermute x33, waiting for transfers between devices, swap(): return lax.ppermute(values, axis, [(0, 1), (1, 0)])  176 us
    dot_general x17, matrix products, dot(): lax.dot_general(left, right, (((left_dim,), (right_dim,)), ((), ())), pre...  79.1 us
    all_to_all x11, starting transfers between devices, all_to_all(): return lax.all_to_all(values, 'dp', split_axis=0, concat_axis=0, tiled=True)  48.9 us
    pallas_call x6, Pallas kernels, staged_call(): pl.pallas_call(body, out_shape=outs, in_specs=[pl.BlockSpec(memory_space=...  47.5 us
    ppermute x33, starting transfers between devices, swap(): return lax.ppermute(values, axis, [(0, 1), (1, 0)])  43.7 us
    pallas_call x4, Pallas kernels, expert_back(): pl.pallas_call(functools.partial(expert_kernel, experts=experts), grid=(h...  43.5 us
    ppermute x14, starting transfers between devices, one_way(): return lax.ppermute(values, axis, [(source, target)])  41 us
    all_to_all x11, waiting for transfers between devices, all_to_all(): return lax.all_to_all(values, 'dp', split_axis=0, concat_axis=0, tiled=True)  26.8 us
  transfers between devices with their start and end apart: 61, of which 31 were waited for; matrix products, arithmetic and copies ran while one was open for 21% of the time, Pallas kernels for 10%

commit v1 on v0

--- a/solution.py
+++ b/solution.py
@@ -21,10 +21,6 @@
 
 def swap(values, axis):
     return lax.ppermute(values, axis, [(0, 1), (1, 0)])
-
-
-def one_way(values, axis, source, target):
-    return lax.ppermute(values, axis, [(source, target)])
 
 
 def all_to_all(values):
@@ -468,11 +464,6 @@
     return ordered(tensor, own[None], other[None])
 
 
-def by_section(pairs, fars, section):
-    own = jnp.where(section == 0, pairs[0], pairs[1])
-    return ordered(section, own, jnp.where(section == 0, fars[0], fars[1]))
-
-
 def gelu_pair(before, active_grad):
     activated, back = jax.vjp(smooth_gate, before)
     return (activated.astype(BF16), back(active_grad)[0].astype(BF16))
@@ -494,6 +485,9 @@
     def of_layer(layer, own, other):
         return jnp.where(section == layer, own, other)
 
+    def pick(first, second):
+        return jnp.where(section == 0, first, second)
+
     def by_layer(own):
         other = swap(own, "section")
         return [of_layer(layer, own, other) for layer in range(2)]
@@ -509,13 +503,14 @@
     own_route = entry(routes[0, :, :, 0], own_batch)
     other_route = swap(entry(routes[0, :, :, 0], 2 * (1 - section) + tensor), "section")
     route = [of_layer(layer, own_route, other_route) for layer in range(2)]
-    first_pack = of_layer(0, packed, one_way(packed, "section", 0, 1))
+    far_pack = swap(packed, "section")
+    first_pack = of_layer(0, packed, far_pack)
     first_beside = swap(first_pack, "tensor")
     first_packs = jnp.concatenate([first_pack, first_beside], axis=1)
     first_w = lax.all_gather(first_packs, "dp", axis=0, tiled=True)
     x_own = whole_group(x_in)
-    later_pack, d_last = after((packed, d_out), first_beside)
-    second_pack = of_layer(1, packed, one_way(later_pack, "section", 1, 0))
+    far_pack, d_last = after((far_pack, d_out), first_beside)
+    second_pack = of_layer(1, packed, far_pack)
     second_pack = jnp.concatenate([second_pack, swap(second_pack, "tensor")], axis=1)
     dz_last = whole_group(d_last)
     far_in = swap(w_in[0, 0], "section")
@@ -560,20 +555,18 @@
     second_w = lax.all_gather(after(second_pack, mine0), "dp", axis=0, tiled=True)
     back0 = all_to_all(fold(expert_forward(mine0, 0), expert_forward(peer0, 0)))
 
-    far_mine0 = one_way(after(mine0, peer0), "section", 1, 0)
-    far_peer0 = one_way(after(peer0, back0), "section", 1, 0)
     dz_out1 = dot(placing[1], dz_last, 1, 0).astype(BF16)
     mine_dz1 = all_to_all(after(dz_out1, back0))
     params1 = (gains[1], second_w, router_w[1], experts)
     *state1, outgoing1, out0 = layer_start(
-        {"taking": taking[0], "back": after(back0, far_mine0), "h_before": state0["h"],
+        {"taking": taking[0], "back": back0, "h_before": state0["h"],
          "gate_before": state0["gate"]},
         params1, segments, route_col[1], placing[1],
     )
     state1 = dict(zip(keys, state1))
     peer_dz1 = swap(mine_dz1, "tensor")
     pair_out0 = pair_up(out0, tensor)
-    mine1 = all_to_all(after(outgoing1, mine_dz1, pair_out0, far_peer0))
+    mine1 = all_to_all(after(outgoing1, mine_dz1, pair_out0))
     peer1 = swap(after(mine1, peer_dz1), "tensor")
 
     def both_back(layer, mine, peer, mine_dz, peer_dz):
@@ -584,12 +577,10 @@
 
     own_b1, peer_b1 = both_back(1, mine1, peer1, mine_dz1, peer_dz1)
     peer_dx1 = swap(peer_b1[0], "tensor")
-    far_mine1 = one_way(mine1, "section", 0, 1)
-    far_peer1 = one_way(after(peer1, own_b1[0]), "section", 0, 1)
-    far_out0 = one_way(pair_out0, "section", 1, 0)
-    far_peer0 = one_way(after(peer0, own_b1[0]), "section", 1, 0)
+    far_mine = swap(pick(mine1, mine0), "section")
+    far_peer = swap(pick(after(peer1, own_b1[0]), peer0), "section")
     dback1 = all_to_all(
-        after((own_b1[0] + peer_dx1.astype(F32)).astype(BF16), far_mine1)
+        after((own_b1[0] + peer_dx1.astype(F32)).astype(BF16), far_mine)
     )
     late_mine1, late_peer1 = after((mine1, peer1), peer_b1[0])
     peer_y1 = expert_forward(late_peer1, 1).astype(BF16)
@@ -601,7 +592,7 @@
         for half in after((state1["xn"], state1["o_far"]), peer_dx1)
     ]
     dattn1, dh1, gain_f1 = hidden_end(
-        after(dback1, own_y1, peer_y1, side_xn1, side_o1, far_out0, far_peer1), taking[1], dz_last, state1, params1
+        after(dback1, own_y1, peer_y1, side_xn1, side_o1, far_peer), taking[1], dz_last, state1, params1
     )
     side_dattn1 = swap(dattn1, "tensor")
     grad1, dqkv1, dqkv_far1, gain_a1, outgoing_dz0 = layer_end(
@@ -636,10 +627,7 @@
     reduced1 = all_to_all((keep1 + across1.astype(F32)).astype(BF16))
     peer_dx0 = swap(peer_b0[0], "tensor")
     pair_grad1 = pair_up(after(grad1, peer_dx0), tensor)
-    far_grad1 = one_way(pair_grad1, "section", 0, 1)
-
-    def pick(first, second, index=section):
-        return jnp.where(index == 0, first, second)
+
 
     def gather_rows(number, index):
         return stack((own_b0, own_b1)[number][index], (peer_b0, peer_b1)[number][index])
@@ -648,24 +636,21 @@
     near_rows = pick(stack(late_mine0, peer0), stack(late_mine1, peer1))
     near_dpre = pick(gather_rows(0, 2), gather_rows(1, 2))
     near_in = dot(near_rows, near_dpre, 0, 0)
-    far_dys1 = [
-        one_way(after(part_b1[3], peer_b0[0]), "section", 0, 1) for part_b1 in (own_b1, peer_b1)
-    ]
-    far_dys0 = [
-        one_way(after(part_b0[3], peer_b0[0]), "section", 1, 0) for part_b0 in (own_b0, peer_b0)
+    far_dys = [
+        swap(pick(*after((part_b1[3], part_b0[3]), peer_b0[0])), "section")
+        for part_b1, part_b0 in ((own_b1, own_b0), (peer_b1, peer_b0))
     ]
     total_dx0 = after(
         (own_b0[0] + peer_dx0.astype(F32)).astype(BF16), near_in, reduced1
     )
     dback0 = all_to_all(total_dx0)
     dy0, dy1 = (gather_rows(0, 3), gather_rows(1, 3))
-    late = after(section, total_dx0)
     near_dy = pick(dy0, dy1)
     late_back1 = after(back1, total_dx0)
     out1 = (state1["h"] + state1["gate"] * dot(taking[1], late_back1, 1, 0)).astype(BF16)
     pair_out1 = pair_up(out1, tensor)
-    far_out1 = one_way(pair_out1, "section", 0, 1)
-    near_act = pick(gather_rows(0, 1), gather_rows(1, 1), late)
+    far_outs = swap(pick(pair_out1, pair_out0), "section")
+    near_act = pick(*after((gather_rows(0, 1), gather_rows(1, 1)), total_dx0))
     near_out = dot(near_act, near_dy, 0, 0)
     dattn0, dh0, gain_f0 = hidden_end(
         after(dback0, near_out, pair_out1), taking[0], grad1, state0, params0
@@ -695,9 +680,8 @@
     qkv_keep, qkv_send = across_parts(
         attention_grad(ready_xn0, side_xn0, dqkv0, side_dqkv0), section
     )
-    late = after(section, qkv_send)
-    far_rows = stack(pick(far_mine0, far_mine1, late), pick(far_peer0, far_peer1, late))
-    far_dy = stack(pick(far_dys0[0], far_dys1[0], late), pick(far_dys0[1], far_dys1[1], late))
+    far_rows = stack(*after((far_mine, far_peer), qkv_send))
+    far_dy = stack(*after(tuple(far_dys), qkv_send))
     far_before = dot(far_rows, w_in[0, 0], 1, 0)
     half0 = jnp.concatenate(
         [
@@ -708,7 +692,7 @@
     )
     reduced0 = all_to_all(half0)
     pair_grad0 = pair_up(after(grad0, qkv_send), tensor)
-    far_grad0 = one_way(after(pair_grad0, half0), "section", 1, 0)
+    far_grads = swap(pick(pair_grad1, after(pair_grad0, half0)), "section")
     far_dy, reduced1 = after((far_dy, reduced1), half0)
     far_act, far_dpre = gelu_pair(far_before, dot(far_dy, w_exp_out[0, 0], 1, 1))
     in_w_grad = near_in + dot(far_rows, far_dpre, 0, 0)
@@ -719,15 +703,15 @@
     own_small = pick(smalls[0], smalls[1]) + swap(pick(smalls[1], smalls[0]), "section")
 
     reduced1 = reduced1.astype(F32).sum(axis=0)
-    reduced0 = after(reduced0, in_w_grad, expert_w_grad, far_grad0, far_out1, own_small)
+    reduced0 = after(reduced0, in_w_grad, expert_w_grad, far_grads, far_outs, own_small)
     reduced0 = reduced0.astype(F32).sum(axis=0)
     own_half = pick(reduced0, reduced1)
     other_half = swap(pick(reduced1, reduced0).astype(BF16), "section").astype(F32)
     joined = ordered(section, own_half, other_half)
     qkv_grad = jnp.stack([joined[:, part * kind:part * (kind + 1)] for kind in range(3)])
     out_grad = joined[:, 3 * part:].T
-    section_out = by_section([pair_out0, pair_out1], [far_out0, far_out1], section)
-    section_in_grad = by_section([pair_grad0, pair_grad1], [far_grad0, far_grad1], section)
+    section_out = ordered(section, pick(pair_out0, pair_out1), far_outs)
+    section_in_grad = ordered(section, pick(pair_grad0, pair_grad1), far_grads)
     return (
         section_out[None],
         section_in_grad[None],

time: 634 us -> 603 us (0.951)
  starting transfers between devices: 134 us -> 109 us
  waiting for transfers between devices: 235 us -> 224 us
    ppermute x14 -> x0, starting transfers between devices: 41 us -> none  [one_way(): return lax.ppermute(values, axis, [(source, target)])]
    ppermute x14 -> x0, waiting for transfers between devices: 25 us -> none  [one_way(): return lax.ppermute(values, axis, [(source, target)])]
    all_to_all x11, starting transfers between devices: 48.9 us -> 57.3 us  [all_to_all(): return lax.all_to_all(values, 'dp', split_axis=0, concat_axis=0, tiled=True)]
    ppermute x33 -> x40, starting transfers between devices: 43.7 us -> 52 us  [swap(): return lax.ppermute(values, axis, [(0, 1), (1, 0)])]
    ppermute x33 -> x40, waiting for transfers between devices: 176 us -> 183 us  [swap(): return lax.ppermute(values, axis, [(0, 1), (1, 0)])]
    unnamed x117 -> x151, local copies, waits for them, and re-layouts: 11 us -> 14.3 us
  transfers between devices with their start and end apart: 61 -> 54, of which waited for: 31 -> 27; matrix products, arithmetic and copies ran while one was open for 21% -> 23% of each run, Pallas kernels for 10% -> 11%
where the time goes in v1:
time: 603 us; the launch traced here: 593 us
  waiting for transfers between devices  224 us (37%)
  starting transfers between devices  109 us (18%)
  Pallas kernels  90.4 us (15%)
  matrix products  78.1 us (13%)
  other arithmetic  44.7 us (7%)
  local copies, waits for them, and re-layouts  32 us (5%)
  between operations  14.9 us (2%)
    ppermute x40, waiting for transfers between devices, swap(): return lax.ppermute(values, axis, [(0, 1), (1, 0)])  183 us
    dot_general x17, matrix products, dot(): lax.dot_general(left, right, (((left_dim,), (right_dim,)), ((), ())), pre...  78.1 us
    all_to_all x11, starting transfers between devices, all_to_all(): return lax.all_to_all(values, 'dp', split_axis=0, concat_axis=0, tiled=True)  57.3 us
    ppermute x40, starting transfers between devices, swap(): return lax.ppermute(values, axis, [(0, 1), (1, 0)])  52 us
    pallas_call x6, Pallas kernels, staged_call(): pl.pallas_call(body, out_shape=outs, in_specs=[pl.BlockSpec(memory_space=...  46.9 us
    pallas_call x4, Pallas kernels, expert_back(): pl.pallas_call(functools.partial(expert_kernel, experts=experts), grid=(h...  43.5 us
    all_to_all x11, waiting for transfers between devices, all_to_all(): return lax.all_to_all(values, 'dp', split_axis=0, concat_axis=0, tiled=True)  32.2 us
    unnamed x151, local copies, waits for them, and re-layouts  14.3 us
  transfers between devices with their start and end apart: 54, of which 27 were waited for; matrix products, arithmetic and copies ran while one was open for 23% of the time, Pallas kernels for 11%

profile of v1, /device:TPU:0, one launch (start us, length us, event | category | flops | bytes accessed | tf_op | source)
XLA Modules:
  0.0 593.1 jit_solution(4289345063743348110)
XLA Ops:
  8.3 3.0 collective-permute-start.4
  11.3 7.0 %collective-permute-done.4 = bf16[96,1536]{1,0:T(8,128)(2,1)S(1)} collective-permute-done((bf16[96,1536]{1,0:T(8,128)(2,1)S(1)}, bf16[96,1536]{1,0:T(8,128)(2,1)S(1)}, u32[]{:S(2)}, u32[]{:S(2)}) %collective-permute-start.4) | collective-permute-done | bytes 294944 | tf_op jit(solution)/shard_map/ppermute | solution.py:23
  20.2 6.4 %collective-permute-done.5 = bf16[96,1536]{1,0:T(8,128)(2,1)S(1)} collective-permute-done((bf16[96,1536]{1,0:T(8,128)(2,1)S(1)}, bf16[96,1536]{1,0:T(8,128)(2,1)S(1)}, u32[]{:S(2)}, u32[]{:S(2)}) %collective-permute-start.5) | collective-permute-done | bytes 294944 | tf_op jit(solution)/shard_map/ppermute | solution.py:23
  35.6 44.6 %collective-permute-done = s32[256]{0:T(256)S(1)} collective-permute-done((s32[256]{0:T(256)S(1)}, s32[256]{0:T(256)S(1)}, u32[]{:S(2)}, u32[]{:S(2)}) %collective-permute-start) | collective-permute-done | bytes 1056 | tf_op jit(solution)/shard_map/ppermute | solution.py:23
  84.2 8.6 %shard_map.178 = (bf16[256,768]{1,0:T(8,128)(2,1)}, bf16[256,2304]{1,0:T(8,128)(2,1)}, f32[256,128]{1,0:T(8,128)}, bf16[256,384]{1,0:T(8,128)(2,1)}, bf16[256,38...) custom-call(bf16[256,768]{1,0:T(8,128)(2,1)} %maximum_select_fusion.9.refs_0_.refs_7_, ...), custom_call_target="tpu_custom_call" | custom-call | flops 3000000000 | bytes 9250816 | tf_op jit(solution)/shard_map/pallas_call | solution.py:286
  92.8 4.4 all-to-all-start
  99.9 7.8 %collective-permute-done.10 = bf16[96,1536]{1,0:T(8,128)(2,1)S(1)} collective-permute-done((bf16[96,1536]{1,0:T(8,128)(2,1)S(1)}, bf16[96,1536]{1,0:T(8,128)(2,1)S(1)}, u32[]{:S(2)}, u32[]{:S(2)}) %collective-permute-start.10) | collective-permute-done | bytes 294944 | tf_op jit(solution)/shard_map/ppermute | solution.py:23
  108.6 9.6 %all-to-all-done = bf16[8,64,768]{2,1,0:T(8,128)(2,1)S(1)} async-done(((bf16[8,64,768]{2,1,0:T(8,128)(2,1)}), bf16[8,64,768]{2,1,0:T(8,128)(2,1)S(1)}, u32[]{:S(2)}, u32[]{:S(2)}) %all-to-all-start) | async-done | bytes 786464 | tf_op jit(solution)/shard_map/all_to_all | solution.py:27
  120.3 4.2 broadcast_select_fusion
  126.3 7.1 %collective-permute-done.6 = bf16[256,768]{1,0:T(8,128)(2,1)S(1)} collective-permute-done((bf16[256,768]{1,0:T(8,128)(2,1)}, bf16[256,768]{1,0:T(8,128)(2,1)S(1)}, u32[]{:S(2)}, u32[]{:S(2)}) %collective-permute-start.6) | collective-permute-done | bytes 393248 | tf_op jit(solution)/shard_map/ppermute | solution.py:23
  135.6 7.9 %all-gather.9.cloned.1.call-done = bf16[3072,768]{1,0:T(8,128)(2,1)} async-done(((bf16[1536,768]{1,0:T(8,128)(2,1)}), bf16[3072,768]{1,0:T(8,128)(2,1)}) %all-gather.9.cloned.1.call-update) | async-done | bytes 4718608 | tf_op jit(solution)/shard_map/all_gather | solution.py:518
  143.6 8.9 %collective-permute-done.8.rows_ref = bf16[512,768]{1,0:T(8,128)(2,1)} collective-permute-done((bf16[512,768]{1,0:T(8,128)(2,1)S(1)}, bf16[512,768]{1,0:T(8,128)(2,1)}, u32[]{:S(2)}, u32[]{:S(2)}) %collective-permute-start.8) | collective-permute-done | bytes 786464 | tf_op jit(solution)/shard_map/ppermute | solution.py:23
  152.5 6.7 %fusion.89 = bf16[512,768]{1,0:T(8,128)(2,1)} fusion(bf16[3072,768]{1,0:T(8,128)(2,1)} %all-gather.9.cloned.1.call-done, bf16[512,768]{1,0:T(8,128)(2,1)} %collective-permute-done.8.rows_ref, bf16[768,1536]{1,0:T(8,128)(2,1)} %get-tuple-element.238.in_ref), kind=kOutput, calls=%fused_computation.113 | convolution fusion | flops 2423390208 | bytes 6291456 | tf_op jit(solution)/shard_map/dot_general | solution.py:35
  160.8 5.7 fusion.57
  166.5 10.2 %collective-permute-done.9 = bf16[512,768]{1,0:T(8,128)(2,1)} collective-permute-done((bf16[512,768]{1,0:T(8,128)(2,1)}, bf16[512,768]{1,0:T(8,128)(2,1)}, u32[]{:S(2)}, u32[]{:S(2)}) %collective-permute-start.9) | collective-permute-done | bytes 786464 | tf_op jit(solution)/shard_map/ppermute | solution.py:23
  176.7 2.7 add_convert_fusion.5
  179.4 14.6 %all-to-all-start.1 = ((bf16[8,64,768]{2,1,0:T(8,128)(2,1)}), bf16[8,64,768]{2,1,0:T(8,128)(2,1)S(1)}, u32[]{:S(2)}, u32[]{:S(2)}) async-start(bf16[8,64,768]{2,1,0:T(8,128)(2,1)} %bitcast.20), calls=%async_computation.1 | async-start | bytes 1572864 | tf_op jit(solution)/shard_map/all_to_all | solution.py:27
  196.6 5.8 collective-permute-done.12
  203.7 11.1 %all-to-all-done.1 = bf16[8,64,768]{2,1,0:T(8,128)(2,1)S(1)} async-done(((bf16[8,64,768]{2,1,0:T(8,128)(2,1)}), bf16[8,64,768]{2,1,0:T(8,128)(2,1)S(1)}, u32[]{:S(2)}, u32[]{:S(2)}) %all-to-all-start.1) | async-done | bytes 786464 | tf_op jit(solution)/shard_map/all_to_all | solution.py:27
  214.8 3.5 all-to-all-start.2
  221.3 9.1 %shard_map.179 = (bf16[256,768]{1,0:T(8,128)(2,1)}, bf16[256,2304]{1,0:T(8,128)(2,1)}, f32[256,128]{1,0:T(8,128)}, bf16[256,384]{1,0:T(8,128)(2,1)}, bf16[256,38...) custom-call(bf16[256,512]{1,0:T(8,128)(2,1)} %fusion.130.refs_0_, ...), custom_call_target="tpu_custom_call" | custom-call | flops 3000000000 | bytes 11086848 | tf_op jit(solution)/shard_map/pallas_call | solution.py:286
  233.7 5.7 collective-permute-done.11
  240.0 4.7 all-to-all-start.3
  246.3 18.4 %collective-permute-done.13.dz_ref = bf16[512,768]{1,0:T(8,128)(2,1)S(1)} collective-permute-done((bf16[512,768]{1,0:T(8,128)(2,1)S(1)}, bf16[512,768]{1,0:T(8,128)(2,1)S(1)}, u32[]{:S(2)}, u32[]{:S(2)}) %collective-permute-start.13) | collective-permute-done | bytes 786464 | tf_op jit(solution)/shard_map/ppermute | solution.py:23
  267.9 10.9 %shard_map.180 = (f32[512,768]{1,0:T(8,128)}, bf16[512,1536]{1,0:T(8,128)(2,1)}, bf16[512,1536]{1,0:T(8,128)(2,1)}, bf16[512,768]{1,0:T(8,128)(2,1)}, f32[128,768]{1,0:T(8,128)}) custom-call(bf16[512,768]{1,0:T(8,128)(2,1)} %bitcast.150, bf16[512,768]{1,0:T(8,128)(2,1)} %bitcast.168, bf16[768,1536]{1,0:T(8,128)(2,1)} %get-tuple-element.237.in_ref, ...), custom_call_target="tpu_custom_call" | custom-call | flops 3623878656 | bytes 12000000 | tf_op jit(solution)/shard_map/pallas_call | solution.py:409
  278.8 6.0 %collective-permute-done.14.rows_ref = bf16[512,768]{1,0:T(8,128)(2,1)S(1)} collective-permute-done((bf16[512,768]{1,0:T(8,128)(2,1)S(1)}, bf16[512,768]{1,0:T(8,128)(2,1)S(1)}, u32[]{:S(2)}, u32[]{:S(2)}) %collective-permute-start.14) | collective-permute-done | bytes 786464 | tf_op jit(solution)/shard_map/ppermute | solution.py:23
  285.7 10.8 %shard_map.181 = (bf16[512,768]{1,0:T(8,128)(2,1)}, bf16[512,1536]{1,0:T(8,128)(2,1)}, bf16[512,1536]{1,0:T(8,128)(2,1)}, bf16[512,768]{1,0:T(8,128)(2,1)}, f32[128,768]{1,0:T(8,128)}) custom-call(bf16[512,768]{1,0:T(8,128)(2,1)} %copy-done.30, bf16[512,768]{1,0:T(8,128)(2,1)} %copy-done.58, bf16[768,1536]{1,0:T(8,128)(2,1)} %get-tuple-element.237.in_ref, ...), custom_call_target="tpu_custom_call" | custom-call | flops 3623878656 | bytes 12000000 | tf_op jit(solution)/shard_map/pallas_call | solution.py:409
  300.8 6.3 %fusion.94 = bf16[512,768]{1,0:T(8,128)(2,1)} fusion(bf16[3072,768]{1,0:T(8,128)(2,1)} %all-gather.9.cloned.1.call-done, bf16[512,768]{1,0:T(8,128)(2,1)} %copy-done.30, bf16[768,1536]{1,0:T(8,128)(2,1)} %get-tuple-element.237.in_ref), kind=kOutput, calls=%fused_computation.114 | convolution fusion | flops 2423390208 | bytes 6291456 | tf_op jit(solution)/shard_map/dot_general | solution.py:35
  307.0 8.1 %collective-permute-done.15 = bf16[512,768]{1,0:T(8,128)(2,1)} collective-permute-done((bf16[512,768]{1,0:T(8,128)(2,1)}, bf16[512,768]{1,0:T(8,128)(2,1)}, u32[]{:S(2)}, u32[]{:S(2)}) %collective-permute-start.15) | collective-permute-done | bytes 786464 | tf_op jit(solution)/shard_map/ppermute | solution.py:23
  316.7 2.2 add_convert_fusion.3
  319.8 4.4 all-to-all-start.4
  329.9 4.5 collective-permute-done.16
  334.4 6.3 %add_convert_fusion.4 = bf16[512,768]{1,0:T(8,128)(2,1)} fusion(bf16[512,768]{1,0:T(8,128)(2,1)} %collective-permute-done.16, bf16[3072,768]{1,0:T(8,128)(2,1)} %all-gather.9.cloned.1.call-done, bf16[512,768]{1,0:T(8,128)(2,1)S(1)} %bitcast.151, bf16[768,1536]{1,0:T(8,128)(2,1)} %get-tuple-element.237.in_ref), kind=kOutput, calls=%fused_computation.97 | convolution fusion | flops 2424176640 | bytes 7077888 | tf_op jit(solution)/shard_map/dot_general | solution.py:35
  340.7 4.8 collective-permute-done.20
  346.5 3.1 shard_map.182
  349.6 11.8 %shard_map.183 = (bf16[256,768]{1,0:T(8,128)(2,1)}, bf16[256,1152]{1,0:T(8,128)(2,1)}, bf16[256,1152]{1,0:T(8,128)(2,1)}, f32[1,768]{1,0:T(1,128)}, bf16[512,768]{1,0:T(8,128)(2,1)}) custom-call(f32[2,768]{1,0:T(2,128)} %slice_convert_fusion.refs_4_.refs_2_.refs_0_, bf16[256,768]{1,0:T(8,128)(2,1)} %get-tuple-element.154.refs_1_, ...), custom_call_target="tpu_custom_call" | custom-call | flops 5000000000 | bytes 10234880 | tf_op jit(solution)/shard_map/pallas_call | solution.py:286
  363.6 5.0 all-to-all-start.5
  368.6 16.7 %collective-permute-done.22 = bf16[256,768]{1,0:T(8,128)(2,1)S(1)} collective-permute-done((bf16[256,768]{1,0:T(8,128)(2,1)S(1)}, bf16[256,768]{1,0:T(8,128)(2,1)S(1)}, u32[]{:S(2)}, u32[]{:S(2)}) %collective-permute-start.22) | collective-permute-done | bytes 393248 | tf_op jit(solution)/shard_map/ppermute | solution.py:23
  386.8 2.2 fusion.102
  389.7 2.2 copy-done.2
  393.6 4.2 all-to-all-start.6
  400.4 10.9 %shard_map.184 = (f32[512,768]{1,0:T(8,128)}, bf16[512,1536]{1,0:T(8,128)(2,1)}, bf16[512,1536]{1,0:T(8,128)(2,1)}, bf16[512,768]{1,0:T(8,128)(2,1)}, f32[128,768]{1,0:T(8,128)}) custom-call(bf16[512,768]{1,0:T(8,128)(2,1)} %bitcast.147, bf16[512,768]{1,0:T(8,128)(2,1)} %bitcast.36.dz_ref, bf16[768,1536]{1,0:T(8,128)(2,1)} %get-tuple-element.238.in_ref, ...), custom_call_target="tpu_custom_call" | custom-call | flops 3623878656 | bytes 12000000 | tf_op jit(solution)/shard_map/pallas_call | solution.py:409
  411.3 7.6 %collective-permute-done.24 = bf16[8,48,1536]{2,1,0:T(8,128)(2,1)S(1)} collective-permute-done((bf16[8,48,1536]{2,1,0:T(8,128)(2,1)S(1)}, bf16[8,48,1536]{2,1,0:T(8,128)(2,1)S(1)}, u32[]{:S(2)}, u32[]{:S(2)}) %collective-permute-start.24) | collective-permute-done | bytes 1179680 | tf_op jit(solution)/shard_map/ppermute | solution.py:23
  420.3 3.7 all-to-all-start.7
  424.0 10.8 %shard_map.185 = (bf16[512,768]{1,0:T(8,128)(2,1)}, bf16[512,1536]{1,0:T(8,128)(2,1)}, bf16[512,1536]{1,0:T(8,128)(2,1)}, bf16[512,768]{1,0:T(8,128)(2,1)}, f32[128,768]{1,0:T(8,128)}) custom-call(bf16[512,768]{1,0:T(8,128)(2,1)} %collective-permute-done.8.rows_ref, bf16[512,768]{1,0:T(8,128)(2,1)} %collective-permute-done.23.dz_ref, ...), custom_call_target="tpu_custom_call" | custom-call | flops 3623878656 | bytes 12000000 | tf_op jit(solution)/shard_map/pallas_call | solution.py:409
  442.4 1.9 pad_maximum_fusion.1
  449.3 6.2 %fusion.39 = f32[768,1536]{1,0:T(8,128)} fusion(bf16[512,1536]{1,0:T(8,128)(2,1)S(1)} %copy-done.73, bf16[512,1536]{1,0:T(8,128)(2,1)S(1)} %copy-done.72, bf16[512,1536]{1,0:T(8,128)(2,1)S(1)} %copy-done.71, bf16[512,1536]{1,0:T(8,128)(2,1)S(1)} %copy-done.70, pred[]{:T(512)S(6)} %eq.54, bf16[512,768]{1,0:T(8,128)(2,1)} %collective-permute-done.8.rows_ref, ...), kind=kOutput, calls=%fused_computation.50 | convolution fusion | flops 2437152768 | bytes 14155777 | tf_op jit(solution)/shard_map/dot_general | solution.py:35
  458.9 5.5 all-to-all-start.8
  466.0 7.0 %fusion.48 = f32[1536,768]{1,0:T(8,128)} fusion(bf16[1024,1536]{1,0:T(8,128)(2,1)} %pad_maximum_fusion.1, bf16[1024,1536]{1,0:T(8,128)(2,1)} %pad_maximum_fusion.2, pred[]{:T(512)S(6)} %eq.54, bf16[512,768]{1,0:T(8,128)(2,1)} %get-tuple-element.217, bf16[512,768]{1,0:T(8,128)(2,1)S(1)} %copy-done.33, bf16[512,768]{1,0:T(8,128)(2,1)S(1)} %copy-done.29, ...), kind=kOutput, calls=%fused_computation.61 | convolution fusion | flops 2424569856 | bytes 14155777 | tf_op jit(solution)/shard_map/dot_general | solution.py:35
  474.8 10.5 %all-to-all-done.8 = bf16[8,64,768]{2,1,0:T(8,128)(2,1)S(1)} async-done(((bf16[8,64,768]{2,1,0:T(8,128)(2,1)}), bf16[8,64,768]{2,1,0:T(8,128)(2,1)S(1)}, u32[]{:S(2)}, u32[]{:S(2)}) %all-to-all-start.8) | async-done | bytes 786464 | tf_op jit(solution)/shard_map/all_to_all | solution.py:27
  486.2 3.1 shard_map.186
  490.1 11.2 %shard_map.187 = (bf16[256,768]{1,0:T(8,128)(2,1)}, bf16[256,1152]{1,0:T(8,128)(2,1)}, bf16[256,1152]{1,0:T(8,128)(2,1)}, f32[1,768]{1,0:T(1,128)}) custom-call(f32[2,768]{1,0:T(2,128)} %slice_convert_fusion.1.refs_1_.refs_2_.refs_0_, bf16[256,768]{1,0:T(8,128)(2,1)} %get-tuple-element.205.refs_1_, s32[256,1]{1,0:T(8,128)} %copy.53.refs_2_.refs_5_, ...), custom_call_target="tpu_custom_call" | custom-call | flops 5000000000 | bytes 9186304 | tf_op jit(solution)/shard_map/pallas_call | solution.py:286
  509.3 3.7 all-to-all-start.9
  513.0 3.1 collective-permute-done.29
  516.1 2.3 fusion.106
  523.2 2.2 constant_dynamic-update-slice_fusion.3
  525.5 2.7 constant_dynamic-update-slice_fusion.2
  528.1 4.6 fusion.158
  535.0 2.3 collective-permute-done.37
  538.0 2.3 select_bitcast_fusion
  545.3 3.6 all-to-all-start.10
  548.9 16.1 %convolution_add_fusion.1 = f32[768,1536]{1,0:T(8,128)} fusion(f32[768,1536]{1,0:T(8,128)} %fusion.39, bf16[1024,768]{1,0:T(8,128)(2,1)} %copy-done.44, f32[1024,1536]{1,0:T(8,128)} %fusion.158, bf16[1024,768]{1,0:T(8,128)(2,1)} %constant_dynamic-update-slice_fusion.2, bf16[1,1,1536,768]{3,2,1,0:T(8,128)(2,1)} %param.21), kind=kOutput, calls=%fused_computation.16 | convolution fusion | flops 4864475136 | bytes 21233664 | tf_op jit(solution)/shard_map/dot_general | solution.py:35
  567.0 10.5 %convolution_add_fusion = f32[1536,768]{1,0:T(8,128)} fusion(f32[1536,768]{1,0:T(8,128)} %fusion.48, bf16[1024,768]{1,0:T(8,128)(2,1)} %constant_dynamic-update-slice_fusion.2, f32[1024,1536]{1,0:T(8,128)} %fusion.158), kind=kOutput, calls=%fused_computation.15 | convolution fusion | flops 2431254528 | bytes 17301504 | tf_op jit(solution)/shard_map/dot_general | solution.py:35
  580.3 4.5 collective-permute-done.39
  (311 shorter events, 114.6 us)
Async XLA Ops:
  7.2 27.3 %copy-start = (s32[4,1,4]{2,1,0:T(1,128)S(1)}, s32[4,1,4]{2,1,0:T(1,128)}, u32[]{:S(2)}) copy-start(s32[4,1,4]{2,1,0:T(1,128)} %param.13) | copy-start | bytes 196
  7.2 77.0 %all-gather.5.cloned.1.call-start = ((), (), s32[]{:S(2)}) async-start(), calls=%async_computation.11 | async-start | bytes 5308416 | tf_op jit(solution)/shard_map/all_gather | solution.py:510
  8.3 10.0 %collective-permute-start.4 = (bf16[96,1536]{1,0:T(8,128)(2,1)S(1)}, bf16[96,1536]{1,0:T(8,128)(2,1)S(1)}, u32[]{:S(2)}, u32[]{:S(2)}) collective-permute-start(bf16[96,1536]{1,0:T(8,128)(2,1)S(1)} %bitcast.157), channel_id=1, source_target_pairs={{0,16},{16,0},{1,17},{17,1},{2,18},{18,2},{3,19},{19,3},{4,20},{20... | collective-permute-start | bytes 884744 | tf_op jit(solution)/shard_map/ppermute | solution.py:23
  11.3 19.1 %copy-start.51 = (bf16[1,768]{1,0:T(2,128)(2,1)S(1)}, bf16[1,768]{1,0:T(2,128)(2,1)}, u32[]{:S(2)}) copy-start(bf16[1,768]{1,0:T(2,128)(2,1)} %param.18) | copy-start | bytes 4612
  18.3 8.3 %collective-permute-start.5 = (bf16[96,1536]{1,0:T(8,128)(2,1)S(1)}, bf16[96,1536]{1,0:T(8,128)(2,1)S(1)}, u32[]{:S(2)}, u32[]{:S(2)}) collective-permute-start(bf16[96,1536]{1,0:T(8,128)(2,1)S(1)} %broadcast_select_fusion.9), channel_id=1, source_target_pairs={{0,1},{1,0},{2,3},{3,2},{4,5},{5,4},{6,7},{7,6},{8,9},{9,8},{10,11... | collective-permute-start | bytes 884744 | tf_op jit(solution)/shard_map/ppermute | solution.py:23
  27.5 116.1 %all-gather.9.cloned.1.call-start = ((), (), s32[]{:S(2)}) async-start(), calls=%async_computation.13 | async-start | bytes 7077888 | tf_op jit(solution)/shard_map/all_gather | solution.py:518
  28.3 55.9 %collective-permute-start.2 = (bf16[768,1536]{1,0:T(8,128)(2,1)S(1)}, bf16[768,1536]{1,0:T(8,128)(2,1)}, u32[]{:S(2)}, u32[]{:S(2)}) collective-permute-start(bf16[768,1536]{1,0:T(8,128)(2,1)S(1)} %bitcast.160), channel_id=1, source_target_pairs={{0,16},{16,0},{1,17},{17,1},{2,18},{18,2},{3,19},{19,3},{4,20},{20... | collective-permute-start | bytes 7077896 | tf_op jit(solution)/shard_map/ppermute | solution.py:23
  29.8 50.5 %collective-permute-start = (s32[256]{0:T(256)S(1)}, s32[256]{0:T(256)S(1)}, u32[]{:S(2)}, u32[]{:S(2)}) collective-permute-start(s32[256]{0:T(256)S(1)} %bitcast.195), channel_id=1, source_target_pairs={{0,16},{16,0},{1,17},{17,1},{2,18},{18,2},{3,19},{19,3},{4,20},{20... | collective-permute-start | bytes 3080 | tf_op jit(solution)/shard_map/ppermute | solution.py:23
  30.4 51.6 %collective-permute-start.3 = (bf16[10,768]{1,0:T(8,128)(2,1)S(1)}, bf16[10,768]{1,0:T(8,128)(2,1)S(1)}, u32[]{:S(2)}, u32[]{:S(2)}) collective-permute-start(bf16[10,768]{1,0:T(8,128)(2,1)S(1)} %pad_maximum_fusion.7), channel_id=1, source_target_pairs={{0,16},{16,0},{1,17},{17,1},{2,18},{18,2},{3,19},{19,3},{4,20},{20... | collective-permute-start | bytes 46088 | tf_op jit(solution)/shard_map/ppermute | solution.py:23
  32.9 50.4 %collective-permute-start.1 = (bf16[128,768]{1,0:T(8,128)(2,1)S(1)}, bf16[128,768]{1,0:T(8,128)(2,1)S(1)}, u32[]{:S(2)}, u32[]{:S(2)}) collective-permute-start(bf16[128,768]{1,0:T(8,128)(2,1)S(1)} %get-tuple-element.242), channel_id=1, source_target_pairs={{0,1},{1,0},{2,3},{3,2},{4,5},{5,4},{6,7},{7,6},{8,9},{9,8},{10,11... | collective-permute-start | bytes 589832 | tf_op jit(solution)/shard_map/ppermute | solution.py:23
  34.8 49.4 %copy-start.56 = (s32[256]{0:T(256)}, s32[256]{0:T(256)S(1)}, u32[]{:S(2)}) copy-start(s32[256]{0:T(256)S(1)} %convert_reduce_fusion.2) | copy-start | bytes 3076
  92.8 25.4 %all-to-all-start = ((bf16[8,64,768]{2,1,0:T(8,128)(2,1)}), bf16[8,64,768]{2,1,0:T(8,128)(2,1)S(1)}, u32[]{:S(2)}, u32[]{:S(2)}) async-start(bf16[8,64,768]{2,1,0:T(8,128)(2,1)} %bitcast.172), calls=%async_computation | async-start | bytes 1572864 | tf_op jit(solution)/shard_map/all_to_all | solution.py:27
  97.2 124.1 %all-gather.7.cloned.1.call-start = ((), (), s32[]{:S(2)}) async-start(), calls=%async_computation.12 | async-start | bytes 5308416 | tf_op jit(solution)/shard_map/all_gather | solution.py:555
  98.3 9.4 %collective-permute-start.10 = (bf16[96,1536]{1,0:T(8,128)(2,1)S(1)}, bf16[96,1536]{1,0:T(8,128)(2,1)S(1)}, u32[]{:S(2)}, u32[]{:S(2)}) collective-permute-start(bf16[96,1536]{1,0:T(8,128)(2,1)S(1)} %broadcast_select_fusion.8), channel_id=1, source_target_pairs={{0,1},{1,0},{2,3},{3,2},{4,5},{5,4},{6,7},{7,6},{8,9},{9,8},{10,11... | collective-permute-start | bytes 884744 | tf_op jit(solution)/shard_map/ppermute | solution.py:23
  118.2 180.0 %copy-start.4 = (bf16[8,64,768]{2,1,0:T(8,128)(2,1)}, bf16[8,64,768]{2,1,0:T(8,128)(2,1)S(1)}, u32[]{:S(2)}) copy-start(bf16[8,64,768]{2,1,0:T(8,128)(2,1)S(1)} %all-to-all-done) | copy-start | bytes 2359300
  118.2 8.1 %collective-permute-start.7 = (bf16[256,384]{1,0:T(8,128)(2,1)}, bf16[256,384]{1,0:T(8,128)(2,1)S(1)}, u32[]{:S(2)}, u32[]{:S(2)}) collective-permute-start(bf16[256,384]{1,0:T(8,128)(2,1)} %get-tuple-element.126), channel_id=1, source_target_pairs={{0,1},{1,0},{2,3},{3,2},{4,5},{5,4},{6,7},{7,6},{8,9},{9,8},{10,11... | collective-permute-start | bytes 589832 | tf_op jit(solution)/shard_map/ppermute | solution.py:23
  119.8 13.6 %collective-permute-start.6 = (bf16[256,768]{1,0:T(8,128)(2,1)}, bf16[256,768]{1,0:T(8,128)(2,1)S(1)}, u32[]{:S(2)}, u32[]{:S(2)}) collective-permute-start(bf16[256,768]{1,0:T(8,128)(2,1)} %get-tuple-element.208), channel_id=1, source_target_pairs={{0,1},{1,0},{2,3},{3,2},{4,5},{5,4},{6,7},{7,6},{8,9},{9,8},{10,11... | collective-permute-start | bytes 1179656 | tf_op jit(solution)/shard_map/ppermute | solution.py:23
  134.1 26.7 %copy-start.14 = (bf16[768,1536]{1,0:T(8,128)(2,1)S(1)}, bf16[768,1536]{1,0:T(8,128)(2,1)}, u32[]{:S(2)}) copy-start(bf16[768,1536]{1,0:T(8,128)(2,1)} %get-tuple-element.238.in_ref) | copy-start | bytes 7077892
  134.1 18.4 %collective-permute-start.8 = (bf16[512,768]{1,0:T(8,128)(2,1)S(1)}, bf16[512,768]{1,0:T(8,128)(2,1)}, u32[]{:S(2)}, u32[]{:S(2)}) collective-permute-start(bf16[512,768]{1,0:T(8,128)(2,1)S(1)} %bitcast.145), channel_id=1, source_target_pairs={{0,1},{1,0},{2,3},{3,2},{4,5},{5,4},{6,7},{7,6},{8,9},{9,8},{10,11... | collective-permute-start | bytes 2359304 | tf_op jit(solution)/shard_map/ppermute | solution.py:23
  159.2 17.5 %collective-permute-start.9 = (bf16[512,768]{1,0:T(8,128)(2,1)}, bf16[512,768]{1,0:T(8,128)(2,1)}, u32[]{:S(2)}, u32[]{:S(2)}) collective-permute-start(bf16[512,768]{1,0:T(8,128)(2,1)} %fusion.89), channel_id=1, source_target_pairs={{0,1},{1,0},{2,3},{3,2},{4,5},{5,4},{6,7},{7,6},{8,9},{9,8},{10,11... | collective-permute-start | bytes 2359304 | tf_op jit(solution)/shard_map/ppermute | solution.py:23
  166.5 28.5 %copy-start.46 = (bf16[4,128,768]{2,1,0:T(8,128)(2,1)S(1)}, bf16[4,128,768]{2,1,0:T(8,128)(2,1)}, u32[]{:S(2)}) copy-start(bf16[4,128,768]{2,1,0:T(8,128)(2,1)} %param.12) | copy-start | bytes 2359300
  179.4 35.5 %all-to-all-start.1 = ((bf16[8,64,768]{2,1,0:T(8,128)(2,1)}), bf16[8,64,768]{2,1,0:T(8,128)(2,1)S(1)}, u32[]{:S(2)}, u32[]{:S(2)}) async-start(bf16[8,64,768]{2,1,0:T(8,128)(2,1)} %bitcast.20), calls=%async_computation.1 | async-start | bytes 1572864 | tf_op jit(solution)/shard_map/all_to_all | solution.py:27
  195.0 7.3 %collective-permute-start.12 = (bf16[128,768]{1,0:T(8,128)(2,1)S(1)}, bf16[128,768]{1,0:T(8,128)(2,1)S(1)}, u32[]{:S(2)}, u32[]{:S(2)}) collective-permute-start(bf16[128,768]{1,0:T(8,128)(2,1)S(1)} %get-tuple-element.240), channel_id=1, source_target_pairs={{0,1},{1,0},{2,3},{3,2},{4,5},{5,4},{6,7},{7,6},{8,9},{9,8},{10,11... | collective-permute-start | bytes 589832 | tf_op jit(solution)/shard_map/ppermute | solution.py:23
  202.4 27.9 %copy-start.3 = (bf16[256,768]{1,0:T(8,128)(2,1)}, bf16[256,768]{1,0:T(8,128)(2,1)S(1)}, u32[]{:S(2)}) copy-start(bf16[256,768]{1,0:T(8,128)(2,1)S(1)} %maximum_select_fusion.11.refs_3_) | copy-start | bytes 1179652
  214.8 24.5 %all-to-all-start.2 = ((bf16[8,64,768]{2,1,0:T(8,128)(2,1)}), bf16[8,64,768]{2,1,0:T(8,128)(2,1)S(1)}, u32[]{:S(2)}, u32[]{:S(2)}) async-start(bf16[8,64,768]{2,1,0:T(8,128)(2,1)} %bitcast.28), calls=%async_computation.2 | async-start | bytes 1572864 | tf_op jit(solution)/shard_map/all_to_all | solution.py:27
  232.1 7.2 %collective-permute-start.11 = (bf16[128,768]{1,0:T(8,128)(2,1)S(1)}, bf16[128,768]{1,0:T(8,128)(2,1)S(1)}, u32[]{:S(2)}, u32[]{:S(2)}) collective-permute-start(bf16[128,768]{1,0:T(8,128)(2,1)S(1)} %get-tuple-element.256), channel_id=1, source_target_pairs={{0,1},{1,0},{2,3},{3,2},{4,5},{5,4},{6,7},{7,6},{8,9},{9,8},{10,11... | collective-permute-start | bytes 589832 | tf_op jit(solution)/shard_map/ppermute | solution.py:23
  239.4 28.5 %copy-start.39 = (bf16[8,64,768]{2,1,0:T(8,128)(2,1)}, bf16[8,64,768]{2,1,0:T(8,128)(2,1)S(1)}, u32[]{:S(2)}) copy-start(bf16[8,64,768]{2,1,0:T(8,128)(2,1)S(1)} %all-to-all-done.2) | copy-start | bytes 2359300
  240.0 25.7 %all-to-all-start.3 = ((bf16[8,64,768]{2,1,0:T(8,128)(2,1)}), bf16[8,64,768]{2,1,0:T(8,128)(2,1)S(1)}, u32[]{:S(2)}, u32[]{:S(2)}) async-start(bf16[8,64,768]{2,1,0:T(8,128)(2,1)} %bitcast.171), calls=%async_computation.3 | async-start | bytes 1572864 | tf_op jit(solution)/shard_map/all_to_all | solution.py:27
  244.8 20.0 %collective-permute-start.13 = (bf16[512,768]{1,0:T(8,128)(2,1)S(1)}, bf16[512,768]{1,0:T(8,128)(2,1)S(1)}, u32[]{:S(2)}, u32[]{:S(2)}) collective-permute-start(bf16[512,768]{1,0:T(8,128)(2,1)S(1)} %bitcast.167), channel_id=1, source_target_pairs={{0,1},{1,0},{2,3},{3,2},{4,5},{5,4},{6,7},{7,6},{8,9},{9,8},{10,11... | collective-permute-start | bytes 2359304 | tf_op jit(solution)/shard_map/ppermute | solution.py:23
  265.7 19.1 %collective-permute-start.14 = (bf16[512,768]{1,0:T(8,128)(2,1)S(1)}, bf16[512,768]{1,0:T(8,128)(2,1)S(1)}, u32[]{:S(2)}, u32[]{:S(2)}) collective-permute-start(bf16[512,768]{1,0:T(8,128)(2,1)S(1)} %bitcast.149), channel_id=1, source_target_pairs={{0,1},{1,0},{2,3},{3,2},{4,5},{5,4},{6,7},{7,6},{8,9},{9,8},{10,11... | collective-permute-start | bytes 2359304 | tf_op jit(solution)/shard_map/ppermute | solution.py:23
  296.5 18.6 %collective-permute-start.15 = (bf16[512,768]{1,0:T(8,128)(2,1)}, bf16[512,768]{1,0:T(8,128)(2,1)}, u32[]{:S(2)}, u32[]{:S(2)}) collective-permute-start(bf16[512,768]{1,0:T(8,128)(2,1)} %get-tuple-element.143), channel_id=1, source_target_pairs={{0,1},{1,0},{2,3},{3,2},{4,5},{5,4},{6,7},{7,6},{8,9},{9,8},{10,11... | collective-permute-start | bytes 2359304 | tf_op jit(solution)/shard_map/ppermute | solution.py:23
  299.3 19.7 %collective-permute-start.17 = (bf16[512,768]{1,0:T(8,128)(2,1)}, bf16[512,768]{1,0:T(8,128)(2,1)S(1)}, u32[]{:S(2)}, u32[]{:S(2)}) collective-permute-start(bf16[512,768]{1,0:T(8,128)(2,1)} %broadcast_select_fusion.5), channel_id=1, source_target_pairs={{0,16},{16,0},{1,17},{17,1},{2,18},{18,2},{3,19},{19,3},{4,20},{20... | collective-permute-start | bytes 2359304 | tf_op jit(solution)/shard_map/ppermute | solution.py:23
  315.1 19.3 %collective-permute-start.16 = (bf16[512,768]{1,0:T(8,128)(2,1)}, bf16[512,768]{1,0:T(8,128)(2,1)}, u32[]{:S(2)}, u32[]{:S(2)}) collective-permute-start(bf16[512,768]{1,0:T(8,128)(2,1)} %fusion.94), channel_id=1, source_target_pairs={{0,1},{1,0},{2,3},{3,2},{4,5},{5,4},{6,7},{7,6},{8,9},{9,8},{10,11... | collective-permute-start | bytes 2359304 | tf_op jit(solution)/shard_map/ppermute | solution.py:23
  319.8 25.7 %all-to-all-start.4 = ((bf16[8,64,768]{2,1,0:T(8,128)(2,1)}), bf16[8,64,768]{2,1,0:T(8,128)(2,1)S(1)}, u32[]{:S(2)}, u32[]{:S(2)}) async-start(bf16[8,64,768]{2,1,0:T(8,128)(2,1)} %bitcast.33), calls=%async_computation.4 | async-start | bytes 1572864 | tf_op jit(solution)/shard_map/all_to_all | solution.py:27
  325.5 20.0 %collective-permute-start.20 = (bf16[512,768]{1,0:T(8,128)(2,1)S(1)}, bf16[512,768]{1,0:T(8,128)(2,1)S(1)}, u32[]{:S(2)}, u32[]{:S(2)}) collective-permute-start(bf16[512,768]{1,0:T(8,128)(2,1)S(1)} %broadcast_select_fusion.4), channel_id=1, source_target_pairs={{0,16},{16,0},{1,17},{17,1},{2,18},{18,2},{3,19},{19,3},{4,20},{20... | collective-permute-start | bytes 2359304 | tf_op jit(solution)/shard_map/ppermute | solution.py:23
  327.9 17.6 %collective-permute-start.19 = (bf16[256,384]{1,0:T(8,128)(2,1)}, bf16[256,384]{1,0:T(8,128)(2,1)}, u32[]{:S(2)}, u32[]{:S(2)}) collective-permute-start(bf16[256,384]{1,0:T(8,128)(2,1)} %get-tuple-element.151), channel_id=1, source_target_pairs={{0,1},{1,0},{2,3},{3,2},{4,5},{5,4},{6,7},{7,6},{8,9},{9,8},{10,11... | collective-permute-start | bytes 589832 | tf_op jit(solution)/shard_map/ppermute | solution.py:23
  328.4 17.1 %collective-permute-start.18 = (bf16[256,768]{1,0:T(8,128)(2,1)S(1)}, bf16[256,768]{1,0:T(8,128)(2,1)}, u32[]{:S(2)}, u32[]{:S(2)}) collective-permute-start(bf16[256,768]{1,0:T(8,128)(2,1)S(1)} %copy-done.62), channel_id=1, source_target_pairs={{0,1},{1,0},{2,3},{3,2},{4,5},{5,4},{6,7},{7,6},{8,9},{9,8},{10,11... | collective-permute-start | bytes 1179656 | tf_op jit(solution)/shard_map/ppermute | solution.py:23
  349.6 35.6 %copy-start.69 = (bf16[256,384]{1,0:T(8,128)(2,1)S(1)}, bf16[256,384]{1,0:T(8,128)(2,1)}, u32[]{:S(2)}) copy-start(bf16[256,384]{1,0:T(8,128)(2,1)} %get-tuple-element.163) | copy-start | bytes 589828
  361.5 25.3 %copy-start.67 = (bf16[256,1152]{1,0:T(8,128)(2,1)S(1)}, bf16[256,1152]{1,0:T(8,128)(2,1)}, u32[]{:S(2)}) copy-start(bf16[256,1152]{1,0:T(8,128)(2,1)} %get-tuple-element.161) | copy-start | bytes 1769476
  361.5 25.3 %collective-permute-start.21 = (bf16[256,1152]{1,0:T(8,128)(2,1)}, bf16[256,1152]{1,0:T(8,128)(2,1)S(1)}, u32[]{:S(2)}, u32[]{:S(2)}) collective-permute-start(bf16[256,1152]{1,0:T(8,128)(2,1)} %get-tuple-element.162), channel_id=1, source_target_pairs={{0,1},{1,0},{2,3},{3,2},{4,5},{5,4},{6,7},{7,6},{8,9},{9,8},{10,11... | collective-permute-start | bytes 1769480 | tf_op jit(solution)/shard_map/ppermute | solution.py:23
  362.9 22.4 %collective-permute-start.22 = (bf16[256,768]{1,0:T(8,128)(2,1)S(1)}, bf16[256,768]{1,0:T(8,128)(2,1)S(1)}, u32[]{:S(2)}, u32[]{:S(2)}) collective-permute-start(bf16[256,768]{1,0:T(8,128)(2,1)S(1)} %copy-done.64), channel_id=1, source_target_pairs={{0,1},{1,0},{2,3},{3,2},{4,5},{5,4},{6,7},{7,6},{8,9},{9,8},{10,11... | collective-permute-start | bytes 1179656 | tf_op jit(solution)/shard_map/ppermute | solution.py:23
  363.6 30.0 %all-to-all-start.5 = ((bf16[8,64,768]{2,1,0:T(8,128)(2,1)}), bf16[8,64,768]{2,1,0:T(8,128)(2,1)}, u32[]{:S(2)}, u32[]{:S(2)}) async-start(bf16[8,64,768]{2,1,0:T(8,128)(2,1)} %bitcast.170), calls=%async_computation.5 | async-start | bytes 1572864 | tf_op jit(solution)/shard_map/all_to_all | solution.py:27
  392.0 26.9 %collective-permute-start.24 = (bf16[8,48,1536]{2,1,0:T(8,128)(2,1)S(1)}, bf16[8,48,1536]{2,1,0:T(8,128)(2,1)S(1)}, u32[]{:S(2)}, u32[]{:S(2)}) collective-permute-start(bf16[8,48,1536]{2,1,0:T(8,128)(2,1)S(1)} %fusion.101), channel_id=1, source_target_pairs={{0,16},{16,0},{1,17},{17,1},{2,18},{18,2},{3,19},{19,3},{4,20},{20... | collective-permute-start | bytes 3538952 | tf_op jit(solution)/shard_map/ppermute | solution.py:23
  393.6 26.7 %all-to-all-start.6 = ((bf16[8,64,768]{2,1,0:T(8,128)(2,1)}), bf16[8,64,768]{2,1,0:T(8,128)(2,1)S(1)}, u32[]{:S(2)}, u32[]{:S(2)}) async-start(bf16[8,64,768]{2,1,0:T(8,128)(2,1)} %bitcast.166), calls=%async_computation.6 | async-start | bytes 1572864 | tf_op jit(solution)/shard_map/all_to_all | solution.py:27
  399.8 24.2 %collective-permute-start.23 = (bf16[512,768]{1,0:T(8,128)(2,1)}, bf16[512,768]{1,0:T(8,128)(2,1)}, u32[]{:S(2)}, u32[]{:S(2)}) collective-permute-start(bf16[512,768]{1,0:T(8,128)(2,1)} %bitcast.36.dz_ref), channel_id=1, source_target_pairs={{0,1},{1,0},{2,3},{3,2},{4,5},{5,4},{6,7},{7,6},{8,9},{9,8},{10,11... | collective-permute-start | bytes 2359304 | tf_op jit(solution)/shard_map/ppermute | solution.py:23
  420.3 38.6 %all-to-all-start.7 = ((bf16[8,48,1536]{2,1,0:T(8,128)(2,1)}), bf16[8,48,1536]{2,1,0:T(8,128)(2,1)S(1)}, u32[]{:S(2)}, u32[]{:S(2)}) async-start(bf16[8,48,1536]{2,1,0:T(8,128)(2,1)} %add_convert_fusion), calls=%async_computation.7 | async-start | bytes 2359296 | tf_op jit(solution)/shard_map/all_to_all | solution.py:27
  434.9 20.7 %collective-permute-start.25 = (bf16[512,768]{1,0:T(8,128)(2,1)}, bf16[512,768]{1,0:T(8,128)(2,1)S(1)}, u32[]{:S(2)}, u32[]{:S(2)}) collective-permute-start(bf16[512,768]{1,0:T(8,128)(2,1)} %get-tuple-element.168), channel_id=1, source_target_pairs={{0,1},{1,0},{2,3},{3,2},{4,5},{5,4},{6,7},{7,6},{8,9},{9,8},{10,11... | collective-permute-start | bytes 2359304 | tf_op jit(solution)/shard_map/ppermute | solution.py:23
  436.6 84.4 %collective-permute-start.32 = (bf16[512,768]{1,0:T(8,128)(2,1)}, bf16[512,768]{1,0:T(8,128)(2,1)}, u32[]{:S(2)}, u32[]{:S(2)}) collective-permute-start(bf16[512,768]{1,0:T(8,128)(2,1)} %broadcast_select_fusion.3), channel_id=1, source_target_pairs={{0,16},{16,0},{1,17},{17,1},{2,18},{18,2},{3,19},{19,3},{4,20},{20... | collective-permute-start | bytes 2359304 | tf_op jit(solution)/shard_map/ppermute | solution.py:23
  439.1 81.9 %collective-permute-start.33 = (bf16[512,768]{1,0:T(8,128)(2,1)}, bf16[512,768]{1,0:T(8,128)(2,1)}, u32[]{:S(2)}, u32[]{:S(2)}) collective-permute-start(bf16[512,768]{1,0:T(8,128)(2,1)} %broadcast_select_fusion.2), channel_id=1, source_target_pairs={{0,16},{16,0},{1,17},{17,1},{2,18},{18,2},{3,19},{19,3},{4,20},{20... | collective-permute-start | bytes 2359304 | tf_op jit(solution)/shard_map/ppermute | solution.py:23
  456.4 81.7 %collective-permute-start.31 = (bf16[128,768]{1,0:T(8,128)(2,1)}, bf16[128,768]{1,0:T(8,128)(2,1)}, u32[]{:S(2)}, u32[]{:S(2)}) collective-permute-start(bf16[128,768]{1,0:T(8,128)(2,1)} %get-tuple-element.249), channel_id=1, source_target_pairs={{0,1},{1,0},{2,3},{3,2},{4,5},{5,4},{6,7},{7,6},{8,9},{9,8},{10,11... | collective-permute-start | bytes 589832 | tf_op jit(solution)/shard_map/ppermute | solution.py:23
  458.9 26.5 %all-to-all-start.8 = ((bf16[8,64,768]{2,1,0:T(8,128)(2,1)}), bf16[8,64,768]{2,1,0:T(8,128)(2,1)S(1)}, u32[]{:S(2)}, u32[]{:S(2)}) async-start(bf16[8,64,768]{2,1,0:T(8,128)(2,1)} %bitcast.156), calls=%async_computation.8 | async-start | bytes 1572864 | tf_op jit(solution)/shard_map/all_to_all | solution.py:27
  464.9 8.1 %collective-permute-start.26 = (bf16[128,768]{1,0:T(8,128)(2,1)S(1)}, bf16[128,768]{1,0:T(8,128)(2,1)S(1)}, u32[]{:S(2)}, u32[]{:S(2)}) collective-permute-start(bf16[128,768]{1,0:T(8,128)(2,1)S(1)} %get-tuple-element.253), channel_id=1, source_target_pairs={{0,1},{1,0},{2,3},{3,2},{4,5},{5,4},{6,7},{7,6},{8,9},{9,8},{10,11... | collective-permute-start | bytes 589832 | tf_op jit(solution)/shard_map/ppermute | solution.py:23
  473.3 28.0 %collective-permute-start.27 = (bf16[2,128,768]{2,1,0:T(8,128)(2,1)S(1)}, bf16[2,128,768]{2,1,0:T(8,128)(2,1)S(1)}, u32[]{:S(2)}, u32[]{:S(2)}) collective-permute-start(bf16[2,128,768]{2,1,0:T(8,128)(2,1)S(1)} %broadcast_select_fusion.7), channel_id=1, source_target_pairs={{0,16},{16,0},{1,17},{17,1},{2,18},{18,2},{3,19},{19,3},{4,20},{20... | collective-permute-start | bytes 1179656 | tf_op jit(solution)/shard_map/ppermute | solution.py:23
  489.3 15.1 %collective-permute-start.28 = (bf16[256,768]{1,0:T(8,128)(2,1)}, bf16[256,768]{1,0:T(8,128)(2,1)S(1)}, u32[]{:S(2)}, u32[]{:S(2)}) collective-permute-start(bf16[256,768]{1,0:T(8,128)(2,1)} %get-tuple-element.205.refs_1_), channel_id=1, source_target_pairs={{0,1},{1,0},{2,3},{3,2},{4,5},{5,4},{6,7},{7,6},{8,9},{9,8},{10,11... | collective-permute-start | bytes 1179656 | tf_op jit(solution)/shard_map/ppermute | solution.py:23
  501.2 14.9 %collective-permute-start.29 = (bf16[256,1152]{1,0:T(8,128)(2,1)}, bf16[256,1152]{1,0:T(8,128)(2,1)S(1)}, u32[]{:S(2)}, u32[]{:S(2)}) collective-permute-start(bf16[256,1152]{1,0:T(8,128)(2,1)} %get-tuple-element.209), channel_id=1, source_target_pairs={{0,1},{1,0},{2,3},{3,2},{4,5},{5,4},{6,7},{7,6},{8,9},{9,8},{10,11... | collective-permute-start | bytes 1769480 | tf_op jit(solution)/shard_map/ppermute | solution.py:23
  506.8 26.9 %collective-permute-start.35 = (bf16[8,48,384]{2,1,0:T(8,128)(2,1)}, bf16[8,48,384]{2,1,0:T(8,128)(2,1)}, u32[]{:S(2)}, u32[]{:S(2)}) collective-permute-start(bf16[8,48,384]{2,1,0:T(8,128)(2,1)} %fusion.138), channel_id=1, source_target_pairs={{0,16},{16,0},{1,17},{17,1},{2,18},{18,2},{3,19},{19,3},{4,20},{20... | collective-permute-start | bytes 884744 | tf_op jit(solution)/shard_map/ppermute | solution.py:23
  509.3 23.5 %all-to-all-start.9 = ((f32[8,2,10,768]{3,1,2,0:T(2,128)}), f32[8,2,10,768]{3,1,2,0:T(2,128)S(1)}, u32[]{:S(2)}, u32[]{:S(2)}) async-start(f32[8,2,10,768]{3,1,2,0:T(2,128)} %broadcast_in_dim.27), calls=%async_computation.9 | async-start | bytes 983040 | tf_op jit(solution)/shard_map/all_to_all | solution.py:27
  519.5 23.3 %collective-permute-start.34 = (bf16[8,48,1152]{2,1,0:T(8,128)(2,1)}, bf16[8,48,1152]{2,1,0:T(8,128)(2,1)}, u32[]{:S(2)}, u32[]{:S(2)}) collective-permute-start(bf16[8,48,1152]{2,1,0:T(8,128)(2,1)} %fusion.112), channel_id=1, source_target_pairs={{0,16},{16,0},{1,17},{17,1},{2,18},{18,2},{3,19},{19,3},{4,20},{20... | collective-permute-start | bytes 2654216 | tf_op jit(solution)/shard_map/ppermute | solution.py:23
  521.8 16.3 %collective-permute-start.30 = (bf16[128,768]{1,0:T(8,128)(2,1)}, bf16[128,768]{1,0:T(8,128)(2,1)}, u32[]{:S(2)}, u32[]{:S(2)}) collective-permute-start(bf16[128,768]{1,0:T(8,128)(2,1)} %get-tuple-element.252), channel_id=1, source_target_pairs={{0,1},{1,0},{2,3},{3,2},{4,5},{5,4},{6,7},{7,6},{8,9},{9,8},{10,11... | collective-permute-start | bytes 589832 | tf_op jit(solution)/shard_map/ppermute | solution.py:23
  533.0 4.3 collective-permute-start.37
  537.4 4.2 collective-permute-start.38
  545.3 33.3 %all-to-all-start.10 = ((bf16[8,48,1536]{2,1,0:T(8,128)(2,1)}), bf16[8,48,1536]{2,1,0:T(8,128)(2,1)S(1)}, u32[]{:S(2)}, u32[]{:S(2)}) async-start(bf16[8,48,1536]{2,1,0:T(8,128)(2,1)} %pad_maximum_fusion.3), calls=%async_computation.10 | async-start | bytes 2359296 | tf_op jit(solution)/shard_map/all_to_all | solution.py:27
  566.1 11.5 %collective-permute-start.36 = (bf16[2,128,768]{2,1,0:T(8,128)(2,1)S(1)}, bf16[2,128,768]{2,1,0:T(8,128)(2,1)S(1)}, u32[]{:S(2)}, u32[]{:S(2)}) collective-permute-start(bf16[2,128,768]{2,1,0:T(8,128)(2,1)S(1)} %broadcast_select_fusion.6), channel_id=1, source_target_pairs={{0,16},{16,0},{1,17},{17,1},{2,18},{18,2},{3,19},{19,3},{4,20},{20... | collective-permute-start | bytes 1179656 | tf_op jit(solution)/shard_map/ppermute | solution.py:23
  579.0 5.8 collective-permute-start.39
  (64 other events, 491.6 us)
Sparse Core Ops, SparseCore 0:
  27.6 52.8 all-gather.4
  82.1 61.4 all-gather.8
  145.2 51.7 all-gather.6

commit v2 on v1

--- a/solution.py
+++ b/solution.py
@@ -553,10 +553,11 @@
         after(mine0, side_xn0, side_o0, in_w), "tensor"
     )
     second_w = lax.all_gather(after(second_pack, mine0), "dp", axis=0, tiled=True)
-    back0 = all_to_all(fold(expert_forward(mine0, 0), expert_forward(peer0, 0)))
-
     dz_out1 = dot(placing[1], dz_last, 1, 0).astype(BF16)
-    mine_dz1 = all_to_all(after(dz_out1, back0))
+    mine_dz1 = all_to_all(after(dz_out1, mine0))
+    total_y0 = fold(expert_forward(mine0, 0), expert_forward(peer0, 0))
+    back0 = all_to_all(after(total_y0, mine_dz1))
+
     params1 = (gains[1], second_w, router_w[1], experts)
     *state1, outgoing1, out0 = layer_start(
         {"taking": taking[0], "back": back0, "h_before": state0["h"],
@@ -566,8 +567,8 @@
     state1 = dict(zip(keys, state1))
     peer_dz1 = swap(mine_dz1, "tensor")
     pair_out0 = pair_up(out0, tensor)
-    mine1 = all_to_all(after(outgoing1, mine_dz1, pair_out0))
-    peer1 = swap(after(mine1, peer_dz1), "tensor")
+    mine1 = all_to_all(outgoing1)
+    peer1 = swap(after(mine1, peer_dz1, pair_out0), "tensor")
 
     def both_back(layer, mine, peer, mine_dz, peer_dz):
         args = (in_w[layer], both_out, layer, router_w[layer], hot_row, experts)

time: 603 us -> 603 us (level)
  waiting for transfers between devices: 224 us -> 240 us
  starting transfers between devices: 109 us -> 96.2 us
    all_to_all x11, waiting for transfers between devices: 32.2 us -> 51.2 us  [all_to_all(): return lax.all_to_all(values, 'dp', split_axis=0, concat_axis=0, tiled=True)]
    all_to_all x11, starting transfers between devices: 57.3 us -> 46.2 us  [all_to_all(): return lax.all_to_all(values, 'dp', split_axis=0, concat_axis=0, tiled=True)]
    all_gather x1, waiting for transfers between devices: 7.94 us -> 0.02 us  [shards(): lax.all_gather(after(w_exp_out[0, 0], first_packs), 'section', axis=0)]
  transfers between devices with their start and end apart: 54 -> 54, of which waited for: 27 -> 23; matrix products, arithmetic and copies ran while one was open for 23% -> 23% of each run, Pallas kernels for 11% -> 9%
where the time goes in v2:
time: 603 us; the launch traced here: 596 us
  waiting for transfers between devices  240 us (40%)
  starting transfers between devices  96.2 us (16%)
  Pallas kernels  90.6 us (15%)
  matrix products  76.9 us (13%)
  other arithmetic  45.2 us (7%)
  local copies, waits for them, and re-layouts  32.1 us (5%)
  between operations  14.9 us (2%)
    ppermute x40, waiting for transfers between devices, swap(): return lax.ppermute(values, axis, [(0, 1), (1, 0)])  188 us
    dot_general x17, matrix products, dot(): lax.dot_general(left, right, (((left_dim,), (right_dim,)), ((), ())), pre...  76.9 us
    all_to_all x11, waiting for transfers between devices, all_to_all(): return lax.all_to_all(values, 'dp', split_axis=0, concat_axis=0, tiled=True)  51.2 us
    ppermute x40, starting transfers between devices, swap(): return lax.ppermute(values, axis, [(0, 1), (1, 0)])  49.9 us
    pallas_call x6, Pallas kernels, staged_call(): pl.pallas_call(body, out_shape=outs, in_specs=[pl.BlockSpec(memory_space=...  47.1 us
    all_to_all x11, starting transfers between devices, all_to_all(): return lax.all_to_all(values, 'dp', split_axis=0, concat_axis=0, tiled=True)  46.2 us
    pallas_call x4, Pallas kernels, expert_back(): pl.pallas_call(functools.partial(expert_kernel, experts=experts), grid=(h...  43.5 us
    unnamed x151, local copies, waits for them, and re-layouts  14.4 us
  transfers between devices with their start and end apart: 54, of which 23 were waited for; matrix products, arithmetic and copies ran while one was open for 23% of the time, Pallas kernels for 9%

profile of v2, /device:TPU:0, one launch (start us, length us, event | category | flops | bytes accessed | tf_op | source)
XLA Modules:
  0.0 595.6 jit_solution(840618597942641934)
XLA Ops:
  8.3 3.0 collective-permute-start.4
  11.3 7.0 %collective-permute-done.4 = bf16[96,1536]{1,0:T(8,128)(2,1)S(1)} collective-permute-done((bf16[96,1536]{1,0:T(8,128)(2,1)S(1)}, bf16[96,1536]{1,0:T(8,128)(2,1)S(1)}, u32[]{:S(2)}, u32[]{:S(2)}) %collective-permute-start.4) | collective-permute-done | bytes 294944 | tf_op jit(solution)/shard_map/ppermute | solution.py:23
  20.2 6.4 %collective-permute-done.5 = bf16[96,1536]{1,0:T(8,128)(2,1)S(1)} collective-permute-done((bf16[96,1536]{1,0:T(8,128)(2,1)S(1)}, bf16[96,1536]{1,0:T(8,128)(2,1)S(1)}, u32[]{:S(2)}, u32[]{:S(2)}) %collective-permute-start.5) | collective-permute-done | bytes 294944 | tf_op jit(solution)/shard_map/ppermute | solution.py:23
  35.6 44.6 %collective-permute-done = s32[256]{0:T(256)S(1)} collective-permute-done((s32[256]{0:T(256)S(1)}, s32[256]{0:T(256)S(1)}, u32[]{:S(2)}, u32[]{:S(2)}) %collective-permute-start) | collective-permute-done | bytes 1056 | tf_op jit(solution)/shard_map/ppermute | solution.py:23
  84.8 8.8 %shard_map.178 = (bf16[256,768]{1,0:T(8,128)(2,1)}, bf16[256,2304]{1,0:T(8,128)(2,1)}, f32[256,128]{1,0:T(8,128)}, bf16[256,384]{1,0:T(8,128)(2,1)}, bf16[256,38...) custom-call(bf16[256,768]{1,0:T(8,128)(2,1)} %maximum_select_fusion.9.refs_0_.refs_7_, ...), custom_call_target="tpu_custom_call" | custom-call | flops 3000000000 | bytes 9250816 | tf_op jit(solution)/shard_map/pallas_call | solution.py:286
  93.6 4.3 all-to-all-start
  100.6 7.8 %collective-permute-done.11 = bf16[96,1536]{1,0:T(8,128)(2,1)S(1)} collective-permute-done((bf16[96,1536]{1,0:T(8,128)(2,1)S(1)}, bf16[96,1536]{1,0:T(8,128)(2,1)S(1)}, u32[]{:S(2)}, u32[]{:S(2)}) %collective-permute-start.11) | collective-permute-done | bytes 294944 | tf_op jit(solution)/shard_map/ppermute | solution.py:23
  109.3 9.6 %all-to-all-done = bf16[8,64,768]{2,1,0:T(8,128)(2,1)S(1)} async-done(((bf16[8,64,768]{2,1,0:T(8,128)(2,1)}), bf16[8,64,768]{2,1,0:T(8,128)(2,1)S(1)}, u32[]{:S(2)}, u32[]{:S(2)}) %all-to-all-start) | async-done | bytes 786464 | tf_op jit(solution)/shard_map/all_to_all | solution.py:27
  121.1 4.2 broadcast_select_fusion
  125.2 1.8 collective-permute-done.7
  127.1 7.1 %collective-permute-done.6 = bf16[256,768]{1,0:T(8,128)(2,1)S(1)} collective-permute-done((bf16[256,768]{1,0:T(8,128)(2,1)}, bf16[256,768]{1,0:T(8,128)(2,1)S(1)}, u32[]{:S(2)}, u32[]{:S(2)}) %collective-permute-start.6) | collective-permute-done | bytes 393248 | tf_op jit(solution)/shard_map/ppermute | solution.py:23
  136.5 20.1 %collective-permute-done.10 = bf16[128,768]{1,0:T(8,128)(2,1)S(1)} collective-permute-done((bf16[128,768]{1,0:T(8,128)(2,1)S(1)}, bf16[128,768]{1,0:T(8,128)(2,1)S(1)}, u32[]{:S(2)}, u32[]{:S(2)}) %collective-permute-start.10) | collective-permute-done | bytes 196640 | tf_op jit(solution)/shard_map/ppermute | solution.py:23
  158.0 4.4 all-to-all-start.1
  162.4 5.6 fusion.89
  169.6 5.6 fusion.57
  175.2 13.1 %collective-permute-done.9 = bf16[512,768]{1,0:T(8,128)(2,1)} collective-permute-done((bf16[512,768]{1,0:T(8,128)(2,1)}, bf16[512,768]{1,0:T(8,128)(2,1)}, u32[]{:S(2)}, u32[]{:S(2)}) %collective-permute-start.9) | collective-permute-done | bytes 786464 | tf_op jit(solution)/shard_map/ppermute | solution.py:23
  188.3 2.6 add_convert_fusion.5
  190.9 13.9 %all-to-all-done.1 = bf16[8,64,768]{2,1,0:T(8,128)(2,1)} async-done(((bf16[8,64,768]{2,1,0:T(8,128)(2,1)}), bf16[8,64,768]{2,1,0:T(8,128)(2,1)}, u32[]{:S(2)}, u32[]{:S(2)}) %all-to-all-start.1) | async-done | bytes 786464 | tf_op jit(solution)/shard_map/all_to_all | solution.py:27
  204.8 3.5 all-to-all-start.2
  212.0 17.2 %all-to-all-done.2 = bf16[8,64,768]{2,1,0:T(8,128)(2,1)S(1)} async-done(((bf16[8,64,768]{2,1,0:T(8,128)(2,1)}), bf16[8,64,768]{2,1,0:T(8,128)(2,1)S(1)}, u32[]{:S(2)}, u32[]{:S(2)}) %all-to-all-start.2) | async-done | bytes 786464 | tf_op jit(solution)/shard_map/all_to_all | solution.py:27
  230.1 9.1 %shard_map.179 = (bf16[256,768]{1,0:T(8,128)(2,1)}, bf16[256,2304]{1,0:T(8,128)(2,1)}, f32[256,128]{1,0:T(8,128)}, bf16[256,384]{1,0:T(8,128)(2,1)}, bf16[256,38...) custom-call(bf16[256,512]{1,0:T(8,128)(2,1)} %fusion.130.refs_0_, ...), custom_call_target="tpu_custom_call" | custom-call | flops 3000000000 | bytes 11086848 | tf_op jit(solution)/shard_map/pallas_call | solution.py:286
  239.2 3.8 all-to-all-start.3
  246.8 20.6 %collective-permute-done.12 = bf16[128,768]{1,0:T(8,128)(2,1)S(1)} collective-permute-done((bf16[128,768]{1,0:T(8,128)(2,1)S(1)}, bf16[128,768]{1,0:T(8,128)(2,1)S(1)}, u32[]{:S(2)}, u32[]{:S(2)}) %collective-permute-start.12) | collective-permute-done | bytes 196640 | tf_op jit(solution)/shard_map/ppermute | solution.py:23
  270.2 10.9 %shard_map.180 = (f32[512,768]{1,0:T(8,128)}, bf16[512,1536]{1,0:T(8,128)(2,1)}, bf16[512,1536]{1,0:T(8,128)(2,1)}, bf16[512,768]{1,0:T(8,128)(2,1)}, f32[128,768]{1,0:T(8,128)}) custom-call(bf16[512,768]{1,0:T(8,128)(2,1)} %bitcast.150, bf16[512,768]{1,0:T(8,128)(2,1)} %bitcast.23.dz_ref, bf16[768,1536]{1,0:T(8,128)(2,1)} %get-tuple-element.237.in_ref, ...), custom_call_target="tpu_custom_call" | custom-call | flops 3623878656 | bytes 12000000 | tf_op jit(solution)/shard_map/pallas_call | solution.py:409
  281.2 6.1 %collective-permute-done.14.rows_ref = bf16[512,768]{1,0:T(8,128)(2,1)S(1)} collective-permute-done((bf16[512,768]{1,0:T(8,128)(2,1)S(1)}, bf16[512,768]{1,0:T(8,128)(2,1)S(1)}, u32[]{:S(2)}, u32[]{:S(2)}) %collective-permute-start.14) | collective-permute-done | bytes 786464 | tf_op jit(solution)/shard_map/ppermute | solution.py:23
  288.1 10.8 %shard_map.181 = (bf16[512,768]{1,0:T(8,128)(2,1)}, bf16[512,1536]{1,0:T(8,128)(2,1)}, bf16[512,1536]{1,0:T(8,128)(2,1)}, bf16[512,768]{1,0:T(8,128)(2,1)}, f32[128,768]{1,0:T(8,128)}) custom-call(bf16[512,768]{1,0:T(8,128)(2,1)} %copy-done.30, bf16[512,768]{1,0:T(8,128)(2,1)} %copy-done.58, bf16[768,1536]{1,0:T(8,128)(2,1)} %get-tuple-element.237.in_ref, ...), custom_call_target="tpu_custom_call" | custom-call | flops 3623878656 | bytes 12000000 | tf_op jit(solution)/shard_map/pallas_call | solution.py:409
  303.1 6.3 %fusion.94 = bf16[512,768]{1,0:T(8,128)(2,1)} fusion(bf16[3072,768]{1,0:T(8,128)(2,1)} %all-gather.9.cloned.1.call-done, bf16[512,768]{1,0:T(8,128)(2,1)} %copy-done.30, bf16[768,1536]{1,0:T(8,128)(2,1)} %get-tuple-element.237.in_ref), kind=kOutput, calls=%fused_computation.114 | convolution fusion | flops 2423390208 | bytes 6291456 | tf_op jit(solution)/shard_map/dot_general | solution.py:35
  309.4 8.2 %collective-permute-done.15 = bf16[512,768]{1,0:T(8,128)(2,1)} collective-permute-done((bf16[512,768]{1,0:T(8,128)(2,1)}, bf16[512,768]{1,0:T(8,128)(2,1)}, u32[]{:S(2)}, u32[]{:S(2)}) %collective-permute-start.15) | collective-permute-done | bytes 786464 | tf_op jit(solution)/shard_map/ppermute | solution.py:23
  319.1 2.2 add_convert_fusion.3
  322.2 4.5 all-to-all-start.4
  332.4 4.4 collective-permute-done.16
  336.7 6.3 %add_convert_fusion.4 = bf16[512,768]{1,0:T(8,128)(2,1)} fusion(bf16[512,768]{1,0:T(8,128)(2,1)} %collective-permute-done.16, bf16[3072,768]{1,0:T(8,128)(2,1)} %all-gather.9.cloned.1.call-done, bf16[512,768]{1,0:T(8,128)(2,1)S(1)} %bitcast.151, bf16[768,1536]{1,0:T(8,128)(2,1)} %get-tuple-element.237.in_ref), kind=kOutput, calls=%fused_computation.97 | convolution fusion | flops 2424176640 | bytes 7077888 | tf_op jit(solution)/shard_map/dot_general | solution.py:35
  343.0 5.0 collective-permute-done.20
  349.0 3.1 shard_map.182
  352.1 11.8 %shard_map.183 = (bf16[256,768]{1,0:T(8,128)(2,1)}, bf16[256,1152]{1,0:T(8,128)(2,1)}, bf16[256,1152]{1,0:T(8,128)(2,1)}, f32[1,768]{1,0:T(1,128)}, bf16[512,768]{1,0:T(8,128)(2,1)}) custom-call(f32[2,768]{1,0:T(2,128)} %slice_convert_fusion.refs_4_.refs_2_.refs_0_, bf16[256,768]{1,0:T(8,128)(2,1)} %get-tuple-element.154.refs_1_, ...), custom_call_target="tpu_custom_call" | custom-call | flops 5000000000 | bytes 10234880 | tf_op jit(solution)/shard_map/pallas_call | solution.py:286
  366.1 5.0 all-to-all-start.5
  371.1 16.7 %collective-permute-done.22 = bf16[256,768]{1,0:T(8,128)(2,1)S(1)} collective-permute-done((bf16[256,768]{1,0:T(8,128)(2,1)S(1)}, bf16[256,768]{1,0:T(8,128)(2,1)S(1)}, u32[]{:S(2)}, u32[]{:S(2)}) %collective-permute-start.22) | collective-permute-done | bytes 393248 | tf_op jit(solution)/shard_map/ppermute | solution.py:23
  389.3 2.2 fusion.102
  392.2 2.2 copy-done.2
  396.1 4.2 all-to-all-start.6
  402.9 10.9 %shard_map.184 = (f32[512,768]{1,0:T(8,128)}, bf16[512,1536]{1,0:T(8,128)(2,1)}, bf16[512,1536]{1,0:T(8,128)(2,1)}, bf16[512,768]{1,0:T(8,128)(2,1)}, f32[128,768]{1,0:T(8,128)}) custom-call(bf16[512,768]{1,0:T(8,128)(2,1)} %bitcast.147, bf16[512,768]{1,0:T(8,128)(2,1)} %bitcast.36.dz_ref, bf16[768,1536]{1,0:T(8,128)(2,1)} %get-tuple-element.238.in_ref, ...), custom_call_target="tpu_custom_call" | custom-call | flops 3623878656 | bytes 12000000 | tf_op jit(solution)/shard_map/pallas_call | solution.py:409
  413.8 7.6 %collective-permute-done.24 = bf16[8,48,1536]{2,1,0:T(8,128)(2,1)S(1)} collective-permute-done((bf16[8,48,1536]{2,1,0:T(8,128)(2,1)S(1)}, bf16[8,48,1536]{2,1,0:T(8,128)(2,1)S(1)}, u32[]{:S(2)}, u32[]{:S(2)}) %collective-permute-start.24) | collective-permute-done | bytes 1179680 | tf_op jit(solution)/shard_map/ppermute | solution.py:23
  422.8 3.7 all-to-all-start.7
  426.5 10.8 %shard_map.185 = (bf16[512,768]{1,0:T(8,128)(2,1)}, bf16[512,1536]{1,0:T(8,128)(2,1)}, bf16[512,1536]{1,0:T(8,128)(2,1)}, bf16[512,768]{1,0:T(8,128)(2,1)}, f32[128,768]{1,0:T(8,128)}) custom-call(bf16[512,768]{1,0:T(8,128)(2,1)} %collective-permute-done.8.rows_ref, bf16[512,768]{1,0:T(8,128)(2,1)} %collective-permute-done.23.dz_ref, ...), custom_call_target="tpu_custom_call" | custom-call | flops 3623878656 | bytes 12000000 | tf_op jit(solution)/shard_map/pallas_call | solution.py:409
  444.9 1.9 pad_maximum_fusion.1
  448.0 1.8 pad_maximum_fusion.2
  451.9 6.2 %fusion.39 = f32[768,1536]{1,0:T(8,128)} fusion(bf16[512,1536]{1,0:T(8,128)(2,1)S(1)} %copy-done.73, bf16[512,1536]{1,0:T(8,128)(2,1)S(1)} %copy-done.72, bf16[512,1536]{1,0:T(8,128)(2,1)S(1)} %copy-done.71, bf16[512,1536]{1,0:T(8,128)(2,1)S(1)} %copy-done.70, pred[]{:T(512)S(6)} %eq.54, bf16[512,768]{1,0:T(8,128)(2,1)} %collective-permute-done.8.rows_ref, ...), kind=kOutput, calls=%fused_computation.50 | convolution fusion | flops 2437152768 | bytes 14155777 | tf_op jit(solution)/shard_map/dot_general | solution.py:35
  461.3 5.5 all-to-all-start.8
  468.5 7.0 %fusion.48 = f32[1536,768]{1,0:T(8,128)} fusion(bf16[1024,1536]{1,0:T(8,128)(2,1)} %pad_maximum_fusion.1, bf16[1024,1536]{1,0:T(8,128)(2,1)} %pad_maximum_fusion.2, pred[]{:T(512)S(6)} %eq.54, bf16[512,768]{1,0:T(8,128)(2,1)} %get-tuple-element.217, bf16[512,768]{1,0:T(8,128)(2,1)S(1)} %copy-done.33, bf16[512,768]{1,0:T(8,128)(2,1)S(1)} %copy-done.29, ...), kind=kOutput, calls=%fused_computation.61 | convolution fusion | flops 2424569856 | bytes 14155777 | tf_op jit(solution)/shard_map/dot_general | solution.py:35
  477.3 10.5 %all-to-all-done.8 = bf16[8,64,768]{2,1,0:T(8,128)(2,1)S(1)} async-done(((bf16[8,64,768]{2,1,0:T(8,128)(2,1)}), bf16[8,64,768]{2,1,0:T(8,128)(2,1)S(1)}, u32[]{:S(2)}, u32[]{:S(2)}) %all-to-all-start.8) | async-done | bytes 786464 | tf_op jit(solution)/shard_map/all_to_all | solution.py:27
  488.7 3.1 shard_map.186
  492.6 11.2 %shard_map.187 = (bf16[256,768]{1,0:T(8,128)(2,1)}, bf16[256,1152]{1,0:T(8,128)(2,1)}, bf16[256,1152]{1,0:T(8,128)(2,1)}, f32[1,768]{1,0:T(1,128)}) custom-call(f32[2,768]{1,0:T(2,128)} %slice_convert_fusion.1.refs_1_.refs_2_.refs_0_, bf16[256,768]{1,0:T(8,128)(2,1)} %get-tuple-element.205.refs_1_, s32[256,1]{1,0:T(8,128)} %copy.53.refs_2_.refs_5_, ...), custom_call_target="tpu_custom_call" | custom-call | flops 5000000000 | bytes 9186304 | tf_op jit(solution)/shard_map/pallas_call | solution.py:286
  511.8 3.7 all-to-all-start.9
  515.5 3.2 collective-permute-done.29
  518.7 2.3 fusion.106
  525.6 2.2 constant_dynamic-update-slice_fusion.3
  528.0 2.7 constant_dynamic-update-slice_fusion.2
  530.6 4.6 fusion.158
  537.5 2.3 collective-permute-done.37
  540.5 2.3 select_bitcast_fusion
  547.8 3.6 all-to-all-start.10
  551.4 16.1 %convolution_add_fusion.1 = f32[768,1536]{1,0:T(8,128)} fusion(f32[768,1536]{1,0:T(8,128)} %fusion.39, bf16[1024,768]{1,0:T(8,128)(2,1)} %copy-done.43, f32[1024,1536]{1,0:T(8,128)} %fusion.158, bf16[1024,768]{1,0:T(8,128)(2,1)} %constant_dynamic-update-slice_fusion.2, bf16[1,1,1536,768]{3,2,1,0:T(8,128)(2,1)} %param.21), kind=kOutput, calls=%fused_computation.16 | convolution fusion | flops 4864475136 | bytes 21233664 | tf_op jit(solution)/shard_map/dot_general | solution.py:35
  569.5 10.5 %convolution_add_fusion = f32[1536,768]{1,0:T(8,128)} fusion(f32[1536,768]{1,0:T(8,128)} %fusion.48, bf16[1024,768]{1,0:T(8,128)(2,1)} %constant_dynamic-update-slice_fusion.2, f32[1024,1536]{1,0:T(8,128)} %fusion.158), kind=kOutput, calls=%fused_computation.15 | convolution fusion | flops 2431254528 | bytes 17301504 | tf_op jit(solution)/shard_map/dot_general | solution.py:35
  582.7 4.6 collective-permute-done.39
  (311 shorter events, 108.4 us)
Async XLA Ops:
  7.2 27.3 %copy-start = (s32[4,1,4]{2,1,0:T(1,128)S(1)}, s32[4,1,4]{2,1,0:T(1,128)}, u32[]{:S(2)}) copy-start(s32[4,1,4]{2,1,0:T(1,128)} %param.13) | copy-start | bytes 196
  7.2 77.6 %all-gather.5.cloned.1.call-start = ((), (), s32[]{:S(2)}) async-start(), calls=%async_computation.11 | async-start | bytes 5308416 | tf_op jit(solution)/shard_map/all_gather | solution.py:510
  8.3 10.0 %collective-permute-start.4 = (bf16[96,1536]{1,0:T(8,128)(2,1)S(1)}, bf16[96,1536]{1,0:T(8,128)(2,1)S(1)}, u32[]{:S(2)}, u32[]{:S(2)}) collective-permute-start(bf16[96,1536]{1,0:T(8,128)(2,1)S(1)} %bitcast.157), channel_id=1, source_target_pairs={{0,16},{16,0},{1,17},{17,1},{2,18},{18,2},{3,19},{19,3},{4,20},{20... | collective-permute-start | bytes 884744 | tf_op jit(solution)/shard_map/ppermute | solution.py:23
  11.3 19.1 %copy-start.51 = (bf16[1,768]{1,0:T(2,128)(2,1)S(1)}, bf16[1,768]{1,0:T(2,128)(2,1)}, u32[]{:S(2)}) copy-start(bf16[1,768]{1,0:T(2,128)(2,1)} %param.18) | copy-start | bytes 4612
  18.3 8.3 %collective-permute-start.5 = (bf16[96,1536]{1,0:T(8,128)(2,1)S(1)}, bf16[96,1536]{1,0:T(8,128)(2,1)S(1)}, u32[]{:S(2)}, u32[]{:S(2)}) collective-permute-start(bf16[96,1536]{1,0:T(8,128)(2,1)S(1)} %broadcast_select_fusion.9), channel_id=1, source_target_pairs={{0,1},{1,0},{2,3},{3,2},{4,5},{5,4},{6,7},{7,6},{8,9},{9,8},{10,11... | collective-permute-start | bytes 884744 | tf_op jit(solution)/shard_map/ppermute | solution.py:23
  27.5 134.9 %all-gather.9.cloned.1.call-start = ((), (), s32[]{:S(2)}) async-start(), calls=%async_computation.13 | async-start | bytes 7077888 | tf_op jit(solution)/shard_map/all_gather | solution.py:518
  28.3 56.5 %collective-permute-start.2 = (bf16[768,1536]{1,0:T(8,128)(2,1)S(1)}, bf16[768,1536]{1,0:T(8,128)(2,1)}, u32[]{:S(2)}, u32[]{:S(2)}) collective-permute-start(bf16[768,1536]{1,0:T(8,128)(2,1)S(1)} %bitcast.160), channel_id=1, source_target_pairs={{0,16},{16,0},{1,17},{17,1},{2,18},{18,2},{3,19},{19,3},{4,20},{20... | collective-permute-start | bytes 7077896 | tf_op jit(solution)/shard_map/ppermute | solution.py:23
  29.8 50.5 %collective-permute-start = (s32[256]{0:T(256)S(1)}, s32[256]{0:T(256)S(1)}, u32[]{:S(2)}, u32[]{:S(2)}) collective-permute-start(s32[256]{0:T(256)S(1)} %bitcast.193), channel_id=1, source_target_pairs={{0,16},{16,0},{1,17},{17,1},{2,18},{18,2},{3,19},{19,3},{4,20},{20... | collective-permute-start | bytes 3080 | tf_op jit(solution)/shard_map/ppermute | solution.py:23
  30.4 51.6 %collective-permute-start.3 = (bf16[10,768]{1,0:T(8,128)(2,1)S(1)}, bf16[10,768]{1,0:T(8,128)(2,1)S(1)}, u32[]{:S(2)}, u32[]{:S(2)}) collective-permute-start(bf16[10,768]{1,0:T(8,128)(2,1)S(1)} %pad_maximum_fusion.7), channel_id=1, source_target_pairs={{0,16},{16,0},{1,17},{17,1},{2,18},{18,2},{3,19},{19,3},{4,20},{20... | collective-permute-start | bytes 46088 | tf_op jit(solution)/shard_map/ppermute | solution.py:23
  32.9 51.0 %collective-permute-start.1 = (bf16[128,768]{1,0:T(8,128)(2,1)S(1)}, bf16[128,768]{1,0:T(8,128)(2,1)S(1)}, u32[]{:S(2)}, u32[]{:S(2)}) collective-permute-start(bf16[128,768]{1,0:T(8,128)(2,1)S(1)} %get-tuple-element.242), channel_id=1, source_target_pairs={{0,1},{1,0},{2,3},{3,2},{4,5},{5,4},{6,7},{7,6},{8,9},{9,8},{10,11... | collective-permute-start | bytes 589832 | tf_op jit(solution)/shard_map/ppermute | solution.py:23
  34.8 50.0 %copy-start.56 = (s32[256]{0:T(256)}, s32[256]{0:T(256)S(1)}, u32[]{:S(2)}) copy-start(s32[256]{0:T(256)S(1)} %convert_reduce_fusion.2) | copy-start | bytes 3076
  93.6 25.3 %all-to-all-start = ((bf16[8,64,768]{2,1,0:T(8,128)(2,1)}), bf16[8,64,768]{2,1,0:T(8,128)(2,1)S(1)}, u32[]{:S(2)}, u32[]{:S(2)}) async-start(bf16[8,64,768]{2,1,0:T(8,128)(2,1)} %bitcast.170), calls=%async_computation | async-start | bytes 1572864 | tf_op jit(solution)/shard_map/all_to_all | solution.py:27
  98.0 131.3 %all-gather.7.cloned.1.call-start = ((), (), s32[]{:S(2)}) async-start(), calls=%async_computation.12 | async-start | bytes 5308416 | tf_op jit(solution)/shard_map/all_gather | solution.py:555
  99.0 9.4 %collective-permute-start.11 = (bf16[96,1536]{1,0:T(8,128)(2,1)S(1)}, bf16[96,1536]{1,0:T(8,128)(2,1)S(1)}, u32[]{:S(2)}, u32[]{:S(2)}) collective-permute-start(bf16[96,1536]{1,0:T(8,128)(2,1)S(1)} %broadcast_select_fusion.8), channel_id=1, source_target_pairs={{0,1},{1,0},{2,3},{3,2},{4,5},{5,4},{6,7},{7,6},{8,9},{9,8},{10,11... | collective-permute-start | bytes 884744 | tf_op jit(solution)/shard_map/ppermute | solution.py:23
  118.9 181.6 %copy-start.4 = (bf16[8,64,768]{2,1,0:T(8,128)(2,1)}, bf16[8,64,768]{2,1,0:T(8,128)(2,1)S(1)}, u32[]{:S(2)}) copy-start(bf16[8,64,768]{2,1,0:T(8,128)(2,1)S(1)} %all-to-all-done) | copy-start | bytes 2359300
  119.0 8.1 %collective-permute-start.7 = (bf16[256,384]{1,0:T(8,128)(2,1)}, bf16[256,384]{1,0:T(8,128)(2,1)S(1)}, u32[]{:S(2)}, u32[]{:S(2)}) collective-permute-start(bf16[256,384]{1,0:T(8,128)(2,1)} %get-tuple-element.126), channel_id=1, source_target_pairs={{0,1},{1,0},{2,3},{3,2},{4,5},{5,4},{6,7},{7,6},{8,9},{9,8},{10,11... | collective-permute-start | bytes 589832 | tf_op jit(solution)/shard_map/ppermute | solution.py:23
  120.6 13.6 %collective-permute-start.6 = (bf16[256,768]{1,0:T(8,128)(2,1)}, bf16[256,768]{1,0:T(8,128)(2,1)S(1)}, u32[]{:S(2)}, u32[]{:S(2)}) collective-permute-start(bf16[256,768]{1,0:T(8,128)(2,1)} %get-tuple-element.208), channel_id=1, source_target_pairs={{0,1},{1,0},{2,3},{3,2},{4,5},{5,4},{6,7},{7,6},{8,9},{9,8},{10,11... | collective-permute-start | bytes 1179656 | tf_op jit(solution)/shard_map/ppermute | solution.py:23
  125.2 37.2 %copy-start.14 = (bf16[768,1536]{1,0:T(8,128)(2,1)S(1)}, bf16[768,1536]{1,0:T(8,128)(2,1)}, u32[]{:S(2)}) copy-start(bf16[768,1536]{1,0:T(8,128)(2,1)} %get-tuple-element.238.in_ref) | copy-start | bytes 7077892
  134.1 22.6 %copy-start.60 = (bf16[256,768]{1,0:T(8,128)(2,1)}, bf16[256,768]{1,0:T(8,128)(2,1)S(1)}, u32[]{:S(2)}) copy-start(bf16[256,768]{1,0:T(8,128)(2,1)S(1)} %collective-permute-done.6) | copy-start | bytes 1179652
  134.1 28.3 %collective-permute-start.8 = (bf16[512,768]{1,0:T(8,128)(2,1)S(1)}, bf16[512,768]{1,0:T(8,128)(2,1)}, u32[]{:S(2)}, u32[]{:S(2)}) collective-permute-start(bf16[512,768]{1,0:T(8,128)(2,1)S(1)} %bitcast.145), channel_id=1, source_target_pairs={{0,1},{1,0},{2,3},{3,2},{4,5},{5,4},{6,7},{7,6},{8,9},{9,8},{10,11... | collective-permute-start | bytes 2359304 | tf_op jit(solution)/shard_map/ppermute | solution.py:23
  135.9 20.7 %collective-permute-start.10 = (bf16[128,768]{1,0:T(8,128)(2,1)S(1)}, bf16[128,768]{1,0:T(8,128)(2,1)S(1)}, u32[]{:S(2)}, u32[]{:S(2)}) collective-permute-start(bf16[128,768]{1,0:T(8,128)(2,1)S(1)} %get-tuple-element.240), channel_id=1, source_target_pairs={{0,1},{1,0},{2,3},{3,2},{4,5},{5,4},{6,7},{7,6},{8,9},{9,8},{10,11... | collective-permute-start | bytes 589832 | tf_op jit(solution)/shard_map/ppermute | solution.py:23
  158.0 46.8 %all-to-all-start.1 = ((bf16[8,64,768]{2,1,0:T(8,128)(2,1)}), bf16[8,64,768]{2,1,0:T(8,128)(2,1)}, u32[]{:S(2)}, u32[]{:S(2)}) async-start(bf16[8,64,768]{2,1,0:T(8,128)(2,1)} %bitcast.22), calls=%async_computation.1 | async-start | bytes 1572864 | tf_op jit(solution)/shard_map/all_to_all | solution.py:27
  168.0 20.3 %collective-permute-start.9 = (bf16[512,768]{1,0:T(8,128)(2,1)}, bf16[512,768]{1,0:T(8,128)(2,1)}, u32[]{:S(2)}, u32[]{:S(2)}) collective-permute-start(bf16[512,768]{1,0:T(8,128)(2,1)} %fusion.89), channel_id=1, source_target_pairs={{0,1},{1,0},{2,3},{3,2},{4,5},{5,4},{6,7},{7,6},{8,9},{9,8},{10,11... | collective-permute-start | bytes 2359304 | tf_op jit(solution)/shard_map/ppermute | solution.py:23
  175.2 35.5 %copy-start.49 = (bf16[10,768]{1,0:T(8,128)(2,1)S(1)}, bf16[10,768]{1,0:T(8,128)(2,1)}, u32[]{:S(2)}) copy-start(bf16[10,768]{1,0:T(8,128)(2,1)} %get-tuple-element.262) | copy-start | bytes 46084
  204.8 24.5 %all-to-all-start.2 = ((bf16[8,64,768]{2,1,0:T(8,128)(2,1)}), bf16[8,64,768]{2,1,0:T(8,128)(2,1)S(1)}, u32[]{:S(2)}, u32[]{:S(2)}) async-start(bf16[8,64,768]{2,1,0:T(8,128)(2,1)} %bitcast.24), calls=%async_computation.2 | async-start | bytes 1572864 | tf_op jit(solution)/shard_map/all_to_all | solution.py:27
  239.2 28.8 %all-to-all-start.3 = ((bf16[8,64,768]{2,1,0:T(8,128)(2,1)}), bf16[8,64,768]{2,1,0:T(8,128)(2,1)S(1)}, u32[]{:S(2)}, u32[]{:S(2)}) async-start(bf16[8,64,768]{2,1,0:T(8,128)(2,1)} %bitcast.168), calls=%async_computation.3 | async-start | bytes 1572864 | tf_op jit(solution)/shard_map/all_to_all | solution.py:27
  243.0 25.0 %collective-permute-start.13 = (bf16[512,768]{1,0:T(8,128)(2,1)}, bf16[512,768]{1,0:T(8,128)(2,1)S(1)}, u32[]{:S(2)}, u32[]{:S(2)}) collective-permute-start(bf16[512,768]{1,0:T(8,128)(2,1)} %bitcast.23.dz_ref), channel_id=1, source_target_pairs={{0,1},{1,0},{2,3},{3,2},{4,5},{5,4},{6,7},{7,6},{8,9},{9,8},{10,11... | collective-permute-start | bytes 2359304 | tf_op jit(solution)/shard_map/ppermute | solution.py:23
  246.3 21.1 %collective-permute-start.12 = (bf16[128,768]{1,0:T(8,128)(2,1)S(1)}, bf16[128,768]{1,0:T(8,128)(2,1)S(1)}, u32[]{:S(2)}, u32[]{:S(2)}) collective-permute-start(bf16[128,768]{1,0:T(8,128)(2,1)S(1)} %get-tuple-element.256), channel_id=1, source_target_pairs={{0,1},{1,0},{2,3},{3,2},{4,5},{5,4},{6,7},{7,6},{8,9},{9,8},{10,11... | collective-permute-start | bytes 589832 | tf_op jit(solution)/shard_map/ppermute | solution.py:23
  268.1 19.2 %copy-start.58 = (bf16[512,768]{1,0:T(8,128)(2,1)}, bf16[512,768]{1,0:T(8,128)(2,1)S(1)}, u32[]{:S(2)}) copy-start(bf16[512,768]{1,0:T(8,128)(2,1)S(1)} %collective-permute-done.13.dz_ref) | copy-start | bytes 2359300
  268.1 19.2 %collective-permute-start.14 = (bf16[512,768]{1,0:T(8,128)(2,1)S(1)}, bf16[512,768]{1,0:T(8,128)(2,1)S(1)}, u32[]{:S(2)}, u32[]{:S(2)}) collective-permute-start(bf16[512,768]{1,0:T(8,128)(2,1)S(1)} %bitcast.149), channel_id=1, source_target_pairs={{0,1},{1,0},{2,3},{3,2},{4,5},{5,4},{6,7},{7,6},{8,9},{9,8},{10,11... | collective-permute-start | bytes 2359304 | tf_op jit(solution)/shard_map/ppermute | solution.py:23
  299.0 18.6 %collective-permute-start.15 = (bf16[512,768]{1,0:T(8,128)(2,1)}, bf16[512,768]{1,0:T(8,128)(2,1)}, u32[]{:S(2)}, u32[]{:S(2)}) collective-permute-start(bf16[512,768]{1,0:T(8,128)(2,1)} %get-tuple-element.143), channel_id=1, source_target_pairs={{0,1},{1,0},{2,3},{3,2},{4,5},{5,4},{6,7},{7,6},{8,9},{9,8},{10,11... | collective-permute-start | bytes 2359304 | tf_op jit(solution)/shard_map/ppermute | solution.py:23
  301.6 19.7 %collective-permute-start.17 = (bf16[512,768]{1,0:T(8,128)(2,1)}, bf16[512,768]{1,0:T(8,128)(2,1)S(1)}, u32[]{:S(2)}, u32[]{:S(2)}) collective-permute-start(bf16[512,768]{1,0:T(8,128)(2,1)} %broadcast_select_fusion.5), channel_id=1, source_target_pairs={{0,16},{16,0},{1,17},{17,1},{2,18},{18,2},{3,19},{19,3},{4,20},{20... | collective-permute-start | bytes 2359304 | tf_op jit(solution)/shard_map/ppermute | solution.py:23
  317.5 19.2 %collective-permute-start.16 = (bf16[512,768]{1,0:T(8,128)(2,1)}, bf16[512,768]{1,0:T(8,128)(2,1)}, u32[]{:S(2)}, u32[]{:S(2)}) collective-permute-start(bf16[512,768]{1,0:T(8,128)(2,1)} %fusion.94), channel_id=1, source_target_pairs={{0,1},{1,0},{2,3},{3,2},{4,5},{5,4},{6,7},{7,6},{8,9},{9,8},{10,11... | collective-permute-start | bytes 2359304 | tf_op jit(solution)/shard_map/ppermute | solution.py:23
  322.2 25.8 %all-to-all-start.4 = ((bf16[8,64,768]{2,1,0:T(8,128)(2,1)}), bf16[8,64,768]{2,1,0:T(8,128)(2,1)S(1)}, u32[]{:S(2)}, u32[]{:S(2)}) async-start(bf16[8,64,768]{2,1,0:T(8,128)(2,1)} %bitcast.33), calls=%async_computation.4 | async-start | bytes 1572864 | tf_op jit(solution)/shard_map/all_to_all | solution.py:27
  328.0 20.0 %collective-permute-start.20 = (bf16[512,768]{1,0:T(8,128)(2,1)S(1)}, bf16[512,768]{1,0:T(8,128)(2,1)S(1)}, u32[]{:S(2)}, u32[]{:S(2)}) collective-permute-start(bf16[512,768]{1,0:T(8,128)(2,1)S(1)} %broadcast_select_fusion.4), channel_id=1, source_target_pairs={{0,16},{16,0},{1,17},{17,1},{2,18},{18,2},{3,19},{19,3},{4,20},{20... | collective-permute-start | bytes 2359304 | tf_op jit(solution)/shard_map/ppermute | solution.py:23
  330.3 17.7 %collective-permute-start.19 = (bf16[256,384]{1,0:T(8,128)(2,1)}, bf16[256,384]{1,0:T(8,128)(2,1)}, u32[]{:S(2)}, u32[]{:S(2)}) collective-permute-start(bf16[256,384]{1,0:T(8,128)(2,1)} %get-tuple-element.151), channel_id=1, source_target_pairs={{0,1},{1,0},{2,3},{3,2},{4,5},{5,4},{6,7},{7,6},{8,9},{9,8},{10,11... | collective-permute-start | bytes 589832 | tf_op jit(solution)/shard_map/ppermute | solution.py:23
  330.9 17.1 %collective-permute-start.18 = (bf16[256,768]{1,0:T(8,128)(2,1)S(1)}, bf16[256,768]{1,0:T(8,128)(2,1)}, u32[]{:S(2)}, u32[]{:S(2)}) collective-permute-start(bf16[256,768]{1,0:T(8,128)(2,1)S(1)} %copy-done.62), channel_id=1, source_target_pairs={{0,1},{1,0},{2,3},{3,2},{4,5},{5,4},{6,7},{7,6},{8,9},{9,8},{10,11... | collective-permute-start | bytes 1179656 | tf_op jit(solution)/shard_map/ppermute | solution.py:23
  352.1 35.6 %copy-start.69 = (bf16[256,384]{1,0:T(8,128)(2,1)S(1)}, bf16[256,384]{1,0:T(8,128)(2,1)}, u32[]{:S(2)}) copy-start(bf16[256,384]{1,0:T(8,128)(2,1)} %get-tuple-element.163) | copy-start | bytes 589828
  364.0 25.3 %copy-start.67 = (bf16[256,1152]{1,0:T(8,128)(2,1)S(1)}, bf16[256,1152]{1,0:T(8,128)(2,1)}, u32[]{:S(2)}) copy-start(bf16[256,1152]{1,0:T(8,128)(2,1)} %get-tuple-element.161) | copy-start | bytes 1769476
  364.0 25.3 %collective-permute-start.21 = (bf16[256,1152]{1,0:T(8,128)(2,1)}, bf16[256,1152]{1,0:T(8,128)(2,1)S(1)}, u32[]{:S(2)}, u32[]{:S(2)}) collective-permute-start(bf16[256,1152]{1,0:T(8,128)(2,1)} %get-tuple-element.162), channel_id=1, source_target_pairs={{0,1},{1,0},{2,3},{3,2},{4,5},{5,4},{6,7},{7,6},{8,9},{9,8},{10,11... | collective-permute-start | bytes 1769480 | tf_op jit(solution)/shard_map/ppermute | solution.py:23
  365.3 22.5 %collective-permute-start.22 = (bf16[256,768]{1,0:T(8,128)(2,1)S(1)}, bf16[256,768]{1,0:T(8,128)(2,1)S(1)}, u32[]{:S(2)}, u32[]{:S(2)}) collective-permute-start(bf16[256,768]{1,0:T(8,128)(2,1)S(1)} %copy-done.64), channel_id=1, source_target_pairs={{0,1},{1,0},{2,3},{3,2},{4,5},{5,4},{6,7},{7,6},{8,9},{9,8},{10,11... | collective-permute-start | bytes 1179656 | tf_op jit(solution)/shard_map/ppermute | solution.py:23
  366.1 30.0 %all-to-all-start.5 = ((bf16[8,64,768]{2,1,0:T(8,128)(2,1)}), bf16[8,64,768]{2,1,0:T(8,128)(2,1)}, u32[]{:S(2)}, u32[]{:S(2)}) async-start(bf16[8,64,768]{2,1,0:T(8,128)(2,1)} %bitcast.167), calls=%async_computation.5 | async-start | bytes 1572864 | tf_op jit(solution)/shard_map/all_to_all | solution.py:27
  394.5 26.9 %collective-permute-start.24 = (bf16[8,48,1536]{2,1,0:T(8,128)(2,1)S(1)}, bf16[8,48,1536]{2,1,0:T(8,128)(2,1)S(1)}, u32[]{:S(2)}, u32[]{:S(2)}) collective-permute-start(bf16[8,48,1536]{2,1,0:T(8,128)(2,1)S(1)} %fusion.101), channel_id=1, source_target_pairs={{0,16},{16,0},{1,17},{17,1},{2,18},{18,2},{3,19},{19,3},{4,20},{20... | collective-permute-start | bytes 3538952 | tf_op jit(solution)/shard_map/ppermute | solution.py:23
  396.1 26.7 %all-to-all-start.6 = ((bf16[8,64,768]{2,1,0:T(8,128)(2,1)}), bf16[8,64,768]{2,1,0:T(8,128)(2,1)S(1)}, u32[]{:S(2)}, u32[]{:S(2)}) async-start(bf16[8,64,768]{2,1,0:T(8,128)(2,1)} %bitcast.166), calls=%async_computation.6 | async-start | bytes 1572864 | tf_op jit(solution)/shard_map/all_to_all | solution.py:27
  402.2 24.2 %collective-permute-start.23 = (bf16[512,768]{1,0:T(8,128)(2,1)}, bf16[512,768]{1,0:T(8,128)(2,1)}, u32[]{:S(2)}, u32[]{:S(2)}) collective-permute-start(bf16[512,768]{1,0:T(8,128)(2,1)} %bitcast.36.dz_ref), channel_id=1, source_target_pairs={{0,1},{1,0},{2,3},{3,2},{4,5},{5,4},{6,7},{7,6},{8,9},{9,8},{10,11... | collective-permute-start | bytes 2359304 | tf_op jit(solution)/shard_map/ppermute | solution.py:23
  422.8 38.6 %all-to-all-start.7 = ((bf16[8,48,1536]{2,1,0:T(8,128)(2,1)}), bf16[8,48,1536]{2,1,0:T(8,128)(2,1)S(1)}, u32[]{:S(2)}, u32[]{:S(2)}) async-start(bf16[8,48,1536]{2,1,0:T(8,128)(2,1)} %add_convert_fusion), calls=%async_computation.7 | async-start | bytes 2359296 | tf_op jit(solution)/shard_map/all_to_all | solution.py:27
  437.3 20.8 %collective-permute-start.25 = (bf16[512,768]{1,0:T(8,128)(2,1)}, bf16[512,768]{1,0:T(8,128)(2,1)S(1)}, u32[]{:S(2)}, u32[]{:S(2)}) collective-permute-start(bf16[512,768]{1,0:T(8,128)(2,1)} %get-tuple-element.168), channel_id=1, source_target_pairs={{0,1},{1,0},{2,3},{3,2},{4,5},{5,4},{6,7},{7,6},{8,9},{9,8},{10,11... | collective-permute-start | bytes 2359304 | tf_op jit(solution)/shard_map/ppermute | solution.py:23
  439.1 84.4 %collective-permute-start.32 = (bf16[512,768]{1,0:T(8,128)(2,1)}, bf16[512,768]{1,0:T(8,128)(2,1)}, u32[]{:S(2)}, u32[]{:S(2)}) collective-permute-start(bf16[512,768]{1,0:T(8,128)(2,1)} %broadcast_select_fusion.3), channel_id=1, source_target_pairs={{0,16},{16,0},{1,17},{17,1},{2,18},{18,2},{3,19},{19,3},{4,20},{20... | collective-permute-start | bytes 2359304 | tf_op jit(solution)/shard_map/ppermute | solution.py:23
  441.6 81.9 %collective-permute-start.33 = (bf16[512,768]{1,0:T(8,128)(2,1)}, bf16[512,768]{1,0:T(8,128)(2,1)}, u32[]{:S(2)}, u32[]{:S(2)}) collective-permute-start(bf16[512,768]{1,0:T(8,128)(2,1)} %broadcast_select_fusion.2), channel_id=1, source_target_pairs={{0,16},{16,0},{1,17},{17,1},{2,18},{18,2},{3,19},{19,3},{4,20},{20... | collective-permute-start | bytes 2359304 | tf_op jit(solution)/shard_map/ppermute | solution.py:23
  458.9 81.6 %collective-permute-start.31 = (bf16[128,768]{1,0:T(8,128)(2,1)}, bf16[128,768]{1,0:T(8,128)(2,1)}, u32[]{:S(2)}, u32[]{:S(2)}) collective-permute-start(bf16[128,768]{1,0:T(8,128)(2,1)} %get-tuple-element.249), channel_id=1, source_target_pairs={{0,1},{1,0},{2,3},{3,2},{4,5},{5,4},{6,7},{7,6},{8,9},{9,8},{10,11... | collective-permute-start | bytes 589832 | tf_op jit(solution)/shard_map/ppermute | solution.py:23
  461.3 26.5 %all-to-all-start.8 = ((bf16[8,64,768]{2,1,0:T(8,128)(2,1)}), bf16[8,64,768]{2,1,0:T(8,128)(2,1)S(1)}, u32[]{:S(2)}, u32[]{:S(2)}) async-start(bf16[8,64,768]{2,1,0:T(8,128)(2,1)} %bitcast.156), calls=%async_computation.8 | async-start | bytes 1572864 | tf_op jit(solution)/shard_map/all_to_all | solution.py:27
  467.4 8.1 %collective-permute-start.26 = (bf16[128,768]{1,0:T(8,128)(2,1)S(1)}, bf16[128,768]{1,0:T(8,128)(2,1)S(1)}, u32[]{:S(2)}, u32[]{:S(2)}) collective-permute-start(bf16[128,768]{1,0:T(8,128)(2,1)S(1)} %get-tuple-element.253), channel_id=1, source_target_pairs={{0,1},{1,0},{2,3},{3,2},{4,5},{5,4},{6,7},{7,6},{8,9},{9,8},{10,11... | collective-permute-start | bytes 589832 | tf_op jit(solution)/shard_map/ppermute | solution.py:23
  475.8 28.0 %collective-permute-start.27 = (bf16[2,128,768]{2,1,0:T(8,128)(2,1)S(1)}, bf16[2,128,768]{2,1,0:T(8,128)(2,1)S(1)}, u32[]{:S(2)}, u32[]{:S(2)}) collective-permute-start(bf16[2,128,768]{2,1,0:T(8,128)(2,1)S(1)} %broadcast_select_fusion.7), channel_id=1, source_target_pairs={{0,16},{16,0},{1,17},{17,1},{2,18},{18,2},{3,19},{19,3},{4,20},{20... | collective-permute-start | bytes 1179656 | tf_op jit(solution)/shard_map/ppermute | solution.py:23
  491.8 15.1 %collective-permute-start.28 = (bf16[256,768]{1,0:T(8,128)(2,1)}, bf16[256,768]{1,0:T(8,128)(2,1)S(1)}, u32[]{:S(2)}, u32[]{:S(2)}) collective-permute-start(bf16[256,768]{1,0:T(8,128)(2,1)} %get-tuple-element.205.refs_1_), channel_id=1, source_target_pairs={{0,1},{1,0},{2,3},{3,2},{4,5},{5,4},{6,7},{7,6},{8,9},{9,8},{10,11... | collective-permute-start | bytes 1179656 | tf_op jit(solution)/shard_map/ppermute | solution.py:23
  503.8 14.9 %collective-permute-start.29 = (bf16[256,1152]{1,0:T(8,128)(2,1)}, bf16[256,1152]{1,0:T(8,128)(2,1)S(1)}, u32[]{:S(2)}, u32[]{:S(2)}) collective-permute-start(bf16[256,1152]{1,0:T(8,128)(2,1)} %get-tuple-element.209), channel_id=1, source_target_pairs={{0,1},{1,0},{2,3},{3,2},{4,5},{5,4},{6,7},{7,6},{8,9},{9,8},{10,11... | collective-permute-start | bytes 1769480 | tf_op jit(solution)/shard_map/ppermute | solution.py:23
  509.3 27.0 %collective-permute-start.35 = (bf16[8,48,384]{2,1,0:T(8,128)(2,1)}, bf16[8,48,384]{2,1,0:T(8,128)(2,1)}, u32[]{:S(2)}, u32[]{:S(2)}) collective-permute-start(bf16[8,48,384]{2,1,0:T(8,128)(2,1)} %fusion.138), channel_id=1, source_target_pairs={{0,16},{16,0},{1,17},{17,1},{2,18},{18,2},{3,19},{19,3},{4,20},{20... | collective-permute-start | bytes 884744 | tf_op jit(solution)/shard_map/ppermute | solution.py:23
  511.8 23.5 %all-to-all-start.9 = ((f32[8,2,10,768]{3,1,2,0:T(2,128)}), f32[8,2,10,768]{3,1,2,0:T(2,128)S(1)}, u32[]{:S(2)}, u32[]{:S(2)}) async-start(f32[8,2,10,768]{3,1,2,0:T(2,128)} %broadcast_in_dim.27), calls=%async_computation.9 | async-start | bytes 983040 | tf_op jit(solution)/shard_map/all_to_all | solution.py:27
  522.0 23.3 %collective-permute-start.34 = (bf16[8,48,1152]{2,1,0:T(8,128)(2,1)}, bf16[8,48,1152]{2,1,0:T(8,128)(2,1)}, u32[]{:S(2)}, u32[]{:S(2)}) collective-permute-start(bf16[8,48,1152]{2,1,0:T(8,128)(2,1)} %fusion.112), channel_id=1, source_target_pairs={{0,16},{16,0},{1,17},{17,1},{2,18},{18,2},{3,19},{19,3},{4,20},{20... | collective-permute-start | bytes 2654216 | tf_op jit(solution)/shard_map/ppermute | solution.py:23
  524.3 16.2 %collective-permute-start.30 = (bf16[128,768]{1,0:T(8,128)(2,1)}, bf16[128,768]{1,0:T(8,128)(2,1)}, u32[]{:S(2)}, u32[]{:S(2)}) collective-permute-start(bf16[128,768]{1,0:T(8,128)(2,1)} %get-tuple-element.252), channel_id=1, source_target_pairs={{0,1},{1,0},{2,3},{3,2},{4,5},{5,4},{6,7},{7,6},{8,9},{9,8},{10,11... | collective-permute-start | bytes 589832 | tf_op jit(solution)/shard_map/ppermute | solution.py:23
  535.5 4.3 collective-permute-start.37
  539.9 4.2 collective-permute-start.38
  547.8 33.3 %all-to-all-start.10 = ((bf16[8,48,1536]{2,1,0:T(8,128)(2,1)}), bf16[8,48,1536]{2,1,0:T(8,128)(2,1)S(1)}, u32[]{:S(2)}, u32[]{:S(2)}) async-start(bf16[8,48,1536]{2,1,0:T(8,128)(2,1)} %pad_maximum_fusion.3), calls=%async_computation.10 | async-start | bytes 2359296 | tf_op jit(solution)/shard_map/all_to_all | solution.py:27
  568.6 11.5 %collective-permute-start.36 = (bf16[2,128,768]{2,1,0:T(8,128)(2,1)S(1)}, bf16[2,128,768]{2,1,0:T(8,128)(2,1)S(1)}, u32[]{:S(2)}, u32[]{:S(2)}) collective-permute-start(bf16[2,128,768]{2,1,0:T(8,128)(2,1)S(1)} %broadcast_select_fusion.6), channel_id=1, source_target_pairs={{0,16},{16,0},{1,17},{17,1},{2,18},{18,2},{3,19},{19,3},{4,20},{20... | collective-permute-start | bytes 1179656 | tf_op jit(solution)/shard_map/ppermute | solution.py:23
  581.5 5.9 collective-permute-start.39
  (64 other events, 512.3 us)
Sparse Core Ops, SparseCore 0:
  27.6 52.8 all-gather.4
  82.1 61.4 all-gather.8
  145.2 68.3 all-gather.6
